TPU v7x, 256 devices: a whole 4x4x8 slice. The times are simulated.
256 devices in a mesh: obs: 64 (over x, z, core), tile: 4 (over y).
Axes of the slice: x: 4, y: 4, z: 8, core: 2. Of those that a mesh axis runs over, the one named last changes fastest.
Arguments:
- jacobian: bfloat16 [16384, 65536], P(('obs', 'tile')), may hold values from -0.1875 to 0.1875
- obs_weight: float32 [16384], P(('obs', 'tile')), may hold values from 0.1 to 10
- block_order: int32 [512], replicated, may hold values from 0 to 511, each once
- tile_pairs: int32 [64, 64, 2], P('obs'), may hold values from 0 to 7, as said below
- tile_count: int32 [64], P('obs'), may hold values from 1 to 64, as said below
Outputs:
- hessian: float32 [4096, 128, 128], P(('obs', 'tile'))
Inputs may be any that keep to these rules, and one draw needn't show every extreme that they name: `tile_pairs`: slot numbers within an owner's own 8 slots; the first tile_count[j] pairs of owner j are distinct. `tile_count`: some owner has 64 live tiles.
All inputs are finite; a program needn't handle non-finite values.
Results may differ from a plain program's by a relative error of at most 0.0015.
Values may be sent and summed in bfloat16 or wider, within the bound.
No kernel may reach another device: no remote copies, remote signals or barrier semaphores. Data moves between devices by JAX's collectives and lax.ppermute only.
A program may use at most 256 MiB of HBM per device.

v0:
```python
import jax
import jax.numpy as jnp
from jax import lax
from jax.sharding import PartitionSpec as P

BLOCK = 128


def body(jacobian, obs_weight, block_order, tile_pairs, tile_count):
    row_count = jacobian.shape[0]
    owners = lax.axis_size("obs")
    total_blocks = block_order.shape[0]
    own_blocks = total_blocks // owners
    own_width = own_blocks * BLOCK
    blocks = jacobian.reshape(row_count, total_blocks, BLOCK)
    ordered = jnp.take(blocks, block_order, axis=1)
    root_weight = jnp.sqrt(obs_weight)[:, None, None]
    scaled = (ordered.astype(jnp.float32) * root_weight).astype(jnp.bfloat16)
    outgoing = scaled.reshape(row_count, owners, own_width)
    arrived = lax.all_to_all(outgoing, "obs", split_axis=1, concat_axis=0, tiled=True)
    columns = arrived.reshape(row_count * owners, own_width)
    pair_list = tile_pairs[0]
    live_count = tile_count[0]
    slot_total = pair_list.shape[0]
    slot_ids = jnp.arange(slot_total, dtype=jnp.int32)
    is_live = slot_ids < live_count
    per_group = min(own_blocks, 8)

    def gram_group(group_index, tiles):
        first_slot = group_index * per_group
        gram_part = lax.dot_general(
            columns, columns, (((0,), (0,)), ((), ())), preferred_element_type=jnp.float32
        )
        gram_tiles = gram_part.reshape(per_group, BLOCK, own_blocks, BLOCK).transpose(0, 2, 1, 3)
        gram_tiles = gram_tiles.reshape(per_group * own_blocks, BLOCK, BLOCK)
        relative = pair_list[:, 0] - first_slot
        inside = (relative >= 0) & (relative < per_group) & is_live
        lookup = jnp.clip(relative, 0, per_group - 1) * own_blocks + pair_list[:, 1]
        picked = jnp.take(gram_tiles, lookup, axis=0)
        return jnp.where(inside[:, None, None], picked, tiles)

    all_tiles = lax.fori_loop(
        0, own_blocks // per_group, gram_group, jnp.zeros((slot_total, BLOCK, BLOCK), jnp.float32)
    )
    hessian = lax.psum_scatter(all_tiles, "tile", scatter_dimension=0, tiled=True)
    return hessian


def solution(mesh):
    return jax.shard_map(
        body,
        mesh=mesh,
        in_specs=(
            P(("obs", "tile"), None),
            P(("obs", "tile")),
            P(),
            P("obs", None, None),
            P("obs"),
        ),
        out_specs=P(("obs", "tile"), None, None),
        check_vma=False,
    )
```

profile of v0, /device:TPU:2, one launch (start us, length us, event | category | flops | bytes accessed | tf_op | source)
XLA Modules:
  0.0 375.3 jit_solution(16123092588798176954)
XLA Ops:
  6.5 0.7 compare_select_fusion
  7.2 0.7 compare_and_fusion
  7.9 9.0 %copy_bitcast_fusion = bf16[64,512,128]{2,0,1:T(8,128)(2,1)} fusion(bf16[64,65536]{1,0:T(8,128)(2,1)} %param.5), kind=kLoop, calls=%fused_computation.3 | loop fusion | bytes 16777216 | tf_op jit(solution)/shard_map/reshape | solution.py:15
  16.9 23.0 %gather_fusion = bf16[512,64,128]{2,1,0:T(8,128)(2,1)} fusion(bf16[64,512,128]{2,0,1:T(8,128)(2,1)} %copy_bitcast_fusion, s32[1024]{0:T(1024)S(1)} %pad_clamp_fusion.1), kind=kCustom, calls=%fused_computation | custom fusion | bytes 16779264 | tf_op jit(solution)/shard_map/jit(_take)/gather | solution.py:16
  40.0 12.0 %copy.13 = bf16[64,512,128]{2,1,0:T(8,128)(2,1)} copy(bf16[64,512,128]{2,0,1:T(8,128)(2,1)} %bitcast.35) | data formatting | bytes 16777216 | tf_op jit(solution)/shard_map/jit(_take)/gather | solution.py:16
  52.0 0.0 copy-start.1
  52.0 13.3 %gather.12 = bf16[64,64,1024]{2,1,0:T(8,128)(2,1)} reshape(bf16[64,512,128]{2,1,0:T(8,128)(2,1)} %copy.13) | data formatting | bytes 16777216 | tf_op jit(solution)/shard_map/jit(_take)/gather | solution.py:16
  65.3 0.1 broadcast_in_dim.50
  65.4 0.1 broadcast_in_dim.51
  65.6 0.0 copy-done.1
  65.6 10.0 %multiply_convert_fusion = bf16[64,64,1024]{2,1,0:T(8,128)(2,1)} fusion(f32[64]{0:T(128)S(1)} %sqrt.3, bf16[64,64,1024]{2,1,0:T(8,128)(2,1)} %gather.12, pred[64,1024]{1,0:T(8,128)(4,1)S(1)} %bitcast.39), kind=kLoop, calls=%fused_computation.2 | loop fusion | flops 16777216 | bytes 16843008 | tf_op jit(solution)/shard_map/convert_element_type | solution.py:18
  75.6 11.3 %copy.14 = bf16[64,64,1024]{2,0,1:T(8,128)(2,1)} copy(bf16[64,64,1024]{2,1,0:T(8,128)(2,1)} %multiply_convert_fusion) | data formatting | bytes 16777216 | tf_op jit(solution)/shard_map/convert_element_type | solution.py:18
  86.9 0.0 copy-start
  86.9 12.3 %all-to-all-start = ((bf16[64,64,1024]{2,0,1:T(8,128)(2,1)}), bf16[64,64,1024]{2,0,1:T(8,128)(2,1)}, u32[]{:S(2)}, u32[]{:S(2)}) async-start(bf16[64,64,1024]{2,0,1:T(8,128)(2,1)} %copy.14), calls=%async_computation | async-start | bytes 16777216 | tf_op jit(solution)/shard_map/all_to_all | solution.py:20
  99.2 0.0 reduce-scatter.2.cloned.1.call-start
  99.9 0.0 copy-done
  100.0 183.6 %all-to-all-done = bf16[64,64,1024]{2,0,1:T(8,128)(2,1)} async-done(((bf16[64,64,1024]{2,0,1:T(8,128)(2,1)}), bf16[64,64,1024]{2,0,1:T(8,128)(2,1)}, u32[]{:S(2)}, u32[]{:S(2)}) %all-to-all-start) | async-done | bytes 8388640 | tf_op jit(solution)/shard_map/all_to_all | solution.py:20
  283.6 11.6 %copy.15 = bf16[1024,4096]{1,0:T(8,128)(2,1)} copy(bf16[1024,4096]{0,1:T(8,128)(2,1)} %bitcast.8) | data formatting | bytes 16777216 | tf_op jit(solution)/shard_map/while/body/eval_jaxpr/dot_general | solution.py:31
  295.1 15.9 %fusion = f32[8,128,8,128]{3,1,2,0:T(8,128)} fusion(bf16[8,128,4096,1]{2,1,3,0:T(8,128)(2,1)} %bitcast.36, bf16[8,128,4096,1]{2,1,0,3:T(8,128)(2,1)} %bitcast.37), kind=kOutput, calls=%fused_computation.13 | convolution fusion | flops 8589934592 | bytes 20971520 | tf_op jit(solution)/shard_map/while/body/eval_jaxpr/dot_general | solution.py:31
  311.0 5.0 %gather_fusion.1 = f32[64,128,128]{2,1,0:T(8,128)} fusion(f32[64,128,128]{2,1,0:T(8,128)} %bitcast.38, s32[1024]{0:T(1024)S(1)} %pad_clamp_fusion), kind=kCustom, calls=%fused_computation.1 | custom fusion | bytes 8388864 | tf_op jit(solution)/shard_map/while/body/eval_jaxpr/jit(_take)/gather | solution.py:39
  316.0 4.7 %select_select_fusion = f32[64,128,128]{2,1,0:T(8,128)} fusion(f32[64,128,128]{2,1,0:T(8,128)} %gather_fusion.1, pred[64]{0:T(512)(128)(4,1)S(1)} %get-tuple-element.15, pred[64]{0:T(512)(128)(4,1)S(1)} %bitcast_and_fusion), kind=kLoop, calls=%fused_computation.4 | loop fusion | flops 2097152 | bytes 8388736 | tf_op jit(solution)/shard_map/while/body/eval_jaxpr/jit(_where)/select_n | solution.py:40
  320.6 0.0 reduce-scatter.2.cloned.1.call-update
  320.6 47.8 %reduce-scatter.2.cloned.1.call-done = f32[16,128,128]{2,1,0:T(8,128)} async-done(((f32[64,128,128]{2,1,0:T(8,128)}), f32[16,128,128]{2,1,0:T(8,128)}) %reduce-scatter.2.cloned.1.call-update) | async-done | bytes 1048592 | tf_op jit(solution)/shard_map/reduce_scatter | solution.py:45
  (6 shorter events, 0.1 us)
Async XLA Ops:
  52.0 13.6 %copy-start.1 = (f32[64]{0:T(128)S(1)}, f32[64]{0:T(128)}, u32[]{:S(2)}) copy-start(f32[64]{0:T(128)} %param.6) | copy-start | bytes 772
  86.9 13.1 %copy-start = (s32[1,64,2]{1,2,0:T(2,128)S(1)}, s32[1,64,2]{1,2,0:T(2,128)}, u32[]{:S(2)}) copy-start(s32[1,64,2]{1,2,0:T(2,128)} %param.8) | copy-start | bytes 1540
  86.9 196.7 %all-to-all-start = ((bf16[64,64,1024]{2,0,1:T(8,128)(2,1)}), bf16[64,64,1024]{2,0,1:T(8,128)(2,1)}, u32[]{:S(2)}, u32[]{:S(2)}) async-start(bf16[64,64,1024]{2,0,1:T(8,128)(2,1)} %copy.14), calls=%async_computation | async-start | bytes 16777216 | tf_op jit(solution)/shard_map/all_to_all | solution.py:20
  99.2 269.2 %reduce-scatter.2.cloned.1.call-start = ((), (), s32[]{:S(2)}) async-start(), calls=%async_computation.2 | async-start | bytes 5242880 | tf_op jit(solution)/shard_map/reduce_scatter | solution.py:45
Sparse Core Ops, SparseCore 0:
  320.8 47.6 reduce-scatter.1
where the time goes:
time: 377 us; the launch traced here: 375 us
  waiting for transfers between devices  231 us (61%)
  local copies, waits for them, and re-layouts  85.5 us (23%)
  other arithmetic  16 us (4%)
  matrix products  15.9 us (4%)
  between operations  14.1 us (4%)
  starting transfers between devices  12.4 us (3%)
    all_to_all x1, waiting for transfers between devices, body(): lax.all_to_all(outgoing, 'obs', split_axis=1, concat_axis=0, tiled=True)  184 us
    gather x3, local copies, waits for them, and re-layouts, body(): ordered = jnp.take(blocks, block_order, axis=1)  48.4 us
    reduce_scatter x1, waiting for transfers between devices, body(): lax.psum_scatter(all_tiles, 'tile', scatter_dimension=0, tiled=True)  47.8 us
    dot_general x1, matrix products, gram_group(): lax.dot_general(columns, columns, (((0,), (0,)), ((), ())), preferred_ele...  15.9 us
    all_to_all x1, starting transfers between devices, body(): lax.all_to_all(outgoing, 'obs', split_axis=1, concat_axis=0, tiled=True)  12.3 us
    dot_general x1, local copies, waits for them, and re-layouts, gram_group(): lax.dot_general(columns, columns, (((0,), (0,)), ((), ())), preferred_ele...  11.6 us
    convert_element_type x1, local copies, waits for them, and re-layouts, body(): scaled = (ordered.astype(jnp.float32) * root_weight).astype(jnp.bfloat16)  11.3 us
    convert_element_type x1, other arithmetic, body(): scaled = (ordered.astype(jnp.float32) * root_weight).astype(jnp.bfloat16)  9.97 us
  transfers between devices with their start and end apart: 2, of which 2 were waited for; matrix products, arithmetic and copies ran while one was open for 0% of the time, Pallas kernels for 0%

commit v1 on v0

v1 whole, which is shorter than its diff:
```python
import jax
import jax.numpy as jnp
from jax import lax
from jax.experimental import pallas as pl
from jax.experimental.pallas import tpu as pltpu
from jax.sharding import PartitionSpec as P

BLOCK = 128
ROW_STEP = 16


def scale_columns(owners, order, jacobian, weight):
    units = owners.shape[0]
    rows, zones = jacobian.shape
    own_blocks = 8
    width = own_blocks * BLOCK

    def kernel(owners_ref, order_ref, jac_ref, weight_ref, out_ref):
        root = jnp.sqrt(weight_ref[...])

        def unit(u, carry):
            base = owners_ref[u] * own_blocks
            for b in range(own_blocks):
                start = pl.multiple_of(order_ref[base + b] * BLOCK, BLOCK)
                piece = jac_ref[:, pl.ds(start, BLOCK)].astype(jnp.float32) * root
                out_ref[u, :, b * BLOCK : (b + 1) * BLOCK] = piece.astype(jnp.bfloat16)
            return carry

        lax.fori_loop(0, units, unit, 0)

    return pl.pallas_call(
        kernel,
        out_shape=jax.ShapeDtypeStruct((units, rows, width), jnp.bfloat16),
        grid_spec=pltpu.PrefetchScalarGridSpec(
            num_scalar_prefetch=2,
            grid=(rows // ROW_STEP,),
            in_specs=[
                pl.BlockSpec((ROW_STEP, zones), lambda i, *_: (i, 0)),
                pl.BlockSpec((ROW_STEP, BLOCK), lambda i, *_: (i, 0)),
            ],
            out_specs=pl.BlockSpec((units, ROW_STEP, width), lambda i, *_: (0, i, 0)),
        ),
        compiler_params=pltpu.CompilerParams(vmem_limit_bytes=40 << 20),
        cost_estimate=pl.CostEstimate(
            flops=units * rows * width, bytes_accessed=2 * (rows * zones + units * rows * width), transcendentals=0
        ),
        name="scale_columns",
    )(owners, order, jacobian, weight)


def gram_tiles(pieces, step, pairs, count):
    rows, width = pieces[0].shape
    slots = pairs.shape[0] // 2
    steps = rows // step
    strip = 256

    def kernel(pairs_ref, count_ref, *refs):
        piece_refs, out_ref, gram = refs[:-2], refs[-2], refs[-1]
        first = pl.program_id(0) == 0

        @pl.when(first)
        def _():
            gram[...] = jnp.zeros_like(gram)

        for ref in piece_refs:
            for m in range(0, width, strip):
                gram[m : m + strip, :] += lax.dot_general(
                    ref[:, m : m + strip], ref[...], (((0,), (0,)), ((), ())), preferred_element_type=jnp.float32
                )

        @pl.when(pl.program_id(0) == steps - 1)
        def _():
            def pick(k, carry):
                row = pl.multiple_of(pairs_ref[2 * k] * BLOCK, BLOCK)
                col = pl.multiple_of(pairs_ref[2 * k + 1] * BLOCK, BLOCK)
                tile = gram[pl.ds(row, BLOCK), pl.ds(col, BLOCK)]
                out_ref[k] = jnp.where(k < count_ref[0], tile, 0.0)
                return carry

            lax.fori_loop(0, slots, pick, 0)

    return pl.pallas_call(
        kernel,
        out_shape=jax.ShapeDtypeStruct((slots, BLOCK, BLOCK), jnp.float32),
        grid_spec=pltpu.PrefetchScalarGridSpec(
            num_scalar_prefetch=2,
            grid=(steps,),
            in_specs=[pl.BlockSpec((step, width), lambda i, *_: (i, 0)) for _ in pieces],
            out_specs=pl.BlockSpec((slots, BLOCK, BLOCK), lambda i, *_: (0, 0, 0)),
            scratch_shapes=[pltpu.VMEM((width, width), jnp.float32)],
        ),
        compiler_params=pltpu.CompilerParams(vmem_limit_bytes=40 << 20),
        cost_estimate=pl.CostEstimate(
            flops=2 * len(pieces) * rows * width * width,
            bytes_accessed=2 * len(pieces) * rows * width + 4 * slots * BLOCK * BLOCK,
            transcendentals=0,
        ),
        name="gram_tiles",
    )(pairs, count, *pieces)


def body(jacobian, obs_weight, block_order, tile_pairs, tile_count):
    rows = jacobian.shape[0]
    owners = lax.axis_size("obs")
    weight = jnp.broadcast_to(obs_weight[:, None], (rows, BLOCK))
    outgoing = scale_columns(jnp.arange(owners, dtype=jnp.int32), block_order, jacobian, weight)
    arrived = lax.all_to_all(outgoing, "obs", split_axis=0, concat_axis=0, tiled=True)
    columns = arrived.reshape(owners * rows, arrived.shape[2])
    tiles = gram_tiles([columns], 512, tile_pairs.reshape(-1), tile_count)
    return lax.psum_scatter(tiles, "tile", scatter_dimension=0, tiled=True)


def solution(mesh):
    return jax.shard_map(
        body,
        mesh=mesh,
        in_specs=(
            P(("obs", "tile"), None),
            P(("obs", "tile")),
            P(),
            P("obs", None, None),
            P("obs"),
        ),
        out_specs=P(("obs", "tile"), None, None),
        check_vma=False,
    )
```

time: 377 us -> 288 us (0.76)
  local copies, waits for them, and re-layouts: 85.5 us -> 6.81 us
  Pallas kernels: 0 us -> 22.5 us
  other arithmetic: 16 us -> 0 us
  matrix products: 15.9 us -> 0 us
    gather x4 -> x0, local copies, waits for them, and re-layouts: 53.3 us -> none  [the longest x3 48.4 us: body(): ordered = jnp.take(blocks, block_order, axis=1)]
    pallas_call x0 -> x2, Pallas kernels: none -> 22.5 us  [the longest x1 13.5 us: gram_tiles(): pl.pallas_call(kernel, out_shape=jax.ShapeDtypeStruct((slots, BLOCK, BLOC...]
    dot_general x1 -> x0, matrix products: 15.9 us -> none  [gram_group(): lax.dot_general(columns, columns, (((0,), (0,)), ((), ())), preferred_ele...]
    dot_general x1 -> x0, local copies, waits for them, and re-layouts: 11.6 us -> none  [gram_group(): lax.dot_general(columns, columns, (((0,), (0,)), ((), ())), preferred_ele...]
    convert_element_type x1 -> x0, local copies, waits for them, and re-layouts: 11.3 us -> none  [body(): scaled = (ordered.astype(jnp.float32) * root_weight).astype(jnp.bfloat16)]
    convert_element_type x1 -> x0, other arithmetic: 9.97 us -> none  [body(): scaled = (ordered.astype(jnp.float32) * root_weight).astype(jnp.bfloat16)]
    reshape x1, local copies, waits for them, and re-layouts: 9.01 us -> 0.14 us  [body(): tiles = gram_tiles([columns], 512, tile_pairs.reshape(-1), tile_count)]
    unnamed x5 -> x9, local copies, waits for them, and re-layouts: 0.04 us -> 5.94 us
where the time goes in v1:
time: 288 us; the launch traced here: 287 us
  waiting for transfers between devices  231 us (80%)
  Pallas kernels  22.5 us (8%)
  between operations  14.1 us (5%)
  starting transfers between devices  12.4 us (4%)
  local copies, waits for them, and re-layouts  6.81 us (2%)
    all_to_all x1, waiting for transfers between devices, body(): lax.all_to_all(outgoing, 'obs', split_axis=0, concat_axis=0, tiled=True)  183 us
    reduce_scatter x1, waiting for transfers between devices, body(): return lax.psum_scatter(tiles, 'tile', scatter_dimension=0, tiled=True)  47.8 us
    pallas_call x1, Pallas kernels, gram_tiles(): pl.pallas_call(kernel, out_shape=jax.ShapeDtypeStruct((slots, BLOCK, BLOC...  13.5 us
    all_to_all x1, starting transfers between devices, body(): lax.all_to_all(outgoing, 'obs', split_axis=0, concat_axis=0, tiled=True)  12.3 us
    pallas_call x1, Pallas kernels, scale_columns(): pl.pallas_call(kernel, out_shape=jax.ShapeDtypeStruct((units, rows, width...  9.01 us
    unnamed x9, local copies, waits for them, and re-layouts  5.94 us
  transfers between devices with their start and end apart: 2, of which 2 were waited for; matrix products, arithmetic and copies ran while one was open for 0% of the time, Pallas kernels for 0%

profile of v1, /device:TPU:2, one launch (start us, length us, event | category | flops | bytes accessed | tf_op | source)
XLA Modules:
  0.0 287.0 jit_solution(15409197442537849449)
XLA Ops:
  6.5 0.7 broadcast_in_dim.2.weight_ref
  7.3 0.0 copy-start.2
  7.3 0.7 copy-done.2
  7.9 9.0 %scale_columns.1 = bf16[64,64,1024]{2,1,0:T(8,128)(2,1)S(1)} custom-call(s32[64]{0:T(128)S(1)} %iota.3.owners_ref, s32[512]{0:T(512)S(1)} %copy-done.2, bf16[64,65536]{1,0:T(8,128)(2,1)} %jac_ref.1, f32[64,128]{1,0:T(8,128)S(1)} %broadcast_in_dim.2.weight_ref), custom_call_target="tpu_custom_call" | custom-call | flops 4194304 | bytes 16777216 | tf_op jit(solution)/shard_map/scale_columns/pallas_call | solution.py:31
  17.0 0.0 copy-start
  17.0 3.2 %copy-done = bf16[64,64,1024]{2,1,0:T(8,128)(2,1)} copy-done((bf16[64,64,1024]{2,1,0:T(8,128)(2,1)}, bf16[64,64,1024]{2,1,0:T(8,128)(2,1)S(1)}, u32[]{:S(2)}) %copy-start) | copy-done | bytes 8388632
  20.2 0.0 copy-start.3
  20.2 12.3 %all-to-all-start = ((bf16[64,64,1024]{2,1,0:T(8,128)(2,1)}), bf16[64,64,1024]{2,1,0:T(8,128)(2,1)}, u32[]{:S(2)}, u32[]{:S(2)}) async-start(bf16[64,64,1024]{2,1,0:T(8,128)(2,1)} %copy-done), calls=%async_computation | async-start | bytes 16777216 | tf_op jit(solution)/shard_map/all_to_all | solution.py:107
  32.5 0.0 reduce-scatter.2.cloned.1.call-start
  32.6 0.0 copy-done.3
  32.6 0.1 copy.7
  32.7 0.1 reshape.7.pairs_ref
  33.5 183.4 %all-to-all-done = bf16[64,64,1024]{2,1,0:T(8,128)(2,1)} async-done(((bf16[64,64,1024]{2,1,0:T(8,128)(2,1)}), bf16[64,64,1024]{2,1,0:T(8,128)(2,1)}, u32[]{:S(2)}, u32[]{:S(2)}) %all-to-all-start) | async-done | bytes 8388640 | tf_op jit(solution)/shard_map/all_to_all | solution.py:107
  216.9 13.5 %gram_tiles.1 = f32[64,128,128]{2,1,0:T(8,128)S(1)} custom-call(s32[128]{0:T(128)S(1)} %reshape.7.pairs_ref, s32[1]{0:T(128)S(6)} %copy.8.count_ref, bf16[4096,1024]{1,0:T(8,128)(2,1)} %bitcast.refs_0_), custom_call_target="tpu_custom_call" | custom-call | flops 8589934592 | bytes 12582912 | tf_op jit(solution)/shard_map/gram_tiles/pallas_call | solution.py:82
  230.4 0.0 copy-start.1
  230.4 1.9 copy-done.1
  232.3 0.0 reduce-scatter.2.cloned.1.call-update
  232.3 47.8 %reduce-scatter.2.cloned.1.call-done = f32[16,128,128]{2,1,0:T(8,128)} async-done(((f32[64,128,128]{2,1,0:T(8,128)}), f32[16,128,128]{2,1,0:T(8,128)}) %reduce-scatter.2.cloned.1.call-update) | async-done | bytes 1048592 | tf_op jit(solution)/shard_map/reduce_scatter | solution.py:110
  (1 shorter events, 0.0 us)
Async XLA Ops:
  7.3 0.7 copy-start.2
  17.0 3.2 %copy-start = (bf16[64,64,1024]{2,1,0:T(8,128)(2,1)}, bf16[64,64,1024]{2,1,0:T(8,128)(2,1)S(1)}, u32[]{:S(2)}) copy-start(bf16[64,64,1024]{2,1,0:T(8,128)(2,1)S(1)} %scale_columns.1) | copy-start | bytes 25165828
  20.2 12.4 %copy-start.3 = (s32[1,64,2]{1,2,0:T(2,128)S(1)}, s32[1,64,2]{1,2,0:T(2,128)}, u32[]{:S(2)}) copy-start(s32[1,64,2]{1,2,0:T(2,128)} %param.8) | copy-start | bytes 1540
  20.2 196.7 %all-to-all-start = ((bf16[64,64,1024]{2,1,0:T(8,128)(2,1)}), bf16[64,64,1024]{2,1,0:T(8,128)(2,1)}, u32[]{:S(2)}, u32[]{:S(2)}) async-start(bf16[64,64,1024]{2,1,0:T(8,128)(2,1)} %copy-done), calls=%async_computation | async-start | bytes 16777216 | tf_op jit(solution)/shard_map/all_to_all | solution.py:107
  32.5 247.6 %reduce-scatter.2.cloned.1.call-start = ((), (), s32[]{:S(2)}) async-start(), calls=%async_computation.2 | async-start | bytes 5242880 | tf_op jit(solution)/shard_map/reduce_scatter | solution.py:110
  230.4 1.9 copy-start.1
Sparse Core Ops, SparseCore 0:
  232.5 47.6 reduce-scatter.1

commit v2 on v1

v2 whole, which is shorter than its diff:
```python
import jax
import jax.numpy as jnp
import numpy as np
from jax import lax
from jax.experimental import pallas as pl
from jax.experimental.pallas import tpu as pltpu
from jax.sharding import PartitionSpec as P

BLOCK = 128
OWN_BLOCKS = 8
WIDTH = OWN_BLOCKS * BLOCK
ROW_STEP = 16
FAR = 3
BOTH_STEPS = (0, 1, -1)
FAR_STEP = -2
NEAR_STEP = 2
NEAR_AHEAD = 6
VMEM = 62 << 20
CODES = 32000.0
HBM = pl.BlockSpec(memory_space=pltpu.HBM)


def scale_columns(owners, order, jacobian, weight, sizes):
    units = sum(sizes)
    firsts = np.cumsum([0, *sizes])
    rows, zones = jacobian.shape
    groups = rows // ROW_STEP
    batch = 8

    def kernel(owners_ref, order_ref, jac_ref, weight_ref, *refs):
        out_refs, (held, made, in_sems, out_sems) = refs[:-4], refs[-4:]
        cut = zones // 4

        def load(g, q):
            place = (pl.ds(g * ROW_STEP, ROW_STEP), pl.ds(q * cut, cut))
            return pltpu.make_async_copy(jac_ref.at[place], held.at[place], in_sems.at[g, q])

        def store(q):
            unit = made.at[pl.ds(int(firsts[q]), sizes[q])]
            return pltpu.make_async_copy(unit, out_refs[q], out_sems.at[q])

        for g in range(groups):
            for q in range(4):
                load(g, q).start()
        stored = 0
        for g in range(groups):
            for q in range(4):
                load(g, q).wait()
            span = pl.ds(g * ROW_STEP, ROW_STEP)
            root = jnp.sqrt(weight_ref[span, :])

            def unit(u, carry, span=span, root=root):
                base = owners_ref[u] * OWN_BLOCKS
                for b in range(OWN_BLOCKS):
                    start = pl.multiple_of(order_ref[base + b] * BLOCK, BLOCK)
                    piece = held[span, pl.ds(start, BLOCK)].astype(jnp.float32) * root
                    made[u, span, b * BLOCK : (b + 1) * BLOCK] = piece.astype(jnp.bfloat16)
                return carry

            if g < groups - 1:
                lax.fori_loop(0, units, unit, 0)
            else:
                for first in range(0, units, batch):
                    lax.fori_loop(first, first + batch, unit, 0)
                    while stored < len(sizes) and firsts[stored + 1] <= first + batch:
                        store(stored).start()
                        stored += 1
        for q in range(len(sizes)):
            store(q).wait()

    return pl.pallas_call(
        kernel,
        out_shape=[jax.ShapeDtypeStruct((size, rows, WIDTH), jnp.bfloat16) for size in sizes],
        grid_spec=pltpu.PrefetchScalarGridSpec(
            num_scalar_prefetch=2,
            grid=(),
            in_specs=[HBM, pl.BlockSpec(memory_space=pltpu.VMEM)],
            out_specs=[HBM] * len(sizes),
            scratch_shapes=[
                pltpu.VMEM((rows, zones), jnp.bfloat16),
                pltpu.VMEM((units, rows, WIDTH), jnp.bfloat16),
                pltpu.SemaphoreType.DMA((groups, 4)),
                pltpu.SemaphoreType.DMA((len(sizes),)),
            ],
        ),
        compiler_params=pltpu.CompilerParams(vmem_limit_bytes=VMEM),
        cost_estimate=pl.CostEstimate(
            flops=units * rows * WIDTH, bytes_accessed=2 * (rows * zones + units * rows * WIDTH), transcendentals=0
        ),
        name="scale_columns",
    )(owners, order, jacobian, weight)


def code_tile(tile):
    top = jnp.maximum(jnp.max(jnp.abs(tile), axis=0, keepdims=True), 1e-30)
    power = jnp.floor(jnp.log2(top)) + 1.0
    codes = jnp.round(tile * (jnp.exp2(-power) * CODES)).astype(jnp.int32).astype(jnp.int16)
    return codes, power


def decode_tile(codes, power):
    return codes.astype(jnp.int32).astype(jnp.float32) * (jnp.exp2(power) * (1.0 / CODES))


def gram_tiles(pieces, parts, pairs, count):
    rows, width = pieces[0].shape[1:]
    total = len(pieces) * rows
    slots = pairs.shape[0] // 2
    quarter = slots // 4
    strip, deep = 256, 512
    per = deep // rows

    def kernel(pairs_ref, count_ref, *refs):
        piece_refs, (out_ref, held, gram, made, powers, sems, out_sems) = refs[:-7], refs[-7:]

        def store(t):
            return pltpu.make_async_copy(made.at[t], out_ref.at[t], out_sems.at[t])

        def load(p):
            return pltpu.make_async_copy(piece_refs[p].at[parts[p]], held.at[pl.ds(p * rows, rows)], sems.at[p])

        for p in range(len(pieces)):
            load(p).start()
        for first in range(0, len(pieces), per):
            for p in range(first, first + per):
                load(p).wait()
            span = pl.ds(first * rows, deep)

            def multiply(m, carry, first=first, span=span):
                lanes = pl.ds(pl.multiple_of(m * strip, strip), strip)
                part = lax.dot_general(
                    held[span, lanes], held[span, :], (((0,), (0,)), ((), ())), preferred_element_type=jnp.float32
                )
                if first == 0:
                    gram[lanes, :] = part
                else:
                    gram[lanes, :] += part
                return carry

            lax.fori_loop(0, width // strip, multiply, 0)

        for t in range(4):

            def pick(k, carry, t=t):
                slot = t * quarter + k
                row = pl.multiple_of(pairs_ref[2 * slot] * BLOCK, BLOCK)
                col = pl.multiple_of(pairs_ref[2 * slot + 1] * BLOCK, BLOCK)
                tile = gram[pl.ds(row, BLOCK), pl.ds(col, BLOCK)]
                tile = jnp.where(slot < count_ref[0], tile, 0.0)
                codes, power = code_tile(tile)
                made[t, pl.ds(pl.multiple_of(k * BLOCK, BLOCK), BLOCK), :] = codes
                powers[pl.ds(k, 1), :] = power
                return carry

            lax.fori_loop(0, quarter, pick, 0)
            made[t, quarter * BLOCK :, :] = powers[...].astype(jnp.int32).astype(jnp.int16)
            store(t).start()
        for t in range(4):
            store(t).wait()

    return pl.pallas_call(
        kernel,
        out_shape=jax.ShapeDtypeStruct((4, quarter * BLOCK + quarter, BLOCK), jnp.int16),
        grid_spec=pltpu.PrefetchScalarGridSpec(
            num_scalar_prefetch=2,
            grid=(),
            in_specs=[HBM] * len(pieces),
            out_specs=HBM,
            scratch_shapes=[
                pltpu.VMEM((total, width), jnp.bfloat16),
                pltpu.VMEM((width, width), jnp.float32),
                pltpu.VMEM((4, quarter * BLOCK + quarter, BLOCK), jnp.int16),
                pltpu.VMEM((quarter, BLOCK), jnp.float32),
                pltpu.SemaphoreType.DMA((len(pieces),)),
                pltpu.SemaphoreType.DMA((4,)),
            ],
        ),
        compiler_params=pltpu.CompilerParams(vmem_limit_bytes=VMEM),
        cost_estimate=pl.CostEstimate(
            flops=2 * total * width * width, bytes_accessed=2 * total * width + 2 * slots * BLOCK * BLOCK,
            transcendentals=0,
        ),
        name="gram_tiles",
    )(pairs, count, *pieces)


def sum_tiles(parts, coded):
    rows = parts[0].shape[1]
    tiles = rows // (BLOCK + 1)
    sources = sum(p.shape[0] for p in parts)

    def kernel(*refs):
        part_refs, out_ref, powers = refs[: len(parts)], refs[len(parts)], refs[len(parts) + 1]
        scales, at = [], 0
        for ref in part_refs:
            for q in range(ref.shape[0]):
                powers[pl.ds(at * tiles, tiles), :] = ref[q, tiles * BLOCK :, :].astype(jnp.int32).astype(jnp.float32)
                at += 1

        def one(k, carry):
            span = pl.ds(pl.multiple_of(k * BLOCK, BLOCK), BLOCK)
            total, at = None, 0
            for ref in part_refs:
                for q in range(ref.shape[0]):
                    term = decode_tile(ref[q, span, :], powers[pl.ds(at * tiles + k, 1), :])
                    total = term if total is None else total + term
                    at += 1
            if coded:
                codes, power = code_tile(total)
                out_ref[0, span, :] = codes
                powers[pl.ds(sources * tiles + k, 1), :] = power
            else:
                out_ref[k] = total
            return carry

        lax.fori_loop(0, tiles, one, 0)
        if coded:
            own = powers[pl.ds(sources * tiles, tiles), :]
            out_ref[0, tiles * BLOCK :, :] = own.astype(jnp.int32).astype(jnp.int16)

    if coded:
        out = jax.ShapeDtypeStruct((1, rows, BLOCK), jnp.int16)
    else:
        out = jax.ShapeDtypeStruct((tiles, BLOCK, BLOCK), jnp.float32)
    vmem = pl.BlockSpec(memory_space=pltpu.VMEM)
    return pl.pallas_call(
        kernel,
        out_shape=out,
        in_specs=[vmem] * len(parts),
        out_specs=vmem,
        scratch_shapes=[pltpu.VMEM(((sources + 1) * tiles, BLOCK), jnp.float32)],
        compiler_params=pltpu.CompilerParams(vmem_limit_bytes=VMEM),
        cost_estimate=pl.CostEstimate(
            flops=4 * sources * rows * BLOCK, bytes_accessed=2 * (sources + 2) * rows * BLOCK, transcendentals=0
        ),
        name="sum_tiles",
    )(*parts)


def body(jacobian, obs_weight, block_order, tile_pairs, tile_count):
    rows = jacobian.shape[0]
    planes, lines, cores = lax.axis_size("z"), lax.axis_size("x"), lax.axis_size("c")
    x, z, c = lax.axis_index("x"), lax.axis_index("z"), lax.axis_index("c")
    weight = jnp.broadcast_to(obs_weight[:, None], (rows, BLOCK))
    places = [(dx, dc) for dx in range(lines) for dc in range(cores)]

    routes = [(dx, dc, s) for s in BOTH_STEPS for dx, dc in places]
    units = [(dx, dc, s, far) for dx, dc, s in routes for far in (0, 1)]
    sizes = [2] * len(routes)
    for far, s in ((1, FAR_STEP), (0, NEAR_STEP)):
        routes += [(dx, dc, s) for dx, dc in places]
        units += [(dx, dc, s, far) for dx, dc in places]
        sizes += [1] * len(places)
    table = np.array(units, np.int32)
    dest_c = c ^ table[:, 1]
    sign = 1 - 2 * dest_c
    dest_z = z + sign * (table[:, 2] - FAR * table[:, 3]) + planes
    owners = ((x + table[:, 0]) % lines * planes + dest_z % planes) * cores + dest_c

    def moved(value, dx, dc, s):
        if (dx, dc, s) == (0, 0, 0):
            return value
        moves = []
        for a in range(lines):
            for b in range(planes):
                for k in range(cores):
                    to_c = k ^ dc
                    to_z = (b + s * (1 - 2 * to_c)) % planes
                    moves.append(((a * planes + b) * cores + k, ((a + dx) % lines * planes + to_z) * cores + to_c))
        return lax.ppermute(value, ("x", "z", "c"), moves)

    wanted = jnp.concatenate([tile_pairs.reshape(-1), tile_count])
    far_wanted = moved(wanted, 0, 0, FAR)

    parts = scale_columns(owners.astype(jnp.int32), block_order, jacobian, weight, sizes)
    arrived = [moved(part, *route) for part, route in zip(parts, routes)]
    both = len(BOTH_STEPS) * len(places)
    shared, far_only, near_only = arrived[:both], arrived[both : both + len(places)], arrived[both + len(places) :]

    def swapped(pieces, index, table):
        index = [index] * len(shared) + [0] * len(places)
        tiles = gram_tiles(pieces, index, table[:-1], table[-1:])
        return lax.all_to_all(tiles, "y", split_axis=0, concat_axis=0, tiled=True)

    held_back = lax.optimization_barrier((far_only[0], *near_only[:NEAR_AHEAD]))
    far_only, near_only = [held_back[0], *far_only[1:]], [*held_back[1:], *near_only[NEAR_AHEAD:]]
    far = sum_tiles([swapped(shared + far_only, 1, far_wanted)], True)
    near = swapped(shared + near_only, 0, wanted)
    return sum_tiles([near, moved(far, 0, 0, -FAR)], False)


def solution(mesh):
    shape = (4, mesh.shape["obs"] // 8, 2, mesh.shape["tile"])
    chips = jax.sharding.Mesh(mesh.devices.reshape(shape), ("x", "z", "c", "y"))
    everywhere = ("x", "z", "c", "y")
    owner = ("x", "z", "c")
    return jax.shard_map(
        body,
        mesh=chips,
        in_specs=(P(everywhere, None), P(everywhere), P(), P(owner, None, None), P(owner)),
        out_specs=P(everywhere, None, None),
        check_vma=False,
    )
```

time: 288 us -> 275 us (0.955)
  waiting for transfers between devices: 231 us -> 77.4 us
  starting transfers between devices: 12.4 us -> 143 us
  Pallas kernels: 22.5 us -> 47.1 us
  between operations: 14.1 us -> 0.97 us
    all_to_all x1 -> x2, waiting for transfers between devices: 183 us -> 19.5 us  [swapped(): return lax.all_to_all(tiles, 'y', split_axis=0, concat_axis=0, tiled=True)]
    ppermute x0 -> x41, starting transfers between devices: none -> 133 us  [moved(): return lax.ppermute(value, ('x', 'z', 'c'), moves)]
    ppermute x0 -> x41, waiting for transfers between devices: none -> 57.8 us  [moved(): return lax.ppermute(value, ('x', 'z', 'c'), moves)]
    reduce_scatter x1 -> x0, waiting for transfers between devices: 47.8 us -> none  [body(): return lax.psum_scatter(tiles, 'tile', scatter_dimension=0, tiled=True)]
    pallas_call x2 -> x5, Pallas kernels: 22.5 us -> 47.1 us  [the longest x2 28 us: gram_tiles(): pl.pallas_call(kernel, out_shape=jax.ShapeDtypeStruct((4, quarter * BLOCK...]
    unnamed x9 -> x57, local copies, waits for them, and re-layouts: 5.94 us -> 2.32 us
    all_to_all x1 -> x2, starting transfers between devices: 12.3 us -> 9.65 us  [swapped(): return lax.all_to_all(tiles, 'y', split_axis=0, concat_axis=0, tiled=True)]
  transfers between devices with their start and end apart: 2 -> 43, of which waited for: 2 -> 13; matrix products, arithmetic and copies ran while one was open for 0% -> 0% of each run, Pallas kernels for 0% -> 6%
where the time goes in v2:
time: 275 us; the launch traced here: 274 us
  starting transfers between devices  143 us (52%)
  waiting for transfers between devices  77.4 us (28%)
  Pallas kernels  47.1 us (17%)
  local copies, waits for them, and re-layouts  4.91 us (2%)
    ppermute x41, starting transfers between devices, moved(): return lax.ppermute(value, ('x', 'z', 'c'), moves)  133 us
    ppermute x41, waiting for transfers between devices, moved(): return lax.ppermute(value, ('x', 'z', 'c'), moves)  57.8 us
    pallas_call x2, Pallas kernels, gram_tiles(): pl.pallas_call(kernel, out_shape=jax.ShapeDtypeStruct((4, quarter * BLOCK...  28 us
    all_to_all x2, waiting for transfers between devices, swapped(): return lax.all_to_all(tiles, 'y', split_axis=0, concat_axis=0, tiled=True)  19.5 us
    pallas_call x1, Pallas kernels, scale_columns(): pl.pallas_call(kernel, out_shape=[jax.ShapeDtypeStruct((size, rows, WIDTH...  12 us
    all_to_all x2, starting transfers between devices, swapped(): return lax.all_to_all(tiles, 'y', split_axis=0, concat_axis=0, tiled=True)  9.65 us
    pallas_call x2, Pallas kernels, sum_tiles(): pl.pallas_call(kernel, out_shape=out, in_specs=[vmem] * len(parts), out_s...  7.04 us
  transfers between devices with their start and end apart: 43, of which 13 were waited for; matrix products, arithmetic and copies ran while one was open for 0% of the time, Pallas kernels for 6%

profile of v2, /device:TPU:2, one launch (start us, length us, event | category | flops | bytes accessed | tf_op | source)
XLA Modules:
  0.0 274.2 jit_solution(15890062935590605814)
XLA Ops:
  1.2 1.3 broadcast_in_dim.2.weight_ref
  2.6 12.0 %scale_columns.1 = (bf16[2,64,1024]{2,1,0:T(8,128)(2,1)}, bf16[2,64,1024]{2,1,0:T(8,128)(2,1)}, bf16[2,64,1024]{2,1,0:T(8,128)(2,1)}, bf16[2,64,1024]{2,1,0:T(8,...) custom-call(s32[64]{0:T(128)} %xor_add_fusion.owners_ref, ...), custom_call_target="tpu_custom_call" | custom-call | flops 4194304 | bytes 16777216 | tf_op jit(solution)/shard_map/scale_columns/pallas_call | solution.py:71
  14.6 6.4 %collective-permute-start.23 = (bf16[1,64,1024]{2,1,0:T(8,128)(2,1)}, bf16[1,64,1024]{2,1,0:T(8,128)(2,1)S(1)}, u32[]{:S(2)}, u32[]{:S(2)}) collective-permute-start(bf16[1,64,1024]{2,1,0:T(8,128)(2,1)} %get-tuple-element.76), channel_id=1, source_target_pairs={{0,48},{4,20},{8,56},{12,28},{16,0},{20,36},{24,8},{28,44},{32,16}... | collective-permute-start | bytes 393224 | tf_op jit(solution)/shard_map/ppermute | solution.py:270
  22.0 2.4 collective-permute-start.24
  25.5 3.5 %collective-permute-start.26 = (bf16[1,64,1024]{2,1,0:T(8,128)(2,1)}, bf16[1,64,1024]{2,1,0:T(8,128)(2,1)S(1)}, u32[]{:S(2)}, u32[]{:S(2)}) collective-permute-start(bf16[1,64,1024]{2,1,0:T(8,128)(2,1)} %get-tuple-element.79), channel_id=1, source_target_pairs={{0,80},{4,116},{8,88},{12,124},{16,96},{20,68},{24,104},{28,76},{3... | collective-permute-start | bytes 393224 | tf_op jit(solution)/shard_map/ppermute | solution.py:270
  29.0 1.5 collective-permute-start.27
  31.2 2.8 %collective-permute-start.28 = (bf16[1,64,1024]{2,1,0:T(8,128)(2,1)}, bf16[1,64,1024]{2,1,0:T(8,128)(2,1)S(1)}, u32[]{:S(2)}, u32[]{:S(2)}) collective-permute-start(bf16[1,64,1024]{2,1,0:T(8,128)(2,1)} %get-tuple-element.81), channel_id=1, source_target_pairs={{0,144},{4,180},{8,152},{12,188},{16,160},{20,132},{24,168},{28,14... | collective-permute-start | bytes 393224 | tf_op jit(solution)/shard_map/ppermute | solution.py:270
  34.0 3.8 %collective-permute-start.29 = (bf16[1,64,1024]{2,1,0:T(8,128)(2,1)}, bf16[1,64,1024]{2,1,0:T(8,128)(2,1)S(1)}, u32[]{:S(2)}, u32[]{:S(2)}) collective-permute-start(bf16[1,64,1024]{2,1,0:T(8,128)(2,1)} %get-tuple-element.82), channel_id=1, source_target_pairs={{0,180},{4,144},{8,188},{12,152},{16,132},{20,160},{24,140},{28,16... | collective-permute-start | bytes 393224 | tf_op jit(solution)/shard_map/ppermute | solution.py:270
  37.8 2.6 collective-permute-start.33
  40.4 1.5 collective-permute-start.34
  41.9 2.6 collective-permute-start.35
  44.5 6.2 %collective-permute-done.28.refs_28_ = bf16[1,64,1024]{2,1,0:T(8,128)(2,1)S(1)} collective-permute-done((bf16[1,64,1024]{2,1,0:T(8,128)(2,1)}, bf16[1,64,1024]{2,1,0:T(8,128)(2,1)S(1)}, u32[]{:S(2)}, u32[]{:S(2)}) %collective-permute-start.28) | collective-permute-done | bytes 131104 | tf_op jit(solution)/shard_map/ppermute | solution.py:270
  51.5 3.5 %collective-permute-start = (bf16[2,64,1024]{2,1,0:T(8,128)(2,1)}, bf16[2,64,1024]{2,1,0:T(8,128)(2,1)S(1)}, u32[]{:S(2)}, u32[]{:S(2)}) collective-permute-start(bf16[2,64,1024]{2,1,0:T(8,128)(2,1)} %get-tuple-element.53), channel_id=1, source_target_pairs={{0,4},{4,0},{8,12},{12,8},{16,20},{20,16},{24,28},{28,24},{32,36},... | collective-permute-start | bytes 786440 | tf_op jit(solution)/shard_map/ppermute | solution.py:270
  55.1 1.9 collective-permute-start.2
  57.1 5.0 %collective-permute-done.36.refs_28_ = bf16[1,64,1024]{2,1,0:T(8,128)(2,1)S(1)} collective-permute-done((bf16[1,64,1024]{2,1,0:T(8,128)(2,1)}, bf16[1,64,1024]{2,1,0:T(8,128)(2,1)S(1)}, u32[]{:S(2)}, u32[]{:S(2)}) %collective-permute-start.36) | collective-permute-done | bytes 131104 | tf_op jit(solution)/shard_map/ppermute | solution.py:270
  62.1 8.7 %collective-permute-start.38 = (bf16[1,64,1024]{2,1,0:T(8,128)(2,1)}, bf16[1,64,1024]{2,1,0:T(8,128)(2,1)S(1)}, u32[]{:S(2)}, u32[]{:S(2)}) collective-permute-start(bf16[1,64,1024]{2,1,0:T(8,128)(2,1)} %get-tuple-element.97), channel_id=1, source_target_pairs={{0,240},{4,212},{8,248},{12,220},{16,192},{20,228},{24,200},{28,23... | collective-permute-start | bytes 393224 | tf_op jit(solution)/shard_map/ppermute | solution.py:270
  70.8 11.8 %collective-permute-start.39 = (bf16[1,64,1024]{2,1,0:T(8,128)(2,1)}, bf16[1,64,1024]{2,1,0:T(8,128)(2,1)S(1)}, u32[]{:S(2)}, u32[]{:S(2)}) collective-permute-start(bf16[1,64,1024]{2,1,0:T(8,128)(2,1)} %get-tuple-element.98), channel_id=1, source_target_pairs={{0,212},{4,240},{8,220},{12,248},{16,228},{20,192},{24,236},{28,20... | collective-permute-start | bytes 393224 | tf_op jit(solution)/shard_map/ppermute | solution.py:270
  82.7 2.2 collective-permute-start.3
  84.8 5.6 %collective-permute-done.39.refs_31_ = bf16[1,64,1024]{2,1,0:T(8,128)(2,1)S(1)} collective-permute-done((bf16[1,64,1024]{2,1,0:T(8,128)(2,1)}, bf16[1,64,1024]{2,1,0:T(8,128)(2,1)S(1)}, u32[]{:S(2)}, u32[]{:S(2)}) %collective-permute-start.39) | collective-permute-done | bytes 131104 | tf_op jit(solution)/shard_map/ppermute | solution.py:270
  90.4 3.8 %collective-permute-start.4 = (bf16[2,64,1024]{2,1,0:T(8,128)(2,1)}, bf16[2,64,1024]{2,1,0:T(8,128)(2,1)S(1)}, u32[]{:S(2)}, u32[]{:S(2)}) collective-permute-start(bf16[2,64,1024]{2,1,0:T(8,128)(2,1)} %get-tuple-element.57), channel_id=1, source_target_pairs={{0,132},{4,128},{8,140},{12,136},{16,148},{20,144},{24,156},{28,15... | collective-permute-start | bytes 786440 | tf_op jit(solution)/shard_map/ppermute | solution.py:270
  95.6 1.4 collective-permute-start.7
  97.1 2.7 collective-permute-start.8
  99.8 1.5 collective-permute-done.4.refs_5_
  101.3 5.7 %collective-permute-done.5.refs_6_ = bf16[2,64,1024]{2,1,0:T(8,128)(2,1)S(1)} collective-permute-done((bf16[2,64,1024]{2,1,0:T(8,128)(2,1)}, bf16[2,64,1024]{2,1,0:T(8,128)(2,1)S(1)}, u32[]{:S(2)}, u32[]{:S(2)}) %collective-permute-start.5) | collective-permute-done | bytes 262176 | tf_op jit(solution)/shard_map/ppermute | solution.py:270
  107.0 2.4 collective-permute-start.10
  109.3 3.0 %collective-permute-done.6.refs_7_ = bf16[2,64,1024]{2,1,0:T(8,128)(2,1)S(1)} collective-permute-done((bf16[2,64,1024]{2,1,0:T(8,128)(2,1)}, bf16[2,64,1024]{2,1,0:T(8,128)(2,1)S(1)}, u32[]{:S(2)}, u32[]{:S(2)}) %collective-permute-start.6) | collective-permute-done | bytes 262176 | tf_op jit(solution)/shard_map/ppermute | solution.py:270
  112.4 3.1 %collective-permute-start.11 = (bf16[2,64,1024]{2,1,0:T(8,128)(2,1)}, bf16[2,64,1024]{2,1,0:T(8,128)(2,1)}, u32[]{:S(2)}, u32[]{:S(2)}) collective-permute-start(bf16[2,64,1024]{2,1,0:T(8,128)(2,1)} %get-tuple-element.64), channel_id=1, source_target_pairs={{0,136},{4,188},{8,144},{12,132},{16,152},{20,140},{24,160},{28,14... | collective-permute-start | bytes 786440 | tf_op jit(solution)/shard_map/ppermute | solution.py:270
  115.5 3.2 %collective-permute-start.12 = (bf16[2,64,1024]{2,1,0:T(8,128)(2,1)}, bf16[2,64,1024]{2,1,0:T(8,128)(2,1)}, u32[]{:S(2)}, u32[]{:S(2)}) collective-permute-start(bf16[2,64,1024]{2,1,0:T(8,128)(2,1)} %get-tuple-element.65), channel_id=1, source_target_pairs={{0,188},{4,136},{8,132},{12,144},{16,140},{20,152},{24,148},{28,16... | collective-permute-start | bytes 786440 | tf_op jit(solution)/shard_map/ppermute | solution.py:270
  119.6 9.9 %collective-permute-start.14 = (bf16[2,64,1024]{2,1,0:T(8,128)(2,1)}, bf16[2,64,1024]{2,1,0:T(8,128)(2,1)}, u32[]{:S(2)}, u32[]{:S(2)}) collective-permute-start(bf16[2,64,1024]{2,1,0:T(8,128)(2,1)} %get-tuple-element.67), channel_id=1, source_target_pairs={{0,252},{4,200},{8,196},{12,208},{16,204},{20,216},{24,212},{28,22... | collective-permute-start | bytes 786440 | tf_op jit(solution)/shard_map/ppermute | solution.py:270
  129.5 4.4 %collective-permute-start.15 = (bf16[2,64,1024]{2,1,0:T(8,128)(2,1)}, bf16[2,64,1024]{2,1,0:T(8,128)(2,1)}, u32[]{:S(2)}, u32[]{:S(2)}) collective-permute-start(bf16[2,64,1024]{2,1,0:T(8,128)(2,1)} %get-tuple-element.68), channel_id=1, source_target_pairs={{0,56},{4,12},{8,0},{12,20},{16,8},{20,28},{24,16},{28,36},{32,24}... | collective-permute-start | bytes 786440 | tf_op jit(solution)/shard_map/ppermute | solution.py:270
  134.0 2.2 collective-permute-start.17
  138.4 2.8 %collective-permute-done.14.refs_15_ = bf16[2,64,1024]{2,1,0:T(8,128)(2,1)} collective-permute-done((bf16[2,64,1024]{2,1,0:T(8,128)(2,1)}, bf16[2,64,1024]{2,1,0:T(8,128)(2,1)}, u32[]{:S(2)}, u32[]{:S(2)}) %collective-permute-start.14) | collective-permute-done | bytes 262176 | tf_op jit(solution)/shard_map/ppermute | solution.py:270
  141.2 5.5 %collective-permute-start.19 = (bf16[2,64,1024]{2,1,0:T(8,128)(2,1)}, bf16[2,64,1024]{2,1,0:T(8,128)(2,1)}, u32[]{:S(2)}, u32[]{:S(2)}) collective-permute-start(bf16[2,64,1024]{2,1,0:T(8,128)(2,1)} %get-tuple-element.72), channel_id=1, source_target_pairs={{0,184},{4,140},{8,128},{12,148},{16,136},{20,156},{24,144},{28,16... | collective-permute-start | bytes 786440 | tf_op jit(solution)/shard_map/ppermute | solution.py:270
  146.7 1.3 collective-permute-start.20
  148.0 10.9 %collective-permute-start.21 = (bf16[2,64,1024]{2,1,0:T(8,128)(2,1)}, bf16[2,64,1024]{2,1,0:T(8,128)(2,1)}, u32[]{:S(2)}, u32[]{:S(2)}) collective-permute-start(bf16[2,64,1024]{2,1,0:T(8,128)(2,1)} %get-tuple-element.74), channel_id=1, source_target_pairs={{0,248},{4,204},{8,192},{12,212},{16,200},{20,220},{24,208},{28,22... | collective-permute-start | bytes 786440 | tf_op jit(solution)/shard_map/ppermute | solution.py:270
  159.0 2.7 collective-permute-done.17.refs_18_
  162.8 14.1 %collective-permute-done.21.refs_22_ = bf16[2,64,1024]{2,1,0:T(8,128)(2,1)} collective-permute-done((bf16[2,64,1024]{2,1,0:T(8,128)(2,1)}, bf16[2,64,1024]{2,1,0:T(8,128)(2,1)}, u32[]{:S(2)}, u32[]{:S(2)}) %collective-permute-start.21) | collective-permute-done | bytes 262176 | tf_op jit(solution)/shard_map/ppermute | solution.py:270
  176.9 14.3 %gram_tiles.3 = s16[4,2064,128]{2,1,0:T(8,128)(2,1)} custom-call(s32[128]{0:T(128)} %slice.6.pairs_ref, s32[1]{0:T(128)} %slice.7.count_ref, bf16[2,64,1024]{2,1,0:T(8,128)(2,1)} %get-tuple-element.52.refs_0_, bf16[2,64,1024]{2,1,0:T(8,128)(2,1)} %copy-done.3, bf16[2,64,1024]{2,1,0:T(8,128)(2,1)} %copy-done.4, bf16[2,64,1024]{2,1,0:T(8,128)(2,1)} %copy-done.5, ...), custom_call_target="tpu_custom_call" | custom-call | flops 4294967296 | bytes 6291456 | tf_op jit(solution)/shard_map/gram_tiles/pallas_call | solution.py:161
  191.3 4.6 %all-to-all-start.1 = ((s16[4,2064,128]{2,1,0:T(8,128)(2,1)}), s16[4,2064,128]{2,1,0:T(8,128)(2,1)}, u32[]{:S(2)}, u32[]{:S(2)}) async-start(s16[4,2064,128]{2,1,0:T(8,128)(2,1)} %gram_tiles.3), calls=%async_computation.1 | async-start | bytes 4227072 | tf_op jit(solution)/shard_map/all_to_all | solution.py:283
  195.9 8.0 %collective-permute-start.30 = (bf16[1,64,1024]{2,1,0:T(8,128)(2,1)S(1)}, bf16[1,64,1024]{2,1,0:T(8,128)(2,1)S(1)}, u32[]{:S(2)}, u32[]{:S(2)}) collective-permute-start(bf16[1,64,1024]{2,1,0:T(8,128)(2,1)S(1)} %copy-done.11), channel_id=1, source_target_pairs={{0,208},{4,244},{8,216},{12,252},{16,224},{20,196},{24,232},{28,20... | collective-permute-start | bytes 393224 | tf_op jit(solution)/shard_map/ppermute | solution.py:270
  204.0 11.8 %collective-permute-start.31 = (bf16[1,64,1024]{2,1,0:T(8,128)(2,1)S(1)}, bf16[1,64,1024]{2,1,0:T(8,128)(2,1)S(1)}, u32[]{:S(2)}, u32[]{:S(2)}) collective-permute-start(bf16[1,64,1024]{2,1,0:T(8,128)(2,1)S(1)} %copy-done.10), channel_id=1, source_target_pairs={{0,244},{4,208},{8,252},{12,216},{16,196},{20,224},{24,204},{28,23... | collective-permute-start | bytes 393224 | tf_op jit(solution)/shard_map/ppermute | solution.py:270
  215.8 9.1 %collective-permute-done.31.refs_31_ = bf16[1,64,1024]{2,1,0:T(8,128)(2,1)S(1)} collective-permute-done((bf16[1,64,1024]{2,1,0:T(8,128)(2,1)S(1)}, bf16[1,64,1024]{2,1,0:T(8,128)(2,1)S(1)}, u32[]{:S(2)}, u32[]{:S(2)}) %collective-permute-start.31) | collective-permute-done | bytes 131104 | tf_op jit(solution)/shard_map/ppermute | solution.py:270
  225.6 13.7 %gram_tiles.2 = s16[4,2064,128]{2,1,0:T(8,128)(2,1)} custom-call(s32[128]{0:T(128)} %copy-done.1, s32[1]{0:T(128)S(6)} %copy.11.count_ref, bf16[2,64,1024]{2,1,0:T(8,128)(2,1)} %get-tuple-element.52.refs_0_, bf16[2,64,1024]{2,1,0:T(8,128)(2,1)} %copy-done.3, bf16[2,64,1024]{2,1,0:T(8,128)(2,1)} %copy-done.4, bf16[2,64,1024]{2,1,0:T(8,128)(2,1)} %copy-done.5, ...), custom_call_target="tpu_custom_call" | custom-call | flops 4294967296 | bytes 6291456 | tf_op jit(solution)/shard_map/gram_tiles/pallas_call | solution.py:161
  239.3 5.0 %all-to-all-start = ((s16[4,2064,128]{2,1,0:T(8,128)(2,1)}), s16[4,2064,128]{2,1,0:T(8,128)(2,1)}, u32[]{:S(2)}, u32[]{:S(2)}) async-start(s16[4,2064,128]{2,1,0:T(8,128)(2,1)} %gram_tiles.2), calls=%async_computation | async-start | bytes 4227072 | tf_op jit(solution)/shard_map/all_to_all | solution.py:283
  244.4 3.6 %sum_tiles.2 = s16[1,2064,128]{2,1,0:T(8,128)(2,1)} custom-call(s16[4,2064,128]{2,1,0:T(8,128)(2,1)} %all-to-all-done.1.refs_0_), custom_call_target="tpu_custom_call" | custom-call | flops 4227072 | bytes 3170304 | tf_op jit(solution)/shard_map/sum_tiles/pallas_call | solution.py:226
  248.0 2.4 collective-permute-start.40
  250.4 19.5 %all-to-all-done.refs_0_ = s16[4,2064,128]{2,1,0:T(8,128)(2,1)} async-done(((s16[4,2064,128]{2,1,0:T(8,128)(2,1)}), s16[4,2064,128]{2,1,0:T(8,128)(2,1)}, u32[]{:S(2)}, u32[]{:S(2)}) %all-to-all-start) | async-done | bytes 2113568 | tf_op jit(solution)/shard_map/all_to_all | solution.py:283
  270.7 3.5 %sum_tiles.3 = f32[16,128,128]{2,1,0:T(8,128)} custom-call(s16[4,2064,128]{2,1,0:T(8,128)(2,1)} %all-to-all-done.refs_0_, s16[1,2064,128]{2,1,0:T(8,128)(2,1)} %copy-done), custom_call_target="tpu_custom_call" | custom-call | flops 5283840 | bytes 3698688 | tf_op jit(solution)/shard_map/sum_tiles/pallas_call | solution.py:226
  (106 shorter events, 11.4 us)
Async XLA Ops:
  14.6 15.9 %collective-permute-start.23 = (bf16[1,64,1024]{2,1,0:T(8,128)(2,1)}, bf16[1,64,1024]{2,1,0:T(8,128)(2,1)S(1)}, u32[]{:S(2)}, u32[]{:S(2)}) collective-permute-start(bf16[1,64,1024]{2,1,0:T(8,128)(2,1)} %get-tuple-element.76), channel_id=1, source_target_pairs={{0,48},{4,20},{8,56},{12,28},{16,0},{20,36},{24,8},{28,44},{32,16}... | collective-permute-start | bytes 393224 | tf_op jit(solution)/shard_map/ppermute | solution.py:270
  21.9 169.4 %copy-start.1 = (s32[128]{0:T(128)}, s32[128]{0:T(128)S(1)}, u32[]{:S(2)}) copy-start(s32[128]{0:T(128)S(1)} %reshape.4.pairs_ref) | copy-start | bytes 1540
  21.9 7.1 %collective-permute-start.32 = (s32[129]{0:T(256)S(1)}, s32[129]{0:T(256)S(1)}, u32[]{:S(2)}, u32[]{:S(2)}) collective-permute-start(s32[129]{0:T(256)S(1)} %pad_add_fusion), channel_id=1, source_target_pairs={{0,24},{4,44},{8,32},{12,52},{16,40},{20,60},{24,48},{28,4},{32,56... | collective-permute-start | bytes 1556 | tf_op jit(solution)/shard_map/ppermute | solution.py:270
  22.0 12.0 %collective-permute-start.24 = (bf16[1,64,1024]{2,1,0:T(8,128)(2,1)}, bf16[1,64,1024]{2,1,0:T(8,128)(2,1)S(1)}, u32[]{:S(2)}, u32[]{:S(2)}) collective-permute-start(bf16[1,64,1024]{2,1,0:T(8,128)(2,1)} %get-tuple-element.77), channel_id=1, source_target_pairs={{0,16},{4,52},{8,24},{12,60},{16,32},{20,4},{24,40},{28,12},{32,48... | collective-permute-start | bytes 393224 | tf_op jit(solution)/shard_map/ppermute | solution.py:270
  24.4 13.3 %collective-permute-start.25 = (bf16[1,64,1024]{2,1,0:T(8,128)(2,1)}, bf16[1,64,1024]{2,1,0:T(8,128)(2,1)S(1)}, u32[]{:S(2)}, u32[]{:S(2)}) collective-permute-start(bf16[1,64,1024]{2,1,0:T(8,128)(2,1)} %get-tuple-element.78), channel_id=1, source_target_pairs={{0,52},{4,16},{8,60},{12,24},{16,4},{20,32},{24,12},{28,40},{32,20... | collective-permute-start | bytes 393224 | tf_op jit(solution)/shard_map/ppermute | solution.py:270
  25.5 14.9 %collective-permute-start.26 = (bf16[1,64,1024]{2,1,0:T(8,128)(2,1)}, bf16[1,64,1024]{2,1,0:T(8,128)(2,1)S(1)}, u32[]{:S(2)}, u32[]{:S(2)}) collective-permute-start(bf16[1,64,1024]{2,1,0:T(8,128)(2,1)} %get-tuple-element.79), channel_id=1, source_target_pairs={{0,80},{4,116},{8,88},{12,124},{16,96},{20,68},{24,104},{28,76},{3... | collective-permute-start | bytes 393224 | tf_op jit(solution)/shard_map/ppermute | solution.py:270
  29.0 12.9 %collective-permute-start.27 = (bf16[1,64,1024]{2,1,0:T(8,128)(2,1)}, bf16[1,64,1024]{2,1,0:T(8,128)(2,1)S(1)}, u32[]{:S(2)}, u32[]{:S(2)}) collective-permute-start(bf16[1,64,1024]{2,1,0:T(8,128)(2,1)} %get-tuple-element.80), channel_id=1, source_target_pairs={{0,116},{4,80},{8,124},{12,88},{16,68},{20,96},{24,76},{28,104},{3... | collective-permute-start | bytes 393224 | tf_op jit(solution)/shard_map/ppermute | solution.py:270
  31.2 19.6 %collective-permute-start.28 = (bf16[1,64,1024]{2,1,0:T(8,128)(2,1)}, bf16[1,64,1024]{2,1,0:T(8,128)(2,1)S(1)}, u32[]{:S(2)}, u32[]{:S(2)}) collective-permute-start(bf16[1,64,1024]{2,1,0:T(8,128)(2,1)} %get-tuple-element.81), channel_id=1, source_target_pairs={{0,144},{4,180},{8,152},{12,188},{16,160},{20,132},{24,168},{28,14... | collective-permute-start | bytes 393224 | tf_op jit(solution)/shard_map/ppermute | solution.py:270
  34.0 157.3 %copy-start.12 = (bf16[1,64,1024]{2,1,0:T(8,128)(2,1)}, bf16[1,64,1024]{2,1,0:T(8,128)(2,1)S(1)}, u32[]{:S(2)}) copy-start(bf16[1,64,1024]{2,1,0:T(8,128)(2,1)S(1)} %collective-permute-done.24.refs_24_) | copy-start | bytes 393220
  34.0 17.5 %collective-permute-start.29 = (bf16[1,64,1024]{2,1,0:T(8,128)(2,1)}, bf16[1,64,1024]{2,1,0:T(8,128)(2,1)S(1)}, u32[]{:S(2)}, u32[]{:S(2)}) collective-permute-start(bf16[1,64,1024]{2,1,0:T(8,128)(2,1)} %get-tuple-element.82), channel_id=1, source_target_pairs={{0,180},{4,144},{8,188},{12,152},{16,132},{20,160},{24,140},{28,16... | collective-permute-start | bytes 393224 | tf_op jit(solution)/shard_map/ppermute | solution.py:270
  37.8 13.7 %collective-permute-start.33 = (bf16[1,64,1024]{2,1,0:T(8,128)(2,1)}, bf16[1,64,1024]{2,1,0:T(8,128)(2,1)S(1)}, u32[]{:S(2)}, u32[]{:S(2)}) collective-permute-start(bf16[1,64,1024]{2,1,0:T(8,128)(2,1)} %get-tuple-element.92), channel_id=1, source_target_pairs={{0,20},{4,48},{8,28},{12,56},{16,36},{20,0},{24,44},{28,8},{32,52}... | collective-permute-start | bytes 393224 | tf_op jit(solution)/shard_map/ppermute | solution.py:270
  40.4 14.6 %collective-permute-start.34 = (bf16[1,64,1024]{2,1,0:T(8,128)(2,1)}, bf16[1,64,1024]{2,1,0:T(8,128)(2,1)S(1)}, u32[]{:S(2)}, u32[]{:S(2)}) collective-permute-start(bf16[1,64,1024]{2,1,0:T(8,128)(2,1)} %get-tuple-element.93), channel_id=1, source_target_pairs={{0,112},{4,84},{8,120},{12,92},{16,64},{20,100},{24,72},{28,108},{... | collective-permute-start | bytes 393224 | tf_op jit(solution)/shard_map/ppermute | solution.py:270
  41.9 13.2 %collective-permute-start.35 = (bf16[1,64,1024]{2,1,0:T(8,128)(2,1)}, bf16[1,64,1024]{2,1,0:T(8,128)(2,1)S(1)}, u32[]{:S(2)}, u32[]{:S(2)}) collective-permute-start(bf16[1,64,1024]{2,1,0:T(8,128)(2,1)} %get-tuple-element.94), channel_id=1, source_target_pairs={{0,84},{4,112},{8,92},{12,120},{16,100},{20,64},{24,108},{28,72},{... | collective-permute-start | bytes 393224 | tf_op jit(solution)/shard_map/ppermute | solution.py:270
  50.7 11.3 %collective-permute-start.36 = (bf16[1,64,1024]{2,1,0:T(8,128)(2,1)}, bf16[1,64,1024]{2,1,0:T(8,128)(2,1)S(1)}, u32[]{:S(2)}, u32[]{:S(2)}) collective-permute-start(bf16[1,64,1024]{2,1,0:T(8,128)(2,1)} %get-tuple-element.95), channel_id=1, source_target_pairs={{0,176},{4,148},{8,184},{12,156},{16,128},{20,164},{24,136},{28,17... | collective-permute-start | bytes 393224 | tf_op jit(solution)/shard_map/ppermute | solution.py:270
  51.5 19.3 %collective-permute-start.37 = (bf16[1,64,1024]{2,1,0:T(8,128)(2,1)}, bf16[1,64,1024]{2,1,0:T(8,128)(2,1)S(1)}, u32[]{:S(2)}, u32[]{:S(2)}) collective-permute-start(bf16[1,64,1024]{2,1,0:T(8,128)(2,1)} %get-tuple-element.96), channel_id=1, source_target_pairs={{0,148},{4,176},{8,156},{12,184},{16,164},{20,128},{24,172},{28,13... | collective-permute-start | bytes 393224 | tf_op jit(solution)/shard_map/ppermute | solution.py:270
  51.5 42.6 %collective-permute-start = (bf16[2,64,1024]{2,1,0:T(8,128)(2,1)}, bf16[2,64,1024]{2,1,0:T(8,128)(2,1)S(1)}, u32[]{:S(2)}, u32[]{:S(2)}) collective-permute-start(bf16[2,64,1024]{2,1,0:T(8,128)(2,1)} %get-tuple-element.53), channel_id=1, source_target_pairs={{0,4},{4,0},{8,12},{12,8},{16,20},{20,16},{24,28},{28,24},{32,36},... | collective-permute-start | bytes 786440 | tf_op jit(solution)/shard_map/ppermute | solution.py:270
  55.0 40.5 %collective-permute-start.1 = (bf16[2,64,1024]{2,1,0:T(8,128)(2,1)}, bf16[2,64,1024]{2,1,0:T(8,128)(2,1)S(1)}, u32[]{:S(2)}, u32[]{:S(2)}) collective-permute-start(bf16[2,64,1024]{2,1,0:T(8,128)(2,1)} %get-tuple-element.54), channel_id=1, source_target_pairs={{0,64},{4,68},{8,72},{12,76},{16,80},{20,84},{24,88},{28,92},{32,9... | collective-permute-start | bytes 786440 | tf_op jit(solution)/shard_map/ppermute | solution.py:270
  55.1 40.5 %collective-permute-start.2 = (bf16[2,64,1024]{2,1,0:T(8,128)(2,1)}, bf16[2,64,1024]{2,1,0:T(8,128)(2,1)S(1)}, u32[]{:S(2)}, u32[]{:S(2)}) collective-permute-start(bf16[2,64,1024]{2,1,0:T(8,128)(2,1)} %get-tuple-element.55), channel_id=1, source_target_pairs={{0,68},{4,64},{8,76},{12,72},{16,84},{20,80},{24,92},{28,88},{32,1... | collective-permute-start | bytes 786440 | tf_op jit(solution)/shard_map/ppermute | solution.py:270
  62.1 20.6 %collective-permute-start.38 = (bf16[1,64,1024]{2,1,0:T(8,128)(2,1)}, bf16[1,64,1024]{2,1,0:T(8,128)(2,1)S(1)}, u32[]{:S(2)}, u32[]{:S(2)}) collective-permute-start(bf16[1,64,1024]{2,1,0:T(8,128)(2,1)} %get-tuple-element.97), channel_id=1, source_target_pairs={{0,240},{4,212},{8,248},{12,220},{16,192},{20,228},{24,200},{28,23... | collective-permute-start | bytes 393224 | tf_op jit(solution)/shard_map/ppermute | solution.py:270
  70.8 19.6 %collective-permute-start.39 = (bf16[1,64,1024]{2,1,0:T(8,128)(2,1)}, bf16[1,64,1024]{2,1,0:T(8,128)(2,1)S(1)}, u32[]{:S(2)}, u32[]{:S(2)}) collective-permute-start(bf16[1,64,1024]{2,1,0:T(8,128)(2,1)} %get-tuple-element.98), channel_id=1, source_target_pairs={{0,212},{4,240},{8,220},{12,248},{16,228},{20,192},{24,236},{28,20... | collective-permute-start | bytes 393224 | tf_op jit(solution)/shard_map/ppermute | solution.py:270
  82.7 14.4 %collective-permute-start.3 = (bf16[2,64,1024]{2,1,0:T(8,128)(2,1)}, bf16[2,64,1024]{2,1,0:T(8,128)(2,1)S(1)}, u32[]{:S(2)}, u32[]{:S(2)}) collective-permute-start(bf16[2,64,1024]{2,1,0:T(8,128)(2,1)} %get-tuple-element.56), channel_id=1, source_target_pairs={{0,128},{4,132},{8,136},{12,140},{16,144},{20,148},{24,152},{28,15... | collective-permute-start | bytes 786440 | tf_op jit(solution)/shard_map/ppermute | solution.py:270
  90.4 10.9 %collective-permute-start.4 = (bf16[2,64,1024]{2,1,0:T(8,128)(2,1)}, bf16[2,64,1024]{2,1,0:T(8,128)(2,1)S(1)}, u32[]{:S(2)}, u32[]{:S(2)}) collective-permute-start(bf16[2,64,1024]{2,1,0:T(8,128)(2,1)} %get-tuple-element.57), channel_id=1, source_target_pairs={{0,132},{4,128},{8,140},{12,136},{16,148},{20,144},{24,156},{28,15... | collective-permute-start | bytes 786440 | tf_op jit(solution)/shard_map/ppermute | solution.py:270
  94.2 82.7 %copy-start.3 = (bf16[2,64,1024]{2,1,0:T(8,128)(2,1)}, bf16[2,64,1024]{2,1,0:T(8,128)(2,1)S(1)}, u32[]{:S(2)}) copy-start(bf16[2,64,1024]{2,1,0:T(8,128)(2,1)S(1)} %collective-permute-done.refs_1_) | copy-start | bytes 786436
  94.2 12.8 %collective-permute-start.5 = (bf16[2,64,1024]{2,1,0:T(8,128)(2,1)}, bf16[2,64,1024]{2,1,0:T(8,128)(2,1)S(1)}, u32[]{:S(2)}, u32[]{:S(2)}) collective-permute-start(bf16[2,64,1024]{2,1,0:T(8,128)(2,1)} %get-tuple-element.58), channel_id=1, source_target_pairs={{0,192},{4,196},{8,200},{12,204},{16,208},{20,212},{24,216},{28,22... | collective-permute-start | bytes 786440 | tf_op jit(solution)/shard_map/ppermute | solution.py:270
  95.5 81.4 %copy-start.4 = (bf16[2,64,1024]{2,1,0:T(8,128)(2,1)}, bf16[2,64,1024]{2,1,0:T(8,128)(2,1)S(1)}, u32[]{:S(2)}) copy-start(bf16[2,64,1024]{2,1,0:T(8,128)(2,1)S(1)} %collective-permute-done.1.refs_2_) | copy-start | bytes 786436
  95.5 16.9 %collective-permute-start.6 = (bf16[2,64,1024]{2,1,0:T(8,128)(2,1)}, bf16[2,64,1024]{2,1,0:T(8,128)(2,1)S(1)}, u32[]{:S(2)}, u32[]{:S(2)}) collective-permute-start(bf16[2,64,1024]{2,1,0:T(8,128)(2,1)} %get-tuple-element.59), channel_id=1, source_target_pairs={{0,196},{4,192},{8,204},{12,200},{16,212},{20,208},{24,220},{28,21... | collective-permute-start | bytes 786440 | tf_op jit(solution)/shard_map/ppermute | solution.py:270
  95.6 81.3 %copy-start.5 = (bf16[2,64,1024]{2,1,0:T(8,128)(2,1)}, bf16[2,64,1024]{2,1,0:T(8,128)(2,1)S(1)}, u32[]{:S(2)}) copy-start(bf16[2,64,1024]{2,1,0:T(8,128)(2,1)S(1)} %collective-permute-done.2.refs_3_) | copy-start | bytes 786436
  95.6 19.9 %collective-permute-start.7 = (bf16[2,64,1024]{2,1,0:T(8,128)(2,1)}, bf16[2,64,1024]{2,1,0:T(8,128)(2,1)}, u32[]{:S(2)}, u32[]{:S(2)}) collective-permute-start(bf16[2,64,1024]{2,1,0:T(8,128)(2,1)} %get-tuple-element.60), channel_id=1, source_target_pairs={{0,8},{4,60},{8,16},{12,4},{16,24},{20,12},{24,32},{28,20},{32,40}... | collective-permute-start | bytes 786440 | tf_op jit(solution)/shard_map/ppermute | solution.py:270
  97.1 21.6 %collective-permute-start.8 = (bf16[2,64,1024]{2,1,0:T(8,128)(2,1)}, bf16[2,64,1024]{2,1,0:T(8,128)(2,1)}, u32[]{:S(2)}, u32[]{:S(2)}) collective-permute-start(bf16[2,64,1024]{2,1,0:T(8,128)(2,1)} %get-tuple-element.61), channel_id=1, source_target_pairs={{0,60},{4,8},{8,4},{12,16},{16,12},{20,24},{24,20},{28,32},{32,28}... | collective-permute-start | bytes 786440 | tf_op jit(solution)/shard_map/ppermute | solution.py:270
  101.3 18.3 %collective-permute-start.9 = (bf16[2,64,1024]{2,1,0:T(8,128)(2,1)}, bf16[2,64,1024]{2,1,0:T(8,128)(2,1)}, u32[]{:S(2)}, u32[]{:S(2)}) collective-permute-start(bf16[2,64,1024]{2,1,0:T(8,128)(2,1)} %get-tuple-element.62), channel_id=1, source_target_pairs={{0,72},{4,124},{8,80},{12,68},{16,88},{20,76},{24,96},{28,84},{32,... | collective-permute-start | bytes 786440 | tf_op jit(solution)/shard_map/ppermute | solution.py:270
  107.0 22.6 %collective-permute-start.10 = (bf16[2,64,1024]{2,1,0:T(8,128)(2,1)}, bf16[2,64,1024]{2,1,0:T(8,128)(2,1)}, u32[]{:S(2)}, u32[]{:S(2)}) collective-permute-start(bf16[2,64,1024]{2,1,0:T(8,128)(2,1)} %get-tuple-element.63), channel_id=1, source_target_pairs={{0,124},{4,72},{8,68},{12,80},{16,76},{20,88},{24,84},{28,96},{32,... | collective-permute-start | bytes 786440 | tf_op jit(solution)/shard_map/ppermute | solution.py:270
  112.4 21.6 %collective-permute-start.11 = (bf16[2,64,1024]{2,1,0:T(8,128)(2,1)}, bf16[2,64,1024]{2,1,0:T(8,128)(2,1)}, u32[]{:S(2)}, u32[]{:S(2)}) collective-permute-start(bf16[2,64,1024]{2,1,0:T(8,128)(2,1)} %get-tuple-element.64), channel_id=1, source_target_pairs={{0,136},{4,188},{8,144},{12,132},{16,152},{20,140},{24,160},{28,14... | collective-permute-start | bytes 786440 | tf_op jit(solution)/shard_map/ppermute | solution.py:270
  115.5 18.4 %collective-permute-start.12 = (bf16[2,64,1024]{2,1,0:T(8,128)(2,1)}, bf16[2,64,1024]{2,1,0:T(8,128)(2,1)}, u32[]{:S(2)}, u32[]{:S(2)}) collective-permute-start(bf16[2,64,1024]{2,1,0:T(8,128)(2,1)} %get-tuple-element.65), channel_id=1, source_target_pairs={{0,188},{4,136},{8,132},{12,144},{16,140},{20,152},{24,148},{28,16... | collective-permute-start | bytes 786440 | tf_op jit(solution)/shard_map/ppermute | solution.py:270
  118.7 18.7 %collective-permute-start.13 = (bf16[2,64,1024]{2,1,0:T(8,128)(2,1)}, bf16[2,64,1024]{2,1,0:T(8,128)(2,1)}, u32[]{:S(2)}, u32[]{:S(2)}) collective-permute-start(bf16[2,64,1024]{2,1,0:T(8,128)(2,1)} %get-tuple-element.66), channel_id=1, source_target_pairs={{0,200},{4,252},{8,208},{12,196},{16,216},{20,204},{24,224},{28,21... | collective-permute-start | bytes 786440 | tf_op jit(solution)/shard_map/ppermute | solution.py:270
  119.6 21.6 %collective-permute-start.14 = (bf16[2,64,1024]{2,1,0:T(8,128)(2,1)}, bf16[2,64,1024]{2,1,0:T(8,128)(2,1)}, u32[]{:S(2)}, u32[]{:S(2)}) collective-permute-start(bf16[2,64,1024]{2,1,0:T(8,128)(2,1)} %get-tuple-element.67), channel_id=1, source_target_pairs={{0,252},{4,200},{8,196},{12,208},{16,204},{20,216},{24,212},{28,22... | collective-permute-start | bytes 786440 | tf_op jit(solution)/shard_map/ppermute | solution.py:270
  129.5 17.2 %collective-permute-start.15 = (bf16[2,64,1024]{2,1,0:T(8,128)(2,1)}, bf16[2,64,1024]{2,1,0:T(8,128)(2,1)}, u32[]{:S(2)}, u32[]{:S(2)}) collective-permute-start(bf16[2,64,1024]{2,1,0:T(8,128)(2,1)} %get-tuple-element.68), channel_id=1, source_target_pairs={{0,56},{4,12},{8,0},{12,20},{16,8},{20,28},{24,16},{28,36},{32,24}... | collective-permute-start | bytes 786440 | tf_op jit(solution)/shard_map/ppermute | solution.py:270
  133.9 14.1 %collective-permute-start.16 = (bf16[2,64,1024]{2,1,0:T(8,128)(2,1)}, bf16[2,64,1024]{2,1,0:T(8,128)(2,1)}, u32[]{:S(2)}, u32[]{:S(2)}) collective-permute-start(bf16[2,64,1024]{2,1,0:T(8,128)(2,1)} %get-tuple-element.69), channel_id=1, source_target_pairs={{0,12},{4,56},{8,20},{12,0},{16,28},{20,8},{24,36},{28,16},{32,44}... | collective-permute-start | bytes 786440 | tf_op jit(solution)/shard_map/ppermute | solution.py:270
  134.0 27.7 %collective-permute-start.17 = (bf16[2,64,1024]{2,1,0:T(8,128)(2,1)}, bf16[2,64,1024]{2,1,0:T(8,128)(2,1)}, u32[]{:S(2)}, u32[]{:S(2)}) collective-permute-start(bf16[2,64,1024]{2,1,0:T(8,128)(2,1)} %get-tuple-element.70), channel_id=1, source_target_pairs={{0,120},{4,76},{8,64},{12,84},{16,72},{20,92},{24,80},{28,100},{32... | collective-permute-start | bytes 786440 | tf_op jit(solution)/shard_map/ppermute | solution.py:270
  137.5 25.3 %collective-permute-start.18 = (bf16[2,64,1024]{2,1,0:T(8,128)(2,1)}, bf16[2,64,1024]{2,1,0:T(8,128)(2,1)}, u32[]{:S(2)}, u32[]{:S(2)}) collective-permute-start(bf16[2,64,1024]{2,1,0:T(8,128)(2,1)} %get-tuple-element.71), channel_id=1, source_target_pairs={{0,76},{4,120},{8,84},{12,64},{16,92},{20,72},{24,100},{28,80},{32... | collective-permute-start | bytes 786440 | tf_op jit(solution)/shard_map/ppermute | solution.py:270
  141.2 21.6 %collective-permute-start.19 = (bf16[2,64,1024]{2,1,0:T(8,128)(2,1)}, bf16[2,64,1024]{2,1,0:T(8,128)(2,1)}, u32[]{:S(2)}, u32[]{:S(2)}) collective-permute-start(bf16[2,64,1024]{2,1,0:T(8,128)(2,1)} %get-tuple-element.72), channel_id=1, source_target_pairs={{0,184},{4,140},{8,128},{12,148},{16,136},{20,156},{24,144},{28,16... | collective-permute-start | bytes 786440 | tf_op jit(solution)/shard_map/ppermute | solution.py:270
  146.7 16.1 %collective-permute-start.20 = (bf16[2,64,1024]{2,1,0:T(8,128)(2,1)}, bf16[2,64,1024]{2,1,0:T(8,128)(2,1)}, u32[]{:S(2)}, u32[]{:S(2)}) collective-permute-start(bf16[2,64,1024]{2,1,0:T(8,128)(2,1)} %get-tuple-element.73), channel_id=1, source_target_pairs={{0,140},{4,184},{8,148},{12,128},{16,156},{20,136},{24,164},{28,14... | collective-permute-start | bytes 786440 | tf_op jit(solution)/shard_map/ppermute | solution.py:270
  148.0 28.8 %collective-permute-start.21 = (bf16[2,64,1024]{2,1,0:T(8,128)(2,1)}, bf16[2,64,1024]{2,1,0:T(8,128)(2,1)}, u32[]{:S(2)}, u32[]{:S(2)}) collective-permute-start(bf16[2,64,1024]{2,1,0:T(8,128)(2,1)} %get-tuple-element.74), channel_id=1, source_target_pairs={{0,248},{4,204},{8,192},{12,212},{16,200},{20,220},{24,208},{28,22... | collective-permute-start | bytes 786440 | tf_op jit(solution)/shard_map/ppermute | solution.py:270
  161.7 15.2 %collective-permute-start.22 = (bf16[2,64,1024]{2,1,0:T(8,128)(2,1)}, bf16[2,64,1024]{2,1,0:T(8,128)(2,1)}, u32[]{:S(2)}, u32[]{:S(2)}) collective-permute-start(bf16[2,64,1024]{2,1,0:T(8,128)(2,1)} %get-tuple-element.75), channel_id=1, source_target_pairs={{0,204},{4,248},{8,212},{12,192},{16,220},{20,200},{24,228},{28,20... | collective-permute-start | bytes 786440 | tf_op jit(solution)/shard_map/ppermute | solution.py:270
  191.3 48.0 %all-to-all-start.1 = ((s16[4,2064,128]{2,1,0:T(8,128)(2,1)}), s16[4,2064,128]{2,1,0:T(8,128)(2,1)}, u32[]{:S(2)}, u32[]{:S(2)}) async-start(s16[4,2064,128]{2,1,0:T(8,128)(2,1)} %gram_tiles.3), calls=%async_computation.1 | async-start | bytes 4227072 | tf_op jit(solution)/shard_map/all_to_all | solution.py:283
  195.9 19.9 %collective-permute-start.30 = (bf16[1,64,1024]{2,1,0:T(8,128)(2,1)S(1)}, bf16[1,64,1024]{2,1,0:T(8,128)(2,1)S(1)}, u32[]{:S(2)}, u32[]{:S(2)}) collective-permute-start(bf16[1,64,1024]{2,1,0:T(8,128)(2,1)S(1)} %copy-done.11), channel_id=1, source_target_pairs={{0,208},{4,244},{8,216},{12,252},{16,224},{20,196},{24,232},{28,20... | collective-permute-start | bytes 393224 | tf_op jit(solution)/shard_map/ppermute | solution.py:270
  204.0 21.0 %collective-permute-start.31 = (bf16[1,64,1024]{2,1,0:T(8,128)(2,1)S(1)}, bf16[1,64,1024]{2,1,0:T(8,128)(2,1)S(1)}, u32[]{:S(2)}, u32[]{:S(2)}) collective-permute-start(bf16[1,64,1024]{2,1,0:T(8,128)(2,1)S(1)} %copy-done.10), channel_id=1, source_target_pairs={{0,244},{4,208},{8,252},{12,216},{16,196},{20,224},{24,204},{28,23... | collective-permute-start | bytes 393224 | tf_op jit(solution)/shard_map/ppermute | solution.py:270
  239.3 30.6 %all-to-all-start = ((s16[4,2064,128]{2,1,0:T(8,128)(2,1)}), s16[4,2064,128]{2,1,0:T(8,128)(2,1)}, u32[]{:S(2)}, u32[]{:S(2)}) async-start(s16[4,2064,128]{2,1,0:T(8,128)(2,1)} %gram_tiles.2), calls=%async_computation | async-start | bytes 4227072 | tf_op jit(solution)/shard_map/all_to_all | solution.py:283
  248.0 22.0 %collective-permute-start.40 = (s16[1,2064,128]{2,1,0:T(8,128)(2,1)}, s16[1,2064,128]{2,1,0:T(8,128)(2,1)S(1)}, u32[]{:S(2)}, u32[]{:S(2)}) collective-permute-start(s16[1,2064,128]{2,1,0:T(8,128)(2,1)} %sum_tiles.2), channel_id=1, source_target_pairs={{0,40},{4,28},{8,48},{12,36},{16,56},{20,44},{24,0},{28,52},{32,8}... | collective-permute-start | bytes 1585160 | tf_op jit(solution)/shard_map/ppermute | solution.py:270
  (23 other events, 505.4 us)

commit v3 on v2

v3 whole, which is shorter than its diff:
```python
import jax
import jax.numpy as jnp
import numpy as np
from jax import lax
from jax.experimental import pallas as pl
from jax.experimental.pallas import tpu as pltpu
from jax.sharding import PartitionSpec as P

BLOCK = 128
OWN_BLOCKS = 8
WIDTH = OWN_BLOCKS * BLOCK
FAR = 3
FAR_STEPS = (-2, -1, 1, 0)
CODES = 32000.0
VMEM = 62 << 20
HBM = pl.BlockSpec(memory_space=pltpu.HBM)


def scale_columns(owners, order, jacobian, weight, shapes):
    sizes = [int(np.prod(shape)) for shape in shapes]
    units = sum(sizes)
    firsts = np.cumsum([0, *sizes])
    rows, zones = jacobian.shape
    cuts, batch = 8, 4

    def kernel(owners_ref, order_ref, jac_ref, weight_ref, *refs):
        out_refs, (held, made, in_sems, out_sems) = refs[:-4], refs[-4:]
        cut = rows // cuts

        def load(q):
            span = pl.ds(q * cut, cut)
            return pltpu.make_async_copy(jac_ref.at[span], held.at[span], in_sems.at[q])

        def store(q):
            unit = made.at[pl.ds(int(firsts[q]), sizes[q])]
            return pltpu.make_async_copy(unit, out_refs[q], out_sems.at[q])

        for q in range(cuts):
            load(q).start()
        for q in range(cuts):
            load(q).wait()
        root = jnp.sqrt(weight_ref[...])

        def unit(u, carry):
            base = owners_ref[u] * OWN_BLOCKS
            for b in range(OWN_BLOCKS):
                start = pl.multiple_of(order_ref[base + b] * BLOCK, BLOCK)
                piece = held[:, pl.ds(start, BLOCK)].astype(jnp.float32) * root
                made[u, :, b * BLOCK : (b + 1) * BLOCK] = piece.astype(jnp.bfloat16)
            return carry

        for q in range(len(sizes)):
            lax.fori_loop(int(firsts[q]), int(firsts[q + 1]), unit, 0)
            store(q).start()
        for q in range(len(sizes)):
            store(q).wait()

    flat = pl.pallas_call(
        kernel,
        out_shape=[jax.ShapeDtypeStruct((size, rows, WIDTH), jnp.bfloat16) for size in sizes],
        grid_spec=pltpu.PrefetchScalarGridSpec(
            num_scalar_prefetch=2,
            grid=(),
            in_specs=[HBM, pl.BlockSpec(memory_space=pltpu.VMEM)],
            out_specs=[HBM] * len(sizes),
            scratch_shapes=[
                pltpu.VMEM((rows, zones), jnp.bfloat16),
                pltpu.VMEM((units, rows, WIDTH), jnp.bfloat16),
                pltpu.SemaphoreType.DMA((cuts,)),
                pltpu.SemaphoreType.DMA((len(sizes),)),
            ],
        ),
        compiler_params=pltpu.CompilerParams(vmem_limit_bytes=VMEM),
        cost_estimate=pl.CostEstimate(
            flops=units * rows * WIDTH, bytes_accessed=2 * (rows * zones + units * rows * WIDTH), transcendentals=0
        ),
        name="scale_columns",
    )(owners, order, jacobian, weight)
    return [part.reshape(*shape, rows, WIDTH) for part, shape in zip(flat, shapes)]


def copy_parts(arrays, shapes, copies, name):
    def kernel(*refs):
        in_refs, out_refs, sems = refs[: len(arrays)], refs[len(arrays) : -1], refs[-1]
        moves = [
            pltpu.make_async_copy(in_refs[a].at[i], out_refs[r].at[k], sems.at[q])
            for q, (a, i, r, k) in enumerate(copies)
        ]
        for move in moves:
            move.start()
        for move in moves:
            move.wait()

    size = 2 * sum(int(np.prod(shape)) for shape in shapes)
    return pl.pallas_call(
        kernel,
        out_shape=[jax.ShapeDtypeStruct(shape, arrays[0].dtype) for shape in shapes],
        in_specs=[HBM] * len(arrays),
        out_specs=[HBM] * len(shapes),
        scratch_shapes=[pltpu.SemaphoreType.DMA((len(copies),))],
        compiler_params=pltpu.CompilerParams(vmem_limit_bytes=VMEM),
        cost_estimate=pl.CostEstimate(flops=0, bytes_accessed=2 * size, transcendentals=0),
        name=name,
    )(*arrays)


def power_of(top):
    return jnp.floor(jnp.log2(jnp.maximum(top, 1e-30))) + 1.0


def code_tile(tile, power):
    return jnp.round(tile * (jnp.exp2(-power) * CODES)).astype(jnp.int32).astype(jnp.int16)


def top_of(tile):
    return jnp.max(jnp.abs(tile), axis=0, keepdims=True)


def gram_tiles(arrays, pieces, pairs, count):
    rows = arrays[0].shape[-2]
    deep = 8 * rows
    total = len(pieces) * deep
    slots = pairs.shape[0] // 2
    quarter = slots // 4
    strip = 256

    def kernel(pairs_ref, count_ref, *refs):
        array_refs, (out_ref, held, gram, made, powers, sems, out_sems) = refs[:-7], refs[-7:]

        def load(p):
            a, i = pieces[p]
            return pltpu.make_async_copy(array_refs[a].at[i], held.at[pl.ds(p * 8, 8)], sems.at[p])

        def store(t):
            return pltpu.make_async_copy(made.at[t], out_ref.at[t], out_sems.at[t])

        for p in range(len(pieces)):
            load(p).start()
        for p in range(len(pieces)):
            load(p).wait()
            units = pl.ds(p * 8, 8)

            def multiply(m, carry, p=p, units=units):
                lanes = pl.ds(pl.multiple_of(m * strip, strip), strip)
                part = lax.dot_general(
                    held[units, :, lanes].reshape(deep, strip), held[units].reshape(deep, WIDTH),
                    (((0,), (0,)), ((), ())), preferred_element_type=jnp.float32,
                )
                if p == 0:
                    gram[lanes, :] = part
                else:
                    gram[lanes, :] += part
                return carry

            lax.fori_loop(0, WIDTH // strip, multiply, 0)

        for t in range(4):

            def tile_of(k, t=t):
                slot = t * quarter + k
                row = pl.multiple_of(pairs_ref[2 * slot] * BLOCK, BLOCK)
                col = pl.multiple_of(pairs_ref[2 * slot + 1] * BLOCK, BLOCK)
                return jnp.where(slot < count_ref[0], gram[pl.ds(row, BLOCK), pl.ds(col, BLOCK)], 0.0)

            def measure(k, carry, tile_of=tile_of):
                powers[pl.ds(k, 1), :] = top_of(tile_of(k))
                return carry

            def code(k, carry, t=t, tile_of=tile_of):
                span = pl.ds(pl.multiple_of(k * BLOCK, BLOCK), BLOCK)
                made[t, span, :] = code_tile(tile_of(k), powers[pl.ds(k, 1), :])
                return carry

            lax.fori_loop(0, quarter, measure, 0, unroll=4)
            powers[...] = power_of(powers[...])
            lax.fori_loop(0, quarter, code, 0, unroll=2)
            made[t, quarter * BLOCK :, :] = powers[...].astype(jnp.int32).astype(jnp.int16)
            store(t).start()
        for t in range(4):
            store(t).wait()

    return pl.pallas_call(
        kernel,
        out_shape=jax.ShapeDtypeStruct((4, quarter * BLOCK + quarter, BLOCK), jnp.int16),
        grid_spec=pltpu.PrefetchScalarGridSpec(
            num_scalar_prefetch=2,
            grid=(),
            in_specs=[HBM] * len(arrays),
            out_specs=HBM,
            scratch_shapes=[
                pltpu.VMEM((len(pieces) * 8, rows, WIDTH), jnp.bfloat16),
                pltpu.VMEM((WIDTH, WIDTH), jnp.float32),
                pltpu.VMEM((4, quarter * BLOCK + quarter, BLOCK), jnp.int16),
                pltpu.VMEM((quarter, BLOCK), jnp.float32),
                pltpu.SemaphoreType.DMA((len(pieces),)),
                pltpu.SemaphoreType.DMA((4,)),
            ],
        ),
        compiler_params=pltpu.CompilerParams(vmem_limit_bytes=VMEM),
        cost_estimate=pl.CostEstimate(
            flops=2 * total * WIDTH * WIDTH, bytes_accessed=2 * total * WIDTH + 2 * slots * BLOCK * BLOCK,
            transcendentals=0,
        ),
        name="gram_tiles",
    )(pairs, count, *arrays)


def sum_tiles(parts, coded):
    rows = parts[0].shape[1]
    tiles = rows // (BLOCK + 1)
    sources = [(a, q) for a, part in enumerate(parts) for q in range(part.shape[0])]
    last = len(sources) * tiles

    def kernel(*refs):
        part_refs, out_ref, powers, sums = refs[: len(parts)], refs[len(parts)], refs[-2], refs[-1]
        for at, (a, q) in enumerate(sources):
            power = part_refs[a][q, tiles * BLOCK :, :].astype(jnp.int32).astype(jnp.float32)
            powers[at * tiles : (at + 1) * tiles, :] = jnp.exp2(power) * (1.0 / CODES)

        def span_of(k):
            return pl.ds(pl.multiple_of(k * BLOCK, BLOCK), BLOCK)

        def one(k, carry):
            total = None
            for at, (a, q) in enumerate(sources):
                values = part_refs[a][q, span_of(k), :].astype(jnp.int32).astype(jnp.float32)
                term = values * powers[pl.ds(at * tiles + k, 1), :]
                total = term if total is None else total + term
            if coded:
                sums[span_of(k), :] = total
                powers[pl.ds(last + k, 1), :] = top_of(total)
            else:
                out_ref[k] = total
            return carry

        lax.fori_loop(0, tiles, one, 0, unroll=2)
        if coded:
            own = power_of(powers[last:, :])
            powers[last:, :] = own

            def code(k, carry):
                out_ref[0, span_of(k), :] = code_tile(sums[span_of(k), :], powers[pl.ds(last + k, 1), :])
                return carry

            lax.fori_loop(0, tiles, code, 0, unroll=2)
            out_ref[0, tiles * BLOCK :, :] = own.astype(jnp.int32).astype(jnp.int16)

    if coded:
        out = jax.ShapeDtypeStruct((1, rows, BLOCK), jnp.int16)
    else:
        out = jax.ShapeDtypeStruct((tiles, BLOCK, BLOCK), jnp.float32)
    vmem = pl.BlockSpec(memory_space=pltpu.VMEM)
    return pl.pallas_call(
        kernel,
        out_shape=out,
        in_specs=[vmem] * len(parts),
        out_specs=vmem,
        scratch_shapes=[
            pltpu.VMEM((last + tiles, BLOCK), jnp.float32),
            pltpu.VMEM((tiles * BLOCK if coded else 8, BLOCK), jnp.float32),
        ],
        compiler_params=pltpu.CompilerParams(vmem_limit_bytes=VMEM),
        cost_estimate=pl.CostEstimate(
            flops=4 * len(sources) * rows * BLOCK, bytes_accessed=2 * (len(sources) + 2) * rows * BLOCK,
            transcendentals=0,
        ),
        name="sum_tiles",
    )(*parts)


def body(jacobian, obs_weight, block_order, tile_pairs, tile_count):
    rows = jacobian.shape[0]
    planes, lines, cores = lax.axis_size("z"), lax.axis_size("x"), lax.axis_size("c")
    z = lax.axis_index("z")
    weight = jnp.broadcast_to(obs_weight[:, None], (rows, BLOCK))
    group = lines * cores

    dests = [(k % lines, k // lines) for k in range(group)]
    units = [(a, c, (s - FAR) * (1 - 2 * c)) for a, c in dests for s in FAR_STEPS]
    for s in (1, -1):
        units += [(a, c, s) for a, c in dests]
    for s in (2, -2):
        units += [(a, c, s) for a, c in dests if (1 - 2 * c) * s > 0]
    units += [(a, c, 0) for a, c in dests]
    shapes = [(group, len(FAR_STEPS)), (group,), (group,), (lines,), (lines,), (group,)]
    table = np.array(units, np.int32)
    owners = table[:, 0] * (planes * cores) + table[:, 1] + (z + table[:, 2] + planes) % planes * cores

    def up(value, step):
        return lax.ppermute(value, "z", [(b, (b + step) % planes) for b in range(planes)])

    def away(value, step):
        moves = [(b * cores + c, (b + step * (1 - 2 * c)) % planes * cores + c) for b in range(planes) for c in range(cores)]
        return lax.ppermute(value, ("z", "c"), moves)

    def spread(value, axes):
        return lax.all_to_all(value, axes, split_axis=0, concat_axis=0, tiled=True)

    wanted = jnp.concatenate([tile_pairs.reshape(-1), tile_count])
    far_wanted = away(wanted, FAR)

    far, up1, down1, up2, down2, stay = scale_columns(owners.astype(jnp.int32), block_order, jacobian, weight, shapes)
    near_parts = [up(up1, 1), up(down1, -1), up(up2, 2), up(down2, -2), stay]
    far = spread(far, ("c", "x"))
    whole = pl.ds(0, group)
    half = [pl.ds(0, lines), pl.ds(lines, lines)]
    unit = (rows, WIDTH)
    (near,) = copy_parts(
        near_parts,
        [(group, 4, *unit)],
        [(0, whole, 0, (whole, 0)), (1, whole, 0, (whole, 1)), (2, half[0], 0, (half[0], 2)),
         (3, half[0], 0, (half[1], 2)), (4, whole, 0, (whole, 3))],
        "join_near",
    )
    near = spread(near, ("c", "x")).reshape(group * 4, *unit)
    sent = [k for k, s in enumerate(FAR_STEPS) if s]
    far_parts = copy_parts(
        [far], [(group, *unit)] * len(sent), [(0, (whole, k), q, whole) for q, k in enumerate(sent)], "part_far"
    )
    far_parts = [away(part, FAR_STEPS[k]) for part, k in zip(far_parts, sent)]
    far_pieces = [(q, whole) for q in range(len(sent))] + [(len(sent), (whole, FAR_STEPS.index(0)))]
    near_pieces = [(0, pl.ds(8 * q, 8)) for q in range(4)]

    far_tiles = gram_tiles([*far_parts, far], far_pieces, far_wanted[:-1], far_wanted[-1:])
    far_sum = sum_tiles([spread(far_tiles, "y")], True)
    near_tiles = gram_tiles([near], near_pieces, wanted[:-1], wanted[-1:])
    return sum_tiles([spread(near_tiles, "y"), away(far_sum, -FAR)], False)


def solution(mesh):
    shape = (4, mesh.shape["obs"] // 8, 2, mesh.shape["tile"])
    chips = jax.sharding.Mesh(mesh.devices.reshape(shape), ("x", "z", "c", "y"))
    everywhere = ("x", "z", "c", "y")
    owner = ("x", "z", "c")
    return jax.shard_map(
        body,
        mesh=chips,
        in_specs=(P(everywhere, None), P(everywhere), P(), P(owner, None, None), P(owner)),
        out_specs=P(everywhere, None, None),
        check_vma=False,
    )
```

time: 275 us -> 432 us (1.57)
  Pallas kernels: 47.1 us -> 266 us
  starting transfers between devices: 143 us -> 41.4 us
  waiting for transfers between devices: 77.4 us -> 115 us
    pallas_call x0 -> x2, Pallas kernels: none -> 225 us  [copy_parts(): pl.pallas_call(kernel, out_shape=[jax.ShapeDtypeStruct(shape, arrays[0].d...]
    ppermute x41 -> x9, starting transfers between devices: 133 us -> 20.7 us  [the longest x5 12.4 us: away(): return lax.ppermute(value, ('z', 'c'), moves)]
    ppermute x41 -> x9, waiting for transfers between devices: 57.8 us -> 81.7 us  [the longest x4 41.2 us: up(): lax.ppermute(value, 'z', [(b, (b + step) % planes) for b in range(planes)])]
    all_to_all x2 -> x4, waiting for transfers between devices: 19.5 us -> 33.2 us  [spread(): return lax.all_to_all(value, axes, split_axis=0, concat_axis=0, tiled=True)]
    all_to_all x2 -> x4, starting transfers between devices: 9.65 us -> 20.7 us  [spread(): return lax.all_to_all(value, axes, split_axis=0, concat_axis=0, tiled=True)]
  transfers between devices with their start and end apart: 43 -> 13, of which waited for: 13 -> 7; matrix products, arithmetic and copies ran while one was open for 0% -> 0% of each run, Pallas kernels for 6% -> 59%
where the time goes in v3:
time: 432 us; the launch traced here: 430 us
  Pallas kernels  266 us (62%)
  waiting for transfers between devices  115 us (27%)
  starting transfers between devices  41.4 us (10%)
  local copies, waits for them, and re-layouts  5.23 us (1%)
    pallas_call x2, Pallas kernels, copy_parts(): pl.pallas_call(kernel, out_shape=[jax.ShapeDtypeStruct(shape, arrays[0].d...  225 us
    ppermute x4, waiting for transfers between devices, up(): lax.ppermute(value, 'z', [(b, (b + step) % planes) for b in range(planes)])  41.2 us
    ppermute x5, waiting for transfers between devices, away(): return lax.ppermute(value, ('z', 'c'), moves)  40.5 us
    all_to_all x4, waiting for transfers between devices, spread(): return lax.all_to_all(value, axes, split_axis=0, concat_axis=0, tiled=True)  33.2 us
    pallas_call x2, Pallas kernels, gram_tiles(): pl.pallas_call(kernel, out_shape=jax.ShapeDtypeStruct((4, quarter * BLOCK...  25.2 us
    all_to_all x4, starting transfers between devices, spread(): return lax.all_to_all(value, axes, split_axis=0, concat_axis=0, tiled=True)  20.7 us
    ppermute x5, starting transfers between devices, away(): return lax.ppermute(value, ('z', 'c'), moves)  12.4 us
    pallas_call x1, Pallas kernels, scale_columns(): pl.pallas_call(kernel, out_shape=[jax.ShapeDtypeStruct((size, rows, WIDTH...  9.82 us
  transfers between devices with their start and end apart: 13, of which 7 were waited for; matrix products, arithmetic and copies ran while one was open for 0% of the time, Pallas kernels for 59%

profile of v3, /device:TPU:2, one launch (start us, length us, event | category | flops | bytes accessed | tf_op | source)
XLA Modules:
  0.0 429.7 jit_solution(12401913488558138028)
XLA Ops:
  0.0 1.3 fusion.1.owners_ref
  1.3 1.3 broadcast_in_dim.2.weight_ref
  2.6 9.8 %scale_columns.1 = (bf16[32,64,1024]{2,1,0:T(8,128)(2,1)}, bf16[8,64,1024]{2,1,0:T(8,128)(2,1)}, bf16[8,64,1024]{2,1,0:T(8,128)(2,1)}, bf16[4,64,1024]{2,1,0:T(8...) custom-call(s32[64]{0:T(128)} %fusion.1.owners_ref, s32[512]{0:T(512)} %order_ref.1, ...), custom_call_target="tpu_custom_call" | custom-call | flops 4194304 | bytes 16777216 | tf_op jit(solution)/shard_map/scale_columns/pallas_call | solution.py:58
  12.4 0.0 copy-start.7
  12.4 6.8 %all-to-all-start.2 = ((bf16[8,4,64,1024]{3,2,1,0:T(8,128)(2,1)}), bf16[8,4,64,1024]{3,2,1,0:T(8,128)(2,1)}, u32[]{:S(2)}, u32[]{:S(2)}) async-start(bf16[8,4,64,1024]{3,2,1,0:T(8,128)(2,1)} %bitcast.2), calls=%async_computation.2 | async-start | bytes 8388608 | tf_op jit(solution)/shard_map/all_to_all | solution.py:297
  19.3 0.2 collective-permute-start
  19.5 0.0 copy-done.7
  19.5 4.0 collective-permute-start.1
  23.5 0.0 collective-permute-start.2
  23.5 4.1 collective-permute-start.3
  27.6 32.8 %collective-permute-done.2.refs_2_ = bf16[4,64,1024]{2,1,0:T(8,128)(2,1)S(1)} collective-permute-done((bf16[4,64,1024]{2,1,0:T(8,128)(2,1)}, bf16[4,64,1024]{2,1,0:T(8,128)(2,1)S(1)}, u32[]{:S(2)}, u32[]{:S(2)}) %collective-permute-start.2) | collective-permute-done | bytes 524320 | tf_op jit(solution)/shard_map/ppermute | solution.py:290
  60.4 8.4 %collective-permute-done.3.refs_3_ = bf16[4,64,1024]{2,1,0:T(8,128)(2,1)S(1)} collective-permute-done((bf16[4,64,1024]{2,1,0:T(8,128)(2,1)}, bf16[4,64,1024]{2,1,0:T(8,128)(2,1)S(1)}, u32[]{:S(2)}, u32[]{:S(2)}) %collective-permute-start.3) | collective-permute-done | bytes 524320 | tf_op jit(solution)/shard_map/ppermute | solution.py:290
  68.8 0.0 collective-permute-done.refs_0_
  68.8 0.8 copy-done.3
  69.6 0.0 collective-permute-done.1.refs_1_
  69.6 0.0 copy-done.2
  69.6 1.0 copy-done
  70.6 128.2 %join_near.1 = bf16[8,4,64,1024]{3,2,1,0:T(8,128)(2,1)} custom-call(bf16[8,64,1024]{2,1,0:T(8,128)(2,1)} %copy-done, bf16[8,64,1024]{2,1,0:T(8,128)(2,1)} %collective-permute-done.1.refs_1_, bf16[4,64,1024]{2,1,0:T(8,128)(2,1)} %copy-done.2, bf16[4,64,1024]{2,1,0:T(8,128)(2,1)} %copy-done.3, bf16[8,64,1024]{2,1,0:T(8,128)(2,1)} %get-tuple-element.18.refs_4_), custom_call_target="tpu_custom_call" | custom-call | bytes 8388608 | tf_op jit(solution)/shard_map/join_near/pallas_call | solution.py:95
  198.8 0.0 all-to-all-done.2.refs_0_.refs_3_
  198.8 4.9 %all-to-all-start = ((bf16[8,4,64,1024]{3,2,1,0:T(8,128)(2,1)}), bf16[8,4,64,1024]{3,2,1,0:T(8,128)(2,1)}, u32[]{:S(2)}, u32[]{:S(2)}) async-start(bf16[8,4,64,1024]{3,2,1,0:T(8,128)(2,1)} %join_near.1), calls=%async_computation | async-start | bytes 8388608 | tf_op jit(solution)/shard_map/all_to_all | solution.py:297
  203.7 96.4 %part_far.1 = (bf16[8,64,1024]{2,1,0:T(8,128)(2,1)}, bf16[8,64,1024]{2,1,0:T(8,128)(2,1)}, bf16[8,64,1024]{2,1,0:T(8,128)(2,1)}) custom-call(bf16[8,4,64,1024]{3,2,1,0:T(8,128)(2,1)} %all-to-all-done.2.refs_0_.refs_3_), custom_call_target="tpu_custom_call" | custom-call | bytes 6291456 | tf_op jit(solution)/shard_map/part_far/pallas_call | solution.py:95
  300.1 4.6 %collective-permute-start.5 = (bf16[8,64,1024]{2,1,0:T(8,128)(2,1)}, bf16[8,64,1024]{2,1,0:T(8,128)(2,1)S(1)}, u32[]{:S(2)}, u32[]{:S(2)}) collective-permute-start(bf16[8,64,1024]{2,1,0:T(8,128)(2,1)} %get-tuple-element.20), channel_id=1, source_target_pairs={{0,48},{4,20},{8,56},{12,28},{16,0},{20,36},{24,8},{28,44},{32,16}... | collective-permute-start | bytes 3145736 | tf_op jit(solution)/shard_map/ppermute | solution.py:294
  304.6 1.2 collective-permute-start.6
  305.8 0.8 collective-permute-start.7
  306.7 0.0 copy-done.5
  306.7 0.1 copy.9
  306.8 0.1 reshape.10.pairs_ref
  306.9 0.0 copy-start.4
  307.6 2.8 collective-permute-start.4
  310.4 32.7 %collective-permute-done.4 = s32[129]{0:T(256)S(1)} collective-permute-done((s32[129]{0:T(256)S(1)}, s32[129]{0:T(256)S(1)}, u32[]{:S(2)}, u32[]{:S(2)}) %collective-permute-start.4) | collective-permute-done | bytes 548 | tf_op jit(solution)/shard_map/ppermute | solution.py:294
  343.1 0.5 slice.6.pairs_ref
  343.6 0.5 slice.7.count_ref
  344.1 0.0 collective-permute-done.5.refs_0_
  344.1 7.3 %collective-permute-done.6.refs_1_ = bf16[8,64,1024]{2,1,0:T(8,128)(2,1)} collective-permute-done((bf16[8,64,1024]{2,1,0:T(8,128)(2,1)}, bf16[8,64,1024]{2,1,0:T(8,128)(2,1)}, u32[]{:S(2)}, u32[]{:S(2)}) %collective-permute-start.6) | collective-permute-done | bytes 1048608 | tf_op jit(solution)/shard_map/ppermute | solution.py:294
  351.5 0.0 collective-permute-done.7.refs_2_
  351.5 0.0 copy-done.6
  351.5 12.9 %gram_tiles.3 = s16[4,2064,128]{2,1,0:T(8,128)(2,1)} custom-call(s32[128]{0:T(128)} %slice.6.pairs_ref, s32[1]{0:T(128)} %slice.7.count_ref, bf16[8,64,1024]{2,1,0:T(8,128)(2,1)} %copy-done.6, bf16[8,64,1024]{2,1,0:T(8,128)(2,1)} %collective-permute-done.6.refs_1_, bf16[8,64,1024]{2,1,0:T(8,128)(2,1)} %collective-permute-done.7.refs_2_, ...), custom_call_target="tpu_custom_call" | custom-call | flops 4294967296 | bytes 6291456 | tf_op jit(solution)/shard_map/gram_tiles/pallas_call | solution.py:182
  364.4 0.0 all-to-all-done
  364.4 4.5 %all-to-all-start.3 = ((s16[4,2064,128]{2,1,0:T(8,128)(2,1)}), s16[4,2064,128]{2,1,0:T(8,128)(2,1)}, u32[]{:S(2)}, u32[]{:S(2)}) async-start(s16[4,2064,128]{2,1,0:T(8,128)(2,1)} %gram_tiles.3), calls=%async_computation.3 | async-start | bytes 4227072 | tf_op jit(solution)/shard_map/all_to_all | solution.py:297
  368.9 12.3 %gram_tiles.2 = s16[4,2064,128]{2,1,0:T(8,128)(2,1)} custom-call(s32[128]{0:T(128)} %copy-done.4, s32[1]{0:T(128)S(6)} %copy.10.count_ref, bf16[32,64,1024]{2,1,0:T(8,128)(2,1)} %bitcast.refs_0_), custom_call_target="tpu_custom_call" | custom-call | flops 4294967296 | bytes 6291456 | tf_op jit(solution)/shard_map/gram_tiles/pallas_call | solution.py:182
  381.2 14.0 %all-to-all-done.3.refs_0_ = s16[4,2064,128]{2,1,0:T(8,128)(2,1)} async-done(((s16[4,2064,128]{2,1,0:T(8,128)(2,1)}), s16[4,2064,128]{2,1,0:T(8,128)(2,1)}, u32[]{:S(2)}, u32[]{:S(2)}) %all-to-all-start.3) | async-done | bytes 2113568 | tf_op jit(solution)/shard_map/all_to_all | solution.py:297
  395.2 4.5 %all-to-all-start.1 = ((s16[4,2064,128]{2,1,0:T(8,128)(2,1)}), s16[4,2064,128]{2,1,0:T(8,128)(2,1)}, u32[]{:S(2)}, u32[]{:S(2)}) async-start(s16[4,2064,128]{2,1,0:T(8,128)(2,1)} %gram_tiles.2), calls=%async_computation.1 | async-start | bytes 4227072 | tf_op jit(solution)/shard_map/all_to_all | solution.py:297
  399.7 3.3 sum_tiles.2
  402.9 3.0 collective-permute-start.8
  405.9 19.1 %all-to-all-done.1.refs_0_ = s16[4,2064,128]{2,1,0:T(8,128)(2,1)} async-done(((s16[4,2064,128]{2,1,0:T(8,128)(2,1)}), s16[4,2064,128]{2,1,0:T(8,128)(2,1)}, u32[]{:S(2)}, u32[]{:S(2)}) %all-to-all-start.1) | async-done | bytes 2113568 | tf_op jit(solution)/shard_map/all_to_all | solution.py:297
  425.1 0.5 collective-permute-done.8.refs_1_
  425.5 0.8 copy-done.1
  426.4 3.4 sum_tiles.3
  (8 shorter events, 0.0 us)
Async XLA Ops:
  12.4 7.0 %copy-start.7 = (bf16[8,64,1024]{2,1,0:T(8,128)(2,1)S(1)}, bf16[8,64,1024]{2,1,0:T(8,128)(2,1)}, u32[]{:S(2)}) copy-start(bf16[8,64,1024]{2,1,0:T(8,128)(2,1)} %get-tuple-element.15) | copy-start | bytes 3145732
  12.4 186.3 %all-to-all-start.2 = ((bf16[8,4,64,1024]{3,2,1,0:T(8,128)(2,1)}), bf16[8,4,64,1024]{3,2,1,0:T(8,128)(2,1)}, u32[]{:S(2)}, u32[]{:S(2)}) async-start(bf16[8,4,64,1024]{3,2,1,0:T(8,128)(2,1)} %bitcast.2), calls=%async_computation.2 | async-start | bytes 8388608 | tf_op jit(solution)/shard_map/all_to_all | solution.py:297
  19.3 49.5 %collective-permute-start = (bf16[8,64,1024]{2,1,0:T(8,128)(2,1)}, bf16[8,64,1024]{2,1,0:T(8,128)(2,1)S(1)}, u32[]{:S(2)}, u32[]{:S(2)}) collective-permute-start(bf16[8,64,1024]{2,1,0:T(8,128)(2,1)} %get-tuple-element.14), channel_id=1, source_target_pairs={{0,8},{8,16},{16,24},{24,32},{32,40},{40,48},{48,56},{56,0},{1,9},... | collective-permute-start | bytes 3145736 | tf_op jit(solution)/shard_map/ppermute | solution.py:290
  19.5 50.1 %collective-permute-start.1 = (bf16[8,64,1024]{2,1,0:T(8,128)(2,1)S(1)}, bf16[8,64,1024]{2,1,0:T(8,128)(2,1)}, u32[]{:S(2)}, u32[]{:S(2)}) collective-permute-start(bf16[8,64,1024]{2,1,0:T(8,128)(2,1)S(1)} %copy-done.7), channel_id=1, source_target_pairs={{0,56},{8,0},{16,8},{24,16},{32,24},{40,32},{48,40},{56,48},{1,57}... | collective-permute-start | bytes 3145736 | tf_op jit(solution)/shard_map/ppermute | solution.py:290
  23.5 37.0 %collective-permute-start.2 = (bf16[4,64,1024]{2,1,0:T(8,128)(2,1)}, bf16[4,64,1024]{2,1,0:T(8,128)(2,1)S(1)}, u32[]{:S(2)}, u32[]{:S(2)}) collective-permute-start(bf16[4,64,1024]{2,1,0:T(8,128)(2,1)} %get-tuple-element.16), channel_id=1, source_target_pairs={{0,16},{8,24},{16,32},{24,40},{32,48},{40,56},{48,0},{56,8},{1,17}... | collective-permute-start | bytes 1572872 | tf_op jit(solution)/shard_map/ppermute | solution.py:290
  23.5 45.3 %collective-permute-start.3 = (bf16[4,64,1024]{2,1,0:T(8,128)(2,1)}, bf16[4,64,1024]{2,1,0:T(8,128)(2,1)S(1)}, u32[]{:S(2)}, u32[]{:S(2)}) collective-permute-start(bf16[4,64,1024]{2,1,0:T(8,128)(2,1)} %get-tuple-element.17), channel_id=1, source_target_pairs={{0,48},{8,56},{16,0},{24,8},{32,16},{40,24},{48,32},{56,40},{1,49}... | collective-permute-start | bytes 1572872 | tf_op jit(solution)/shard_map/ppermute | solution.py:290
  60.4 9.2 %copy-start.2 = (bf16[4,64,1024]{2,1,0:T(8,128)(2,1)}, bf16[4,64,1024]{2,1,0:T(8,128)(2,1)S(1)}, u32[]{:S(2)}) copy-start(bf16[4,64,1024]{2,1,0:T(8,128)(2,1)S(1)} %collective-permute-done.2.refs_2_) | copy-start | bytes 1572868
  68.8 0.8 copy-start.3
  69.6 1.0 copy-start
  198.8 165.6 %all-to-all-start = ((bf16[8,4,64,1024]{3,2,1,0:T(8,128)(2,1)}), bf16[8,4,64,1024]{3,2,1,0:T(8,128)(2,1)}, u32[]{:S(2)}, u32[]{:S(2)}) async-start(bf16[8,4,64,1024]{3,2,1,0:T(8,128)(2,1)} %join_near.1), calls=%async_computation | async-start | bytes 8388608 | tf_op jit(solution)/shard_map/all_to_all | solution.py:297
  203.7 103.0 %copy-start.5 = (s32[1,64,2]{1,2,0:T(2,128)S(1)}, s32[1,64,2]{1,2,0:T(2,128)}, u32[]{:S(2)}) copy-start(s32[1,64,2]{1,2,0:T(2,128)} %param.10) | copy-start | bytes 1540
  300.1 44.1 %collective-permute-start.5 = (bf16[8,64,1024]{2,1,0:T(8,128)(2,1)}, bf16[8,64,1024]{2,1,0:T(8,128)(2,1)S(1)}, u32[]{:S(2)}, u32[]{:S(2)}) collective-permute-start(bf16[8,64,1024]{2,1,0:T(8,128)(2,1)} %get-tuple-element.20), channel_id=1, source_target_pairs={{0,48},{4,20},{8,56},{12,28},{16,0},{20,36},{24,8},{28,44},{32,16}... | collective-permute-start | bytes 3145736 | tf_op jit(solution)/shard_map/ppermute | solution.py:294
  304.6 46.8 %collective-permute-start.6 = (bf16[8,64,1024]{2,1,0:T(8,128)(2,1)}, bf16[8,64,1024]{2,1,0:T(8,128)(2,1)}, u32[]{:S(2)}, u32[]{:S(2)}) collective-permute-start(bf16[8,64,1024]{2,1,0:T(8,128)(2,1)} %get-tuple-element.21), channel_id=1, source_target_pairs={{0,56},{4,12},{8,0},{12,20},{16,8},{20,28},{24,16},{28,36},{32,24}... | collective-permute-start | bytes 3145736 | tf_op jit(solution)/shard_map/ppermute | solution.py:294
  305.8 45.6 %collective-permute-start.7 = (bf16[8,64,1024]{2,1,0:T(8,128)(2,1)}, bf16[8,64,1024]{2,1,0:T(8,128)(2,1)}, u32[]{:S(2)}, u32[]{:S(2)}) collective-permute-start(bf16[8,64,1024]{2,1,0:T(8,128)(2,1)} %get-tuple-element.22), channel_id=1, source_target_pairs={{0,8},{4,60},{8,16},{12,4},{16,24},{20,12},{24,32},{28,20},{32,40}... | collective-permute-start | bytes 3145736 | tf_op jit(solution)/shard_map/ppermute | solution.py:294
  306.9 57.5 %copy-start.4 = (s32[128]{0:T(128)}, s32[128]{0:T(128)S(1)}, u32[]{:S(2)}) copy-start(s32[128]{0:T(128)S(1)} %reshape.10.pairs_ref) | copy-start | bytes 1540
  307.6 35.5 %collective-permute-start.4 = (s32[129]{0:T(256)S(1)}, s32[129]{0:T(256)S(1)}, u32[]{:S(2)}, u32[]{:S(2)}) collective-permute-start(s32[129]{0:T(256)S(1)} %pad_add_fusion), channel_id=1, source_target_pairs={{0,24},{4,44},{8,32},{12,52},{16,40},{20,60},{24,48},{28,4},{32,56... | collective-permute-start | bytes 1556 | tf_op jit(solution)/shard_map/ppermute | solution.py:294
  344.1 7.3 %copy-start.6 = (bf16[8,64,1024]{2,1,0:T(8,128)(2,1)}, bf16[8,64,1024]{2,1,0:T(8,128)(2,1)S(1)}, u32[]{:S(2)}) copy-start(bf16[8,64,1024]{2,1,0:T(8,128)(2,1)S(1)} %collective-permute-done.5.refs_0_) | copy-start | bytes 3145732
  364.4 30.8 %all-to-all-start.3 = ((s16[4,2064,128]{2,1,0:T(8,128)(2,1)}), s16[4,2064,128]{2,1,0:T(8,128)(2,1)}, u32[]{:S(2)}, u32[]{:S(2)}) async-start(s16[4,2064,128]{2,1,0:T(8,128)(2,1)} %gram_tiles.3), calls=%async_computation.3 | async-start | bytes 4227072 | tf_op jit(solution)/shard_map/all_to_all | solution.py:297
  395.2 29.9 %all-to-all-start.1 = ((s16[4,2064,128]{2,1,0:T(8,128)(2,1)}), s16[4,2064,128]{2,1,0:T(8,128)(2,1)}, u32[]{:S(2)}, u32[]{:S(2)}) async-start(s16[4,2064,128]{2,1,0:T(8,128)(2,1)} %gram_tiles.2), calls=%async_computation.1 | async-start | bytes 4227072 | tf_op jit(solution)/shard_map/all_to_all | solution.py:297
  402.9 22.6 %collective-permute-start.8 = (s16[1,2064,128]{2,1,0:T(8,128)(2,1)}, s16[1,2064,128]{2,1,0:T(8,128)(2,1)S(1)}, u32[]{:S(2)}, u32[]{:S(2)}) collective-permute-start(s16[1,2064,128]{2,1,0:T(8,128)(2,1)} %sum_tiles.2), channel_id=1, source_target_pairs={{0,40},{4,28},{8,48},{12,36},{16,56},{20,44},{24,0},{28,52},{32,8}... | collective-permute-start | bytes 1585160 | tf_op jit(solution)/shard_map/ppermute | solution.py:294
  425.5 0.8 copy-start.1

commit v4 on v3

--- a/solution.py
+++ b/solution.py
@@ -81,15 +81,24 @@
 
 def copy_parts(arrays, shapes, copies, name):
     def kernel(*refs):
-        in_refs, out_refs, sems = refs[: len(arrays)], refs[len(arrays) : -1], refs[-1]
-        moves = [
-            pltpu.make_async_copy(in_refs[a].at[i], out_refs[r].at[k], sems.at[q])
-            for q, (a, i, r, k) in enumerate(copies)
-        ]
-        for move in moves:
-            move.start()
-        for move in moves:
-            move.wait()
+        in_refs, out_refs = refs[: len(arrays)], refs[len(arrays) : len(arrays) + len(shapes)]
+        held, (in_sems, out_sems) = refs[len(arrays) + len(shapes) : -2], refs[-2:]
+
+        def load(q):
+            a, i, _, _, _ = copies[q]
+            return pltpu.make_async_copy(in_refs[a].at[i], held[q], in_sems.at[q])
+
+        def store(q):
+            _, _, _, r, k = copies[q]
+            return pltpu.make_async_copy(held[q], out_refs[r].at[k], out_sems.at[q])
+
+        for q in range(len(copies)):
+            load(q).start()
+        for q in range(len(copies)):
+            load(q).wait()
+            store(q).start()
+        for q in range(len(copies)):
+            store(q).wait()
 
     size = 2 * sum(int(np.prod(shape)) for shape in shapes)
     return pl.pallas_call(
@@ -97,7 +106,8 @@
         out_shape=[jax.ShapeDtypeStruct(shape, arrays[0].dtype) for shape in shapes],
         in_specs=[HBM] * len(arrays),
         out_specs=[HBM] * len(shapes),
-        scratch_shapes=[pltpu.SemaphoreType.DMA((len(copies),))],
+        scratch_shapes=[pltpu.VMEM(shape, arrays[0].dtype) for _, _, shape, _, _ in copies]
+        + [pltpu.SemaphoreType.DMA((len(copies),))] * 2,
         compiler_params=pltpu.CompilerParams(vmem_limit_bytes=VMEM),
         cost_estimate=pl.CostEstimate(flops=0, bytes_accessed=2 * size, transcendentals=0),
         name=name,
@@ -305,17 +315,23 @@
     whole = pl.ds(0, group)
     half = [pl.ds(0, lines), pl.ds(lines, lines)]
     unit = (rows, WIDTH)
+    parts = [(0, 0, 4, 0), (0, 4, 4, 0), (1, 0, 4, 1), (1, 4, 4, 1), (2, 0, 4, 2), (3, 4, 4, 2), (4, 0, 4, 3), (4, 4, 4, 3)]
     (near,) = copy_parts(
         near_parts,
         [(group, 4, *unit)],
-        [(0, whole, 0, (whole, 0)), (1, whole, 0, (whole, 1)), (2, half[0], 0, (half[0], 2)),
-         (3, half[0], 0, (half[1], 2)), (4, whole, 0, (whole, 3))],
+        [
+            (a, pl.ds(first if near_parts[a].shape[0] == group else 0, n), (n, *unit), 0, (pl.ds(first, n), slot))
+            for a, first, n, slot in parts
+        ],
         "join_near",
     )
     near = spread(near, ("c", "x")).reshape(group * 4, *unit)
     sent = [k for k, s in enumerate(FAR_STEPS) if s]
     far_parts = copy_parts(
-        [far], [(group, *unit)] * len(sent), [(0, (whole, k), q, whole) for q, k in enumerate(sent)], "part_far"
+        [far],
+        [(group, *unit)] * len(sent),
+        [(0, (h, k), (lines, *unit), q, h) for q, k in enumerate(sent) for h in half],
+        "part_far",
     )
     far_parts = [away(part, FAR_STEPS[k]) for part, k in zip(far_parts, sent)]
     far_pieces = [(q, whole) for q in range(len(sent))] + [(len(sent), (whole, FAR_STEPS.index(0)))]

time: 432 us -> 214 us (0.50)
  Pallas kernels: 266 us -> 48 us
    pallas_call x2, Pallas kernels: 225 us -> 6.42 us  [copy_parts(): pl.pallas_call(kernel, out_shape=[jax.ShapeDtypeStruct(shape, arrays[0].d...]
  transfers between devices with their start and end apart: 13 -> 13, of which waited for: 7 -> 7; matrix products, arithmetic and copies ran while one was open for 0% -> 1% of each run, Pallas kernels for 59% -> 16%
where the time goes in v4:
time: 214 us; the launch traced here: 212 us
  waiting for transfers between devices  115 us (54%)
  Pallas kernels  48 us (22%)
  starting transfers between devices  41.4 us (19%)
  local copies, waits for them, and re-layouts  5.23 us (2%)
    ppermute x4, waiting for transfers between devices, up(): lax.ppermute(value, 'z', [(b, (b + step) % planes) for b in range(planes)])  41.2 us
    ppermute x5, waiting for transfers between devices, away(): return lax.ppermute(value, ('z', 'c'), moves)  40.5 us
    all_to_all x4, waiting for transfers between devices, spread(): return lax.all_to_all(value, axes, split_axis=0, concat_axis=0, tiled=True)  33.2 us
    pallas_call x2, Pallas kernels, gram_tiles(): pl.pallas_call(kernel, out_shape=jax.ShapeDtypeStruct((4, quarter * BLOCK...  25.2 us
    all_to_all x4, starting transfers between devices, spread(): return lax.all_to_all(value, axes, split_axis=0, concat_axis=0, tiled=True)  20.7 us
    ppermute x5, starting transfers between devices, away(): return lax.ppermute(value, ('z', 'c'), moves)  12.4 us
    pallas_call x1, Pallas kernels, scale_columns(): pl.pallas_call(kernel, out_shape=[jax.ShapeDtypeStruct((size, rows, WIDTH...  9.82 us
    ppermute x4, starting transfers between devices, up(): lax.ppermute(value, 'z', [(b, (b + step) % planes) for b in range(planes)])  8.34 us
  transfers between devices with their start and end apart: 13, of which 7 were waited for; matrix products, arithmetic and copies ran while one was open for 1% of the time, Pallas kernels for 16%

profile of v4, /device:TPU:2, one launch (start us, length us, event | category | flops | bytes accessed | tf_op | source)
XLA Modules:
  0.0 211.5 jit_solution(16902897152743086062)
XLA Ops:
  0.0 1.3 fusion.1.owners_ref
  1.3 1.3 broadcast_in_dim.2.weight_ref
  2.6 9.8 %scale_columns.1 = (bf16[32,64,1024]{2,1,0:T(8,128)(2,1)}, bf16[8,64,1024]{2,1,0:T(8,128)(2,1)}, bf16[8,64,1024]{2,1,0:T(8,128)(2,1)}, bf16[4,64,1024]{2,1,0:T(8...) custom-call(s32[64]{0:T(128)} %fusion.1.owners_ref, s32[512]{0:T(512)} %order_ref.1, ...), custom_call_target="tpu_custom_call" | custom-call | flops 4194304 | bytes 16777216 | tf_op jit(solution)/shard_map/scale_columns/pallas_call | solution.py:58
  12.4 0.0 copy-start.7
  12.4 6.8 %all-to-all-start.2 = ((bf16[8,4,64,1024]{3,2,1,0:T(8,128)(2,1)}), bf16[8,4,64,1024]{3,2,1,0:T(8,128)(2,1)}, u32[]{:S(2)}, u32[]{:S(2)}) async-start(bf16[8,4,64,1024]{3,2,1,0:T(8,128)(2,1)} %bitcast.2), calls=%async_computation.2 | async-start | bytes 8388608 | tf_op jit(solution)/shard_map/all_to_all | solution.py:307
  19.3 0.2 collective-permute-start
  19.5 0.0 copy-done.7
  19.5 4.0 %collective-permute-start.1 = (bf16[8,64,1024]{2,1,0:T(8,128)(2,1)S(1)}, bf16[8,64,1024]{2,1,0:T(8,128)(2,1)}, u32[]{:S(2)}, u32[]{:S(2)}) collective-permute-start(bf16[8,64,1024]{2,1,0:T(8,128)(2,1)S(1)} %copy-done.7), channel_id=1, source_target_pairs={{0,56},{8,0},{16,8},{24,16},{32,24},{40,32},{48,40},{56,48},{1,57}... | collective-permute-start | bytes 3145736 | tf_op jit(solution)/shard_map/ppermute | solution.py:300
  23.5 0.0 collective-permute-start.2
  23.5 4.1 %collective-permute-start.3 = (bf16[4,64,1024]{2,1,0:T(8,128)(2,1)}, bf16[4,64,1024]{2,1,0:T(8,128)(2,1)S(1)}, u32[]{:S(2)}, u32[]{:S(2)}) collective-permute-start(bf16[4,64,1024]{2,1,0:T(8,128)(2,1)} %get-tuple-element.17), channel_id=1, source_target_pairs={{0,48},{8,56},{16,0},{24,8},{32,16},{40,24},{48,32},{56,40},{1,49}... | collective-permute-start | bytes 1572872 | tf_op jit(solution)/shard_map/ppermute | solution.py:300
  27.6 32.8 %collective-permute-done.2.refs_2_ = bf16[4,64,1024]{2,1,0:T(8,128)(2,1)S(1)} collective-permute-done((bf16[4,64,1024]{2,1,0:T(8,128)(2,1)}, bf16[4,64,1024]{2,1,0:T(8,128)(2,1)S(1)}, u32[]{:S(2)}, u32[]{:S(2)}) %collective-permute-start.2) | collective-permute-done | bytes 524320 | tf_op jit(solution)/shard_map/ppermute | solution.py:300
  60.4 8.4 %collective-permute-done.3.refs_3_ = bf16[4,64,1024]{2,1,0:T(8,128)(2,1)S(1)} collective-permute-done((bf16[4,64,1024]{2,1,0:T(8,128)(2,1)}, bf16[4,64,1024]{2,1,0:T(8,128)(2,1)S(1)}, u32[]{:S(2)}, u32[]{:S(2)}) %collective-permute-start.3) | collective-permute-done | bytes 524320 | tf_op jit(solution)/shard_map/ppermute | solution.py:300
  68.8 0.0 collective-permute-done.refs_0_
  68.8 0.8 copy-done.3
  69.6 0.0 collective-permute-done.1.refs_1_
  69.6 0.0 copy-done.2
  69.6 1.0 copy-done
  70.6 3.6 %join_near.1 = bf16[8,4,64,1024]{3,2,1,0:T(8,128)(2,1)} custom-call(bf16[8,64,1024]{2,1,0:T(8,128)(2,1)} %copy-done, bf16[8,64,1024]{2,1,0:T(8,128)(2,1)} %collective-permute-done.1.refs_1_, bf16[4,64,1024]{2,1,0:T(8,128)(2,1)} %copy-done.2, bf16[4,64,1024]{2,1,0:T(8,128)(2,1)} %copy-done.3, bf16[8,64,1024]{2,1,0:T(8,128)(2,1)} %get-tuple-element.18.refs_4_), custom_call_target="tpu_custom_call" | custom-call | bytes 8388608 | tf_op jit(solution)/shard_map/join_near/pallas_call | solution.py:104
  74.2 0.0 all-to-all-done.2.refs_0_.refs_3_
  74.2 4.9 %all-to-all-start = ((bf16[8,4,64,1024]{3,2,1,0:T(8,128)(2,1)}), bf16[8,4,64,1024]{3,2,1,0:T(8,128)(2,1)}, u32[]{:S(2)}, u32[]{:S(2)}) async-start(bf16[8,4,64,1024]{3,2,1,0:T(8,128)(2,1)} %join_near.1), calls=%async_computation | async-start | bytes 8388608 | tf_op jit(solution)/shard_map/all_to_all | solution.py:307
  79.1 2.8 %part_far.1 = (bf16[8,64,1024]{2,1,0:T(8,128)(2,1)}, bf16[8,64,1024]{2,1,0:T(8,128)(2,1)}, bf16[8,64,1024]{2,1,0:T(8,128)(2,1)}) custom-call(bf16[8,4,64,1024]{3,2,1,0:T(8,128)(2,1)} %all-to-all-done.2.refs_0_.refs_3_), custom_call_target="tpu_custom_call" | custom-call | bytes 6291456 | tf_op jit(solution)/shard_map/part_far/pallas_call | solution.py:104
  81.9 4.6 %collective-permute-start.5 = (bf16[8,64,1024]{2,1,0:T(8,128)(2,1)}, bf16[8,64,1024]{2,1,0:T(8,128)(2,1)S(1)}, u32[]{:S(2)}, u32[]{:S(2)}) collective-permute-start(bf16[8,64,1024]{2,1,0:T(8,128)(2,1)} %get-tuple-element.20), channel_id=1, source_target_pairs={{0,48},{4,20},{8,56},{12,28},{16,0},{20,36},{24,8},{28,44},{32,16}... | collective-permute-start | bytes 3145736 | tf_op jit(solution)/shard_map/ppermute | solution.py:304
  86.5 1.2 collective-permute-start.6
  87.6 0.8 collective-permute-start.7
  88.5 0.0 copy-done.5
  88.5 0.1 copy.9
  88.6 0.1 reshape.10.pairs_ref
  88.7 0.0 copy-start.4
  89.4 2.8 %collective-permute-start.4 = (s32[129]{0:T(256)S(1)}, s32[129]{0:T(256)S(1)}, u32[]{:S(2)}, u32[]{:S(2)}) collective-permute-start(s32[129]{0:T(256)S(1)} %pad_add_fusion), channel_id=1, source_target_pairs={{0,24},{4,44},{8,32},{12,52},{16,40},{20,60},{24,48},{28,4},{32,56... | collective-permute-start | bytes 1556 | tf_op jit(solution)/shard_map/ppermute | solution.py:304
  92.2 32.7 %collective-permute-done.4 = s32[129]{0:T(256)S(1)} collective-permute-done((s32[129]{0:T(256)S(1)}, s32[129]{0:T(256)S(1)}, u32[]{:S(2)}, u32[]{:S(2)}) %collective-permute-start.4) | collective-permute-done | bytes 548 | tf_op jit(solution)/shard_map/ppermute | solution.py:304
  124.9 0.5 slice.6.pairs_ref
  125.4 0.5 slice.7.count_ref
  125.9 0.0 collective-permute-done.5.refs_0_
  126.0 7.3 %collective-permute-done.6.refs_1_ = bf16[8,64,1024]{2,1,0:T(8,128)(2,1)} collective-permute-done((bf16[8,64,1024]{2,1,0:T(8,128)(2,1)}, bf16[8,64,1024]{2,1,0:T(8,128)(2,1)}, u32[]{:S(2)}, u32[]{:S(2)}) %collective-permute-start.6) | collective-permute-done | bytes 1048608 | tf_op jit(solution)/shard_map/ppermute | solution.py:304
  133.3 0.0 collective-permute-done.7.refs_2_
  133.3 0.0 copy-done.6
  133.3 12.9 %gram_tiles.3 = s16[4,2064,128]{2,1,0:T(8,128)(2,1)} custom-call(s32[128]{0:T(128)} %slice.6.pairs_ref, s32[1]{0:T(128)} %slice.7.count_ref, bf16[8,64,1024]{2,1,0:T(8,128)(2,1)} %copy-done.6, bf16[8,64,1024]{2,1,0:T(8,128)(2,1)} %collective-permute-done.6.refs_1_, bf16[8,64,1024]{2,1,0:T(8,128)(2,1)} %collective-permute-done.7.refs_2_, ...), custom_call_target="tpu_custom_call" | custom-call | flops 4294967296 | bytes 6291456 | tf_op jit(solution)/shard_map/gram_tiles/pallas_call | solution.py:192
  146.2 0.0 all-to-all-done
  146.2 4.5 %all-to-all-start.3 = ((s16[4,2064,128]{2,1,0:T(8,128)(2,1)}), s16[4,2064,128]{2,1,0:T(8,128)(2,1)}, u32[]{:S(2)}, u32[]{:S(2)}) async-start(s16[4,2064,128]{2,1,0:T(8,128)(2,1)} %gram_tiles.3), calls=%async_computation.3 | async-start | bytes 4227072 | tf_op jit(solution)/shard_map/all_to_all | solution.py:307
  150.7 12.3 %gram_tiles.2 = s16[4,2064,128]{2,1,0:T(8,128)(2,1)} custom-call(s32[128]{0:T(128)} %copy-done.4, s32[1]{0:T(128)S(6)} %copy.10.count_ref, bf16[32,64,1024]{2,1,0:T(8,128)(2,1)} %bitcast.refs_0_), custom_call_target="tpu_custom_call" | custom-call | flops 4294967296 | bytes 6291456 | tf_op jit(solution)/shard_map/gram_tiles/pallas_call | solution.py:192
  163.0 14.0 %all-to-all-done.3.refs_0_ = s16[4,2064,128]{2,1,0:T(8,128)(2,1)} async-done(((s16[4,2064,128]{2,1,0:T(8,128)(2,1)}), s16[4,2064,128]{2,1,0:T(8,128)(2,1)}, u32[]{:S(2)}, u32[]{:S(2)}) %all-to-all-start.3) | async-done | bytes 2113568 | tf_op jit(solution)/shard_map/all_to_all | solution.py:307
  177.0 4.5 %all-to-all-start.1 = ((s16[4,2064,128]{2,1,0:T(8,128)(2,1)}), s16[4,2064,128]{2,1,0:T(8,128)(2,1)}, u32[]{:S(2)}, u32[]{:S(2)}) async-start(s16[4,2064,128]{2,1,0:T(8,128)(2,1)} %gram_tiles.2), calls=%async_computation.1 | async-start | bytes 4227072 | tf_op jit(solution)/shard_map/all_to_all | solution.py:307
  181.5 3.3 %sum_tiles.2 = s16[1,2064,128]{2,1,0:T(8,128)(2,1)} custom-call(s16[4,2064,128]{2,1,0:T(8,128)(2,1)} %all-to-all-done.3.refs_0_), custom_call_target="tpu_custom_call" | custom-call | flops 4227072 | bytes 3170304 | tf_op jit(solution)/shard_map/sum_tiles/pallas_call | solution.py:263
  184.7 3.0 %collective-permute-start.8 = (s16[1,2064,128]{2,1,0:T(8,128)(2,1)}, s16[1,2064,128]{2,1,0:T(8,128)(2,1)S(1)}, u32[]{:S(2)}, u32[]{:S(2)}) collective-permute-start(s16[1,2064,128]{2,1,0:T(8,128)(2,1)} %sum_tiles.2), channel_id=1, source_target_pairs={{0,40},{4,28},{8,48},{12,36},{16,56},{20,44},{24,0},{28,52},{32,8}... | collective-permute-start | bytes 1585160 | tf_op jit(solution)/shard_map/ppermute | solution.py:304
  187.7 19.1 %all-to-all-done.1.refs_0_ = s16[4,2064,128]{2,1,0:T(8,128)(2,1)} async-done(((s16[4,2064,128]{2,1,0:T(8,128)(2,1)}), s16[4,2064,128]{2,1,0:T(8,128)(2,1)}, u32[]{:S(2)}, u32[]{:S(2)}) %all-to-all-start.1) | async-done | bytes 2113568 | tf_op jit(solution)/shard_map/all_to_all | solution.py:307
  206.9 0.5 collective-permute-done.8.refs_1_
  207.4 0.8 copy-done.1
  208.2 3.4 %sum_tiles.3 = f32[16,128,128]{2,1,0:T(8,128)} custom-call(s16[4,2064,128]{2,1,0:T(8,128)(2,1)} %all-to-all-done.1.refs_0_, s16[1,2064,128]{2,1,0:T(8,128)(2,1)} %copy-done.1), custom_call_target="tpu_custom_call" | custom-call | flops 5283840 | bytes 3698688 | tf_op jit(solution)/shard_map/sum_tiles/pallas_call | solution.py:263
  (8 shorter events, 0.0 us)
Async XLA Ops:
  12.4 7.0 %copy-start.7 = (bf16[8,64,1024]{2,1,0:T(8,128)(2,1)S(1)}, bf16[8,64,1024]{2,1,0:T(8,128)(2,1)}, u32[]{:S(2)}) copy-start(bf16[8,64,1024]{2,1,0:T(8,128)(2,1)} %get-tuple-element.15) | copy-start | bytes 3145732
  12.4 61.7 %all-to-all-start.2 = ((bf16[8,4,64,1024]{3,2,1,0:T(8,128)(2,1)}), bf16[8,4,64,1024]{3,2,1,0:T(8,128)(2,1)}, u32[]{:S(2)}, u32[]{:S(2)}) async-start(bf16[8,4,64,1024]{3,2,1,0:T(8,128)(2,1)} %bitcast.2), calls=%async_computation.2 | async-start | bytes 8388608 | tf_op jit(solution)/shard_map/all_to_all | solution.py:307
  19.3 49.5 %collective-permute-start = (bf16[8,64,1024]{2,1,0:T(8,128)(2,1)}, bf16[8,64,1024]{2,1,0:T(8,128)(2,1)S(1)}, u32[]{:S(2)}, u32[]{:S(2)}) collective-permute-start(bf16[8,64,1024]{2,1,0:T(8,128)(2,1)} %get-tuple-element.14), channel_id=1, source_target_pairs={{0,8},{8,16},{16,24},{24,32},{32,40},{40,48},{48,56},{56,0},{1,9},... | collective-permute-start | bytes 3145736 | tf_op jit(solution)/shard_map/ppermute | solution.py:300
  19.5 50.1 %collective-permute-start.1 = (bf16[8,64,1024]{2,1,0:T(8,128)(2,1)S(1)}, bf16[8,64,1024]{2,1,0:T(8,128)(2,1)}, u32[]{:S(2)}, u32[]{:S(2)}) collective-permute-start(bf16[8,64,1024]{2,1,0:T(8,128)(2,1)S(1)} %copy-done.7), channel_id=1, source_target_pairs={{0,56},{8,0},{16,8},{24,16},{32,24},{40,32},{48,40},{56,48},{1,57}... | collective-permute-start | bytes 3145736 | tf_op jit(solution)/shard_map/ppermute | solution.py:300
  23.5 37.0 %collective-permute-start.2 = (bf16[4,64,1024]{2,1,0:T(8,128)(2,1)}, bf16[4,64,1024]{2,1,0:T(8,128)(2,1)S(1)}, u32[]{:S(2)}, u32[]{:S(2)}) collective-permute-start(bf16[4,64,1024]{2,1,0:T(8,128)(2,1)} %get-tuple-element.16), channel_id=1, source_target_pairs={{0,16},{8,24},{16,32},{24,40},{32,48},{40,56},{48,0},{56,8},{1,17}... | collective-permute-start | bytes 1572872 | tf_op jit(solution)/shard_map/ppermute | solution.py:300
  23.5 45.3 %collective-permute-start.3 = (bf16[4,64,1024]{2,1,0:T(8,128)(2,1)}, bf16[4,64,1024]{2,1,0:T(8,128)(2,1)S(1)}, u32[]{:S(2)}, u32[]{:S(2)}) collective-permute-start(bf16[4,64,1024]{2,1,0:T(8,128)(2,1)} %get-tuple-element.17), channel_id=1, source_target_pairs={{0,48},{8,56},{16,0},{24,8},{32,16},{40,24},{48,32},{56,40},{1,49}... | collective-permute-start | bytes 1572872 | tf_op jit(solution)/shard_map/ppermute | solution.py:300
  60.4 9.2 %copy-start.2 = (bf16[4,64,1024]{2,1,0:T(8,128)(2,1)}, bf16[4,64,1024]{2,1,0:T(8,128)(2,1)S(1)}, u32[]{:S(2)}) copy-start(bf16[4,64,1024]{2,1,0:T(8,128)(2,1)S(1)} %collective-permute-done.2.refs_2_) | copy-start | bytes 1572868
  68.8 0.8 copy-start.3
  69.6 1.0 copy-start
  74.2 72.0 %all-to-all-start = ((bf16[8,4,64,1024]{3,2,1,0:T(8,128)(2,1)}), bf16[8,4,64,1024]{3,2,1,0:T(8,128)(2,1)}, u32[]{:S(2)}, u32[]{:S(2)}) async-start(bf16[8,4,64,1024]{3,2,1,0:T(8,128)(2,1)} %join_near.1), calls=%async_computation | async-start | bytes 8388608 | tf_op jit(solution)/shard_map/all_to_all | solution.py:307
  79.1 9.4 %copy-start.5 = (s32[1,64,2]{1,2,0:T(2,128)S(1)}, s32[1,64,2]{1,2,0:T(2,128)}, u32[]{:S(2)}) copy-start(s32[1,64,2]{1,2,0:T(2,128)} %param.10) | copy-start | bytes 1540
  81.9 44.1 %collective-permute-start.5 = (bf16[8,64,1024]{2,1,0:T(8,128)(2,1)}, bf16[8,64,1024]{2,1,0:T(8,128)(2,1)S(1)}, u32[]{:S(2)}, u32[]{:S(2)}) collective-permute-start(bf16[8,64,1024]{2,1,0:T(8,128)(2,1)} %get-tuple-element.20), channel_id=1, source_target_pairs={{0,48},{4,20},{8,56},{12,28},{16,0},{20,36},{24,8},{28,44},{32,16}... | collective-permute-start | bytes 3145736 | tf_op jit(solution)/shard_map/ppermute | solution.py:304
  86.5 46.8 %collective-permute-start.6 = (bf16[8,64,1024]{2,1,0:T(8,128)(2,1)}, bf16[8,64,1024]{2,1,0:T(8,128)(2,1)}, u32[]{:S(2)}, u32[]{:S(2)}) collective-permute-start(bf16[8,64,1024]{2,1,0:T(8,128)(2,1)} %get-tuple-element.21), channel_id=1, source_target_pairs={{0,56},{4,12},{8,0},{12,20},{16,8},{20,28},{24,16},{28,36},{32,24}... | collective-permute-start | bytes 3145736 | tf_op jit(solution)/shard_map/ppermute | solution.py:304
  87.6 45.6 %collective-permute-start.7 = (bf16[8,64,1024]{2,1,0:T(8,128)(2,1)}, bf16[8,64,1024]{2,1,0:T(8,128)(2,1)}, u32[]{:S(2)}, u32[]{:S(2)}) collective-permute-start(bf16[8,64,1024]{2,1,0:T(8,128)(2,1)} %get-tuple-element.22), channel_id=1, source_target_pairs={{0,8},{4,60},{8,16},{12,4},{16,24},{20,12},{24,32},{28,20},{32,40}... | collective-permute-start | bytes 3145736 | tf_op jit(solution)/shard_map/ppermute | solution.py:304
  88.7 57.4 %copy-start.4 = (s32[128]{0:T(128)}, s32[128]{0:T(128)S(1)}, u32[]{:S(2)}) copy-start(s32[128]{0:T(128)S(1)} %reshape.10.pairs_ref) | copy-start | bytes 1540
  89.4 35.5 %collective-permute-start.4 = (s32[129]{0:T(256)S(1)}, s32[129]{0:T(256)S(1)}, u32[]{:S(2)}, u32[]{:S(2)}) collective-permute-start(s32[129]{0:T(256)S(1)} %pad_add_fusion), channel_id=1, source_target_pairs={{0,24},{4,44},{8,32},{12,52},{16,40},{20,60},{24,48},{28,4},{32,56... | collective-permute-start | bytes 1556 | tf_op jit(solution)/shard_map/ppermute | solution.py:304
  125.9 7.3 %copy-start.6 = (bf16[8,64,1024]{2,1,0:T(8,128)(2,1)}, bf16[8,64,1024]{2,1,0:T(8,128)(2,1)S(1)}, u32[]{:S(2)}) copy-start(bf16[8,64,1024]{2,1,0:T(8,128)(2,1)S(1)} %collective-permute-done.5.refs_0_) | copy-start | bytes 3145732
  146.2 30.8 %all-to-all-start.3 = ((s16[4,2064,128]{2,1,0:T(8,128)(2,1)}), s16[4,2064,128]{2,1,0:T(8,128)(2,1)}, u32[]{:S(2)}, u32[]{:S(2)}) async-start(s16[4,2064,128]{2,1,0:T(8,128)(2,1)} %gram_tiles.3), calls=%async_computation.3 | async-start | bytes 4227072 | tf_op jit(solution)/shard_map/all_to_all | solution.py:307
  177.0 29.8 %all-to-all-start.1 = ((s16[4,2064,128]{2,1,0:T(8,128)(2,1)}), s16[4,2064,128]{2,1,0:T(8,128)(2,1)}, u32[]{:S(2)}, u32[]{:S(2)}) async-start(s16[4,2064,128]{2,1,0:T(8,128)(2,1)} %gram_tiles.2), calls=%async_computation.1 | async-start | bytes 4227072 | tf_op jit(solution)/shard_map/all_to_all | solution.py:307
  184.7 22.6 %collective-permute-start.8 = (s16[1,2064,128]{2,1,0:T(8,128)(2,1)}, s16[1,2064,128]{2,1,0:T(8,128)(2,1)S(1)}, u32[]{:S(2)}, u32[]{:S(2)}) collective-permute-start(s16[1,2064,128]{2,1,0:T(8,128)(2,1)} %sum_tiles.2), channel_id=1, source_target_pairs={{0,40},{4,28},{8,48},{12,36},{16,56},{20,44},{24,0},{28,52},{32,8}... | collective-permute-start | bytes 1585160 | tf_op jit(solution)/shard_map/ppermute | solution.py:304
  207.4 0.8 copy-start.1

commit v5 on v4

--- a/solution.py
+++ b/solution.py
@@ -10,51 +10,64 @@
 OWN_BLOCKS = 8
 WIDTH = OWN_BLOCKS * BLOCK
 FAR = 3
-FAR_STEPS = (-2, -1, 1, 0)
+FAR_FIRST, FAR_THEN = (-2, -1, 0), (1,)
 CODES = 32000.0
 VMEM = 62 << 20
 HBM = pl.BlockSpec(memory_space=pltpu.HBM)
 
 
-def scale_columns(owners, order, jacobian, weight, shapes):
+def scale_columns(units, order, jacobian, weight, shapes):
     sizes = [int(np.prod(shape)) for shape in shapes]
-    units = sum(sizes)
     firsts = np.cumsum([0, *sizes])
+    total = int(firsts[-1])
     rows, zones = jacobian.shape
-    cuts, batch = 8, 4
-
-    def kernel(owners_ref, order_ref, jac_ref, weight_ref, *refs):
+    planes, cores = lax.axis_size("z"), lax.axis_size("c")
+    halves, cuts = 2, 4
+
+    def kernel(units_ref, order_ref, jac_ref, weight_ref, *refs):
         out_refs, (held, made, in_sems, out_sems) = refs[:-4], refs[-4:]
-        cut = rows // cuts
-
-        def load(q):
-            span = pl.ds(q * cut, cut)
-            return pltpu.make_async_copy(jac_ref.at[span], held.at[span], in_sems.at[q])
-
-        def store(q):
-            unit = made.at[pl.ds(int(firsts[q]), sizes[q])]
-            return pltpu.make_async_copy(unit, out_refs[q], out_sems.at[q])
-
-        for q in range(cuts):
-            load(q).start()
-        for q in range(cuts):
-            load(q).wait()
-        root = jnp.sqrt(weight_ref[...])
-
-        def unit(u, carry):
-            base = owners_ref[u] * OWN_BLOCKS
-            for b in range(OWN_BLOCKS):
-                start = pl.multiple_of(order_ref[base + b] * BLOCK, BLOCK)
-                piece = held[:, pl.ds(start, BLOCK)].astype(jnp.float32) * root
-                made[u, :, b * BLOCK : (b + 1) * BLOCK] = piece.astype(jnp.bfloat16)
-            return carry
-
-        for q in range(len(sizes)):
-            lax.fori_loop(int(firsts[q]), int(firsts[q + 1]), unit, 0)
-            store(q).start()
-        for q in range(len(sizes)):
-            store(q).wait()
-
+        half, cut = rows // halves, rows // halves // cuts
+        z = lax.axis_index("z")
+
+        def load(h, q):
+            span = pl.ds(h * half + q * cut, cut)
+            return pltpu.make_async_copy(jac_ref.at[span], held.at[span], in_sems.at[h, q])
+
+        def store(h, q):
+            span = pl.ds(h * half, half)
+            unit = made.at[pl.ds(int(firsts[q]), sizes[q]), span]
+            return pltpu.make_async_copy(unit, out_refs[q].at[:, span], out_sems.at[h, q])
+
+        for h in range(halves):
+            for q in range(cuts):
+                load(h, q).start()
+        row = lax.broadcasted_iota(jnp.int32, (rows, rows), 0)
+        col = lax.broadcasted_iota(jnp.int32, (rows, rows), 1)
+        root = jnp.sum(jnp.where(row == col, jnp.sqrt(weight_ref[...]), 0.0), axis=1, keepdims=True)
+        for h in range(halves):
+            for q in range(cuts):
+                load(h, q).wait()
+            span = pl.ds(h * half, half)
+            scale = jnp.broadcast_to(root[h * half : (h + 1) * half], (half, BLOCK))
+
+            def unit(u, carry, span=span, scale=scale):
+                what = units_ref[u]
+                plane = (z + what % planes) % planes
+                base = (what // planes + plane * cores) * OWN_BLOCKS
+                for b in range(OWN_BLOCKS):
+                    start = pl.multiple_of(order_ref[base + b] * BLOCK, BLOCK)
+                    piece = held[span, pl.ds(start, BLOCK)].astype(jnp.float32) * scale
+                    made[u, span, b * BLOCK : (b + 1) * BLOCK] = piece.astype(jnp.bfloat16)
+                return carry
+
+            for q in range(len(sizes)):
+                lax.fori_loop(int(firsts[q]), int(firsts[q + 1]), unit, 0, unroll=2)
+                store(h, q).start()
+        for h in range(halves):
+            for q in range(len(sizes)):
+                store(h, q).wait()
+
+    codes = [(a * planes * cores + c) * planes + s % planes for a, c, s in units]
     flat = pl.pallas_call(
         kernel,
         out_shape=[jax.ShapeDtypeStruct((size, rows, WIDTH), jnp.bfloat16) for size in sizes],
@@ -65,17 +78,17 @@
             out_specs=[HBM] * len(sizes),
             scratch_shapes=[
                 pltpu.VMEM((rows, zones), jnp.bfloat16),
-                pltpu.VMEM((units, rows, WIDTH), jnp.bfloat16),
-                pltpu.SemaphoreType.DMA((cuts,)),
-                pltpu.SemaphoreType.DMA((len(sizes),)),
+                pltpu.VMEM((total, rows, WIDTH), jnp.bfloat16),
+                pltpu.SemaphoreType.DMA((halves, cuts)),
+                pltpu.SemaphoreType.DMA((halves, len(sizes))),
             ],
         ),
         compiler_params=pltpu.CompilerParams(vmem_limit_bytes=VMEM),
         cost_estimate=pl.CostEstimate(
-            flops=units * rows * WIDTH, bytes_accessed=2 * (rows * zones + units * rows * WIDTH), transcendentals=0
+            flops=total * rows * WIDTH, bytes_accessed=2 * (rows * zones + total * rows * WIDTH), transcendentals=0
         ),
         name="scale_columns",
-    )(owners, order, jacobian, weight)
+    )(jnp.array(codes, jnp.int32), order, jacobian, weight)
     return [part.reshape(*shape, rows, WIDTH) for part, shape in zip(flat, shapes)]
 
 
@@ -126,23 +139,25 @@
     return jnp.max(jnp.abs(tile), axis=0, keepdims=True)
 
 
-def gram_tiles(arrays, pieces, pairs, count):
+def gram_tiles(arrays, pieces, pairs, count, apart):
     rows = arrays[0].shape[-2]
     deep = 8 * rows
     total = len(pieces) * deep
     slots = pairs.shape[0] // 2
     quarter = slots // 4
     strip = 256
+    outs = [1, 1, 1, 1] if apart else [4]
 
     def kernel(pairs_ref, count_ref, *refs):
-        array_refs, (out_ref, held, gram, made, powers, sems, out_sems) = refs[:-7], refs[-7:]
+        array_refs, out_refs, (held, gram, made, powers, sems, out_sems) = refs[: len(arrays)], refs[len(arrays) : -6], refs[-6:]
+        own = lax.axis_index("y") if apart else 0
 
         def load(p):
             a, i = pieces[p]
             return pltpu.make_async_copy(array_refs[a].at[i], held.at[pl.ds(p * 8, 8)], sems.at[p])
 
         def store(t):
-            return pltpu.make_async_copy(made.at[t], out_ref.at[t], out_sems.at[t])
+            return pltpu.make_async_copy(made.at[t], out_refs[t].at[0] if apart else out_refs[0].at[t], out_sems.at[t])
 
         for p in range(len(pieces)):
             load(p).start()
@@ -150,24 +165,20 @@
             load(p).wait()
             units = pl.ds(p * 8, 8)
 
-            def multiply(m, carry, p=p, units=units):
-                lanes = pl.ds(pl.multiple_of(m * strip, strip), strip)
+            for m in range(0, WIDTH, strip):
                 part = lax.dot_general(
-                    held[units, :, lanes].reshape(deep, strip), held[units].reshape(deep, WIDTH),
+                    held[units, :, m : m + strip].reshape(deep, strip), held[units].reshape(deep, WIDTH),
                     (((0,), (0,)), ((), ())), preferred_element_type=jnp.float32,
                 )
                 if p == 0:
-                    gram[lanes, :] = part
+                    gram[m : m + strip, :] = part
                 else:
-                    gram[lanes, :] += part
-                return carry
-
-            lax.fori_loop(0, WIDTH // strip, multiply, 0)
+                    gram[m : m + strip, :] += part
 
         for t in range(4):
 
             def tile_of(k, t=t):
-                slot = t * quarter + k
+                slot = (own + t) % 4 * quarter + k
                 row = pl.multiple_of(pairs_ref[2 * slot] * BLOCK, BLOCK)
                 col = pl.multiple_of(pairs_ref[2 * slot + 1] * BLOCK, BLOCK)
                 return jnp.where(slot < count_ref[0], gram[pl.ds(row, BLOCK), pl.ds(col, BLOCK)], 0.0)
@@ -191,12 +202,12 @@
 
     return pl.pallas_call(
         kernel,
-        out_shape=jax.ShapeDtypeStruct((4, quarter * BLOCK + quarter, BLOCK), jnp.int16),
+        out_shape=[jax.ShapeDtypeStruct((n, quarter * BLOCK + quarter, BLOCK), jnp.int16) for n in outs],
         grid_spec=pltpu.PrefetchScalarGridSpec(
             num_scalar_prefetch=2,
             grid=(),
             in_specs=[HBM] * len(arrays),
-            out_specs=HBM,
+            out_specs=[HBM] * len(outs),
             scratch_shapes=[
                 pltpu.VMEM((len(pieces) * 8, rows, WIDTH), jnp.bfloat16),
                 pltpu.VMEM((WIDTH, WIDTH), jnp.float32),
@@ -280,21 +291,17 @@
 
 def body(jacobian, obs_weight, block_order, tile_pairs, tile_count):
     rows = jacobian.shape[0]
-    planes, lines, cores = lax.axis_size("z"), lax.axis_size("x"), lax.axis_size("c")
-    z = lax.axis_index("z")
-    weight = jnp.broadcast_to(obs_weight[:, None], (rows, BLOCK))
+    planes, lines, cores, quarters = (lax.axis_size(name) for name in ("z", "x", "c", "y"))
     group = lines * cores
+    weight = obs_weight.reshape(1, rows)
 
     dests = [(k % lines, k // lines) for k in range(group)]
-    units = [(a, c, (s - FAR) * (1 - 2 * c)) for a, c in dests for s in FAR_STEPS]
-    for s in (1, -1):
-        units += [(a, c, s) for a, c in dests]
-    for s in (2, -2):
-        units += [(a, c, s) for a, c in dests if (1 - 2 * c) * s > 0]
-    units += [(a, c, 0) for a, c in dests]
-    shapes = [(group, len(FAR_STEPS)), (group,), (group,), (lines,), (lines,), (group,)]
-    table = np.array(units, np.int32)
-    owners = table[:, 0] * (planes * cores) + table[:, 1] + (z + table[:, 2] + planes) % planes * cores
+
+    def far_units(steps):
+        return [(a, c, (s - FAR) * (1 - 2 * c)) for a, c in dests for s in steps]
+
+    def near_units(step, there):
+        return [(a, c, step) for a, c in dests if c in there]
 
     def up(value, step):
         return lax.ppermute(value, "z", [(b, (b + step) % planes) for b in range(planes)])
@@ -306,41 +313,60 @@
     def spread(value, axes):
         return lax.all_to_all(value, axes, split_axis=0, concat_axis=0, tiled=True)
 
+    def after(value, *others):
+        return lax.optimization_barrier((value, *others))[0]
+
     wanted = jnp.concatenate([tile_pairs.reshape(-1), tile_count])
     far_wanted = away(wanted, FAR)
 
-    far, up1, down1, up2, down2, stay = scale_columns(owners.astype(jnp.int32), block_order, jacobian, weight, shapes)
-    near_parts = [up(up1, 1), up(down1, -1), up(up2, 2), up(down2, -2), stay]
-    far = spread(far, ("c", "x"))
-    whole = pl.ds(0, group)
-    half = [pl.ds(0, lines), pl.ds(lines, lines)]
+    units = far_units(FAR_FIRST) + near_units(1, (0, 1)) + near_units(-1, (0, 1)) + near_units(2, (0,)) + near_units(-2, (1,))
+    shapes = [(group, len(FAR_FIRST)), (group,), (group,), (lines,), (lines,)]
+    far_first, *near_parts = scale_columns(units, block_order, jacobian, weight, shapes)
+    weight = after(weight, far_first)
+    near_parts = [up(part, step) for part, step in zip(near_parts, (1, -1, 2, -2))]
+    units = far_units(FAR_THEN) + near_units(0, (0, 1))
+    far_then, stay = scale_columns(units, block_order, jacobian, weight, [(group, len(FAR_THEN)), (group,)])
+
     unit = (rows, WIDTH)
-    parts = [(0, 0, 4, 0), (0, 4, 4, 0), (1, 0, 4, 1), (1, 4, 4, 1), (2, 0, 4, 2), (3, 4, 4, 2), (4, 0, 4, 3), (4, 4, 4, 3)]
+    whole, half = pl.ds(0, group), [pl.ds(0, lines), pl.ds(lines, lines)]
+
+    def parted(far, steps):
+        sent = [k for k, s in enumerate(steps) if s]
+        copies = [(0, (h, k), (lines, *unit), q, h) for q, k in enumerate(sent) for h in half]
+        parts = copy_parts([far], [(group, *unit)] * len(sent), copies, "part_far")
+        return [away(part, steps[k]) for part, k in zip(parts, sent)]
+
+    far_first = spread(far_first, ("c", "x"))
+    far_parts = parted(far_first, FAR_FIRST)
+    far_then = after(far_then, far_first, *near_parts, far_wanted)
+    far_then = spread(far_then, ("c", "x"))
+    far_parts += parted(far_then, FAR_THEN)
+
+    pieces = [(0, 0, 4, 0), (0, 4, 4, 0), (1, 0, 4, 1), (1, 4, 4, 1), (2, 0, 4, 2), (3, 4, 4, 2), (4, 0, 4, 3), (4, 4, 4, 3)]
+    near_parts.append(stay)
     (near,) = copy_parts(
         near_parts,
         [(group, 4, *unit)],
         [
             (a, pl.ds(first if near_parts[a].shape[0] == group else 0, n), (n, *unit), 0, (pl.ds(first, n), slot))
-            for a, first, n, slot in parts
+            for a, first, n, slot in pieces
         ],
         "join_near",
     )
+    near = after(near, far_then, far_parts[0])
     near = spread(near, ("c", "x")).reshape(group * 4, *unit)
-    sent = [k for k, s in enumerate(FAR_STEPS) if s]
-    far_parts = copy_parts(
-        [far],
-        [(group, *unit)] * len(sent),
-        [(0, (h, k), (lines, *unit), q, h) for q, k in enumerate(sent) for h in half],
-        "part_far",
-    )
-    far_parts = [away(part, FAR_STEPS[k]) for part, k in zip(far_parts, sent)]
-    far_pieces = [(q, whole) for q in range(len(sent))] + [(len(sent), (whole, FAR_STEPS.index(0)))]
+
+    far_pieces = [(q, whole) for q in range(len(far_parts))] + [(len(far_parts), (whole, FAR_FIRST.index(0)))]
+    far_tiles = list(gram_tiles([*far_parts, far_first], far_pieces, far_wanted[:-1], far_wanted[-1:], True))
+    near = after(near, far_tiles[1])
+    for k in range(1, quarters):
+        far_tiles[k] = lax.ppermute(far_tiles[k], "y", [(b, (b + k) % quarters) for b in range(quarters)])
+    near = after(near, far_tiles[1])
+    far_sum = away(sum_tiles(far_tiles, True), -FAR)
     near_pieces = [(0, pl.ds(8 * q, 8)) for q in range(4)]
-
-    far_tiles = gram_tiles([*far_parts, far], far_pieces, far_wanted[:-1], far_wanted[-1:])
-    far_sum = sum_tiles([spread(far_tiles, "y")], True)
-    near_tiles = gram_tiles([near], near_pieces, wanted[:-1], wanted[-1:])
-    return sum_tiles([spread(near_tiles, "y"), away(far_sum, -FAR)], False)
+    (near_tiles,) = gram_tiles([near], near_pieces, wanted[:-1], wanted[-1:], False)
+    near_tiles = after(near_tiles, *far_tiles[1:])
+    return sum_tiles([spread(near_tiles, "y"), far_sum], False)
 
 
 def solution(mesh):

time: 214 us -> 209 us (0.977)
  waiting for transfers between devices: 115 us -> 106 us
  starting transfers between devices: 41.4 us -> 48.8 us
    ppermute x4, waiting for transfers between devices: 41.2 us -> 0.01 us  [up(): lax.ppermute(value, 'z', [(b, (b + step) % planes) for b in range(planes)])]
    ppermute x5, waiting for transfers between devices: 40.5 us -> 56.7 us  [away(): return lax.ppermute(value, ('z', 'c'), moves)]
    all_to_all x4, waiting for transfers between devices: 33.2 us -> 42 us  [spread(): return lax.all_to_all(value, axes, split_axis=0, concat_axis=0, tiled=True)]
    all_to_all x4, starting transfers between devices: 20.7 us -> 29 us  [spread(): return lax.all_to_all(value, axes, split_axis=0, concat_axis=0, tiled=True)]
    ppermute x0 -> x3, waiting for transfers between devices: none -> 7.22 us  [body(): lax.ppermute(far_tiles[k], 'y', [(b, (b + k) % quarters) for b in range(q...]
    ppermute x5, starting transfers between devices: 12.4 us -> 5.72 us  [away(): return lax.ppermute(value, ('z', 'c'), moves)]
    ppermute x0 -> x3, starting transfers between devices: none -> 5.9 us  [body(): lax.ppermute(far_tiles[k], 'y', [(b, (b + k) % quarters) for b in range(q...]
    pallas_call x2, Pallas kernels: 25.2 us -> 20 us  [gram_tiles(): pl.pallas_call(kernel, out_shape=[jax.ShapeDtypeStruct((n, quarter * BLOC...]
  transfers between devices with their start and end apart: 13 -> 16, of which waited for: 7 -> 9; matrix products, arithmetic and copies ran while one was open for 1% -> 1% of each run, Pallas kernels for 16% -> 18%
where the time goes in v5:
time: 209 us; the launch traced here: 208 us
  waiting for transfers between devices  106 us (51%)
  starting transfers between devices  48.8 us (23%)
  Pallas kernels  48.4 us (23%)
  local copies, waits for them, and re-layouts  4.13 us (2%)
    ppermute x5, waiting for transfers between devices, away(): return lax.ppermute(value, ('z', 'c'), moves)  56.7 us
    all_to_all x4, waiting for transfers between devices, spread(): return lax.all_to_all(value, axes, split_axis=0, concat_axis=0, tiled=True)  42 us
    all_to_all x4, starting transfers between devices, spread(): return lax.all_to_all(value, axes, split_axis=0, concat_axis=0, tiled=True)  29 us
    pallas_call x2, Pallas kernels, gram_tiles(): pl.pallas_call(kernel, out_shape=[jax.ShapeDtypeStruct((n, quarter * BLOC...  20 us
    pallas_call x2, Pallas kernels, scale_columns(): pl.pallas_call(kernel, out_shape=[jax.ShapeDtypeStruct((size, rows, WIDTH...  13.8 us
    ppermute x4, starting transfers between devices, up(): lax.ppermute(value, 'z', [(b, (b + step) % planes) for b in range(planes)])  8.26 us
    pallas_call x3, Pallas kernels, copy_parts(): pl.pallas_call(kernel, out_shape=[jax.ShapeDtypeStruct(shape, arrays[0].d...  8.11 us
    ppermute x3, waiting for transfers between devices, body(): lax.ppermute(far_tiles[k], 'y', [(b, (b + k) % quarters) for b in range(q...  7.22 us
  transfers between devices with their start and end apart: 16, of which 9 were waited for; matrix products, arithmetic and copies ran while one was open for 1% of the time, Pallas kernels for 18%

profile of v5, /device:TPU:2, one launch (start us, length us, event | category | flops | bytes accessed | tf_op | source)
XLA Modules:
  0.0 208.2 jit_solution(17047693895785454066)
XLA Ops:
  0.0 7.5 %scale_columns.2 = (bf16[24,64,1024]{2,1,0:T(8,128)(2,1)}, bf16[8,64,1024]{2,1,0:T(8,128)(2,1)}, bf16[8,64,1024]{2,1,0:T(8,128)(2,1)}, bf16[4,64,1024]{2,1,0:T(8,128)(2,1)}, bf16[4,64,1024]{2,1,0:T(8,128)(2,1)}) custom-call(s32[48]{0:T(128)} %constant.4.clone.units_ref, s32[512]{0:T(512)} %order_ref.3, bf16[64,65536]{1,0:T(8,128)(2,1)} %jac_ref.3, ...), custom_call_target="tpu_custom_call" | custom-call | flops 3145728 | bytes 14680064 | tf_op jit(solution)/shard_map/scale_columns/pallas_call | solution.py:71
  7.5 0.0 copy-start.8
  7.5 6.6 %all-to-all-start = ((bf16[8,3,64,1024]{3,2,1,0:T(8,128)(2,1)}), bf16[8,3,64,1024]{3,2,1,0:T(8,128)(2,1)}, u32[]{:S(2)}, u32[]{:S(2)}) async-start(bf16[8,3,64,1024]{3,2,1,0:T(8,128)(2,1)} %bitcast.4), calls=%async_computation | async-start | bytes 6291456 | tf_op jit(solution)/shard_map/all_to_all | solution.py:314
  14.1 0.2 collective-permute-start
  14.3 3.9 %collective-permute-start.1 = (bf16[8,64,1024]{2,1,0:T(8,128)(2,1)}, bf16[8,64,1024]{2,1,0:T(8,128)(2,1)}, u32[]{:S(2)}, u32[]{:S(2)}) collective-permute-start(bf16[8,64,1024]{2,1,0:T(8,128)(2,1)} %get-tuple-element.25), channel_id=1, source_target_pairs={{0,56},{8,0},{16,8},{24,16},{32,24},{40,32},{48,40},{56,48},{1,57}... | collective-permute-start | bytes 3145736 | tf_op jit(solution)/shard_map/ppermute | solution.py:307
  18.2 0.0 collective-permute-start.2
  18.3 4.1 %collective-permute-start.3 = (bf16[4,64,1024]{2,1,0:T(8,128)(2,1)}, bf16[4,64,1024]{2,1,0:T(8,128)(2,1)}, u32[]{:S(2)}, u32[]{:S(2)}) collective-permute-start(bf16[4,64,1024]{2,1,0:T(8,128)(2,1)} %get-tuple-element.27), channel_id=1, source_target_pairs={{0,48},{8,56},{16,0},{24,8},{32,16},{40,24},{48,32},{56,40},{1,49}... | collective-permute-start | bytes 1572872 | tf_op jit(solution)/shard_map/ppermute | solution.py:307
  23.0 0.1 copy.9
  23.1 0.1 reshape.15.pairs_ref
  23.3 0.8 collective-permute-start.4
  24.1 26.7 %all-to-all-done.refs_0_.refs_3_ = bf16[8,3,64,1024]{3,2,1,0:T(8,128)(2,1)} async-done(((bf16[8,3,64,1024]{3,2,1,0:T(8,128)(2,1)}), bf16[8,3,64,1024]{3,2,1,0:T(8,128)(2,1)}, u32[]{:S(2)}, u32[]{:S(2)}) %all-to-all-start) | async-done | bytes 3145760 | tf_op jit(solution)/shard_map/all_to_all | solution.py:314
  50.8 2.5 %part_far.2 = (bf16[8,64,1024]{2,1,0:T(8,128)(2,1)}, bf16[8,64,1024]{2,1,0:T(8,128)(2,1)}) custom-call(bf16[8,3,64,1024]{3,2,1,0:T(8,128)(2,1)} %all-to-all-done.refs_0_.refs_3_), custom_call_target="tpu_custom_call" | custom-call | bytes 4194304 | tf_op jit(solution)/shard_map/part_far/pallas_call | solution.py:117
  53.2 12.8 %collective-permute-done.4 = s32[129]{0:T(256)S(1)} collective-permute-done((s32[129]{0:T(256)S(1)}, s32[129]{0:T(256)S(1)}, u32[]{:S(2)}, u32[]{:S(2)}) %collective-permute-start.4) | collective-permute-done | bytes 548 | tf_op jit(solution)/shard_map/ppermute | solution.py:311
  66.0 2.7 %collective-permute-start.5 = (bf16[8,64,1024]{2,1,0:T(8,128)(2,1)}, bf16[8,64,1024]{2,1,0:T(8,128)(2,1)}, u32[]{:S(2)}, u32[]{:S(2)}) collective-permute-start(bf16[8,64,1024]{2,1,0:T(8,128)(2,1)} %get-tuple-element.33), channel_id=1, source_target_pairs={{0,48},{4,20},{8,56},{12,28},{16,0},{20,36},{24,8},{28,44},{32,16}... | collective-permute-start | bytes 3145736 | tf_op jit(solution)/shard_map/ppermute | solution.py:311
  68.7 6.3 %scale_columns.3 = (bf16[8,64,1024]{2,1,0:T(8,128)(2,1)}, bf16[8,64,1024]{2,1,0:T(8,128)(2,1)}) custom-call(s32[16]{0:T(128)} %constant.5.clone.units_ref, s32[512]{0:T(512)} %order_ref.3, bf16[64,65536]{1,0:T(8,128)(2,1)} %jac_ref.3, f32[1,64]{1,0:T(1,128)} %bitcast.7), custom_call_target="tpu_custom_call" | custom-call | flops 1048576 | bytes 10485760 | tf_op jit(solution)/shard_map/scale_columns/pallas_call | solution.py:71
  75.1 0.0 collective-permute-done.2.refs_2_
  75.1 0.0 collective-permute-done.3.refs_3_
  75.1 0.0 collective-permute-done.refs_0_
  75.1 0.0 copy-start.1
  75.1 0.0 collective-permute-done.1.refs_1_
  75.1 1.0 copy-done.1
  76.1 4.8 %all-to-all-start.1 = ((bf16[8,1,64,1024]{3,2,1,0:T(8,128)(2,1)}), bf16[8,1,64,1024]{3,2,1,0:T(8,128)(2,1)S(1)}, u32[]{:S(2)}, u32[]{:S(2)}) async-start(bf16[8,1,64,1024]{3,2,1,0:T(8,128)(2,1)} %bitcast.5), calls=%async_computation.1 | async-start | bytes 2097152 | tf_op jit(solution)/shard_map/all_to_all | solution.py:314
  80.9 3.6 %join_near.1 = bf16[8,4,64,1024]{3,2,1,0:T(8,128)(2,1)} custom-call(bf16[8,64,1024]{2,1,0:T(8,128)(2,1)} %copy-done.1, bf16[8,64,1024]{2,1,0:T(8,128)(2,1)} %collective-permute-done.1.refs_1_, bf16[4,64,1024]{2,1,0:T(8,128)(2,1)} %copy-done.6, bf16[4,64,1024]{2,1,0:T(8,128)(2,1)} %collective-permute-done.3.refs_3_, ...), custom_call_target="tpu_custom_call" | custom-call | bytes 8388608 | tf_op jit(solution)/shard_map/join_near/pallas_call | solution.py:117
  84.5 10.4 %all-to-all-done.1.refs_0_ = bf16[8,1,64,1024]{3,2,1,0:T(8,128)(2,1)S(1)} async-done(((bf16[8,1,64,1024]{3,2,1,0:T(8,128)(2,1)}), bf16[8,1,64,1024]{3,2,1,0:T(8,128)(2,1)S(1)}, u32[]{:S(2)}, u32[]{:S(2)}) %all-to-all-start.1) | async-done | bytes 1048608 | tf_op jit(solution)/shard_map/all_to_all | solution.py:314
  95.0 0.0 collective-permute-done.5.refs_0_
  95.0 1.0 copy-done
  95.9 5.8 %all-to-all-start.2 = ((bf16[8,4,64,1024]{3,2,1,0:T(8,128)(2,1)}), bf16[8,4,64,1024]{3,2,1,0:T(8,128)(2,1)}, u32[]{:S(2)}, u32[]{:S(2)}) async-start(bf16[8,4,64,1024]{3,2,1,0:T(8,128)(2,1)} %join_near.1), calls=%async_computation.2 | async-start | bytes 8388608 | tf_op jit(solution)/shard_map/all_to_all | solution.py:314
  101.7 1.0 collective-permute-start.6
  102.7 2.1 part_far.3
  104.8 1.3 collective-permute-start.7
  106.0 0.5 slice.7.count_ref
  106.6 0.6 slice.6.pairs_ref
  107.1 19.2 %collective-permute-done.6.refs_1_ = bf16[8,64,1024]{2,1,0:T(8,128)(2,1)S(1)} collective-permute-done((bf16[8,64,1024]{2,1,0:T(8,128)(2,1)}, bf16[8,64,1024]{2,1,0:T(8,128)(2,1)S(1)}, u32[]{:S(2)}, u32[]{:S(2)}) %collective-permute-start.6) | collective-permute-done | bytes 1048608 | tf_op jit(solution)/shard_map/ppermute | solution.py:311
  126.3 2.1 %collective-permute-done.7.refs_2_ = bf16[8,64,1024]{2,1,0:T(8,128)(2,1)} collective-permute-done((bf16[8,64,1024]{2,1,0:T(8,128)(2,1)}, bf16[8,64,1024]{2,1,0:T(8,128)(2,1)}, u32[]{:S(2)}, u32[]{:S(2)}) %collective-permute-start.7) | collective-permute-done | bytes 1048608 | tf_op jit(solution)/shard_map/ppermute | solution.py:311
  128.4 10.3 %gram_tiles.2 = (s16[1,2064,128]{2,1,0:T(8,128)(2,1)}, s16[1,2064,128]{2,1,0:T(8,128)(2,1)}, s16[1,2064,128]{2,1,0:T(8,128)(2,1)}, s16[1,2064,128]{2,1,0:T(8,128)(2,1)}) custom-call(s32[128]{0:T(128)} %slice.6.pairs_ref, s32[1]{0:T(128)} %slice.7.count_ref, bf16[8,64,1024]{2,1,0:T(8,128)(2,1)} %collective-permute-done.5.refs_0_, ...), custom_call_target="tpu_custom_call" | custom-call | flops 4294967296 | bytes 6291456 | tf_op jit(solution)/shard_map/gram_tiles/pallas_call | solution.py:203
  138.8 1.7 collective-permute-start.8
  140.4 2.9 %collective-permute-start.9 = (s16[1,2064,128]{2,1,0:T(8,128)(2,1)}, s16[1,2064,128]{2,1,0:T(8,128)(2,1)S(1)}, u32[]{:S(2)}, u32[]{:S(2)}) collective-permute-start(s16[1,2064,128]{2,1,0:T(8,128)(2,1)} %get-tuple-element.39), channel_id=1, source_target_pairs={{0,2},{1,3},{2,0},{3,1},{4,6},{5,7},{6,4},{7,5},{8,10},{9,11},{10,... | collective-permute-start | bytes 1585160 | tf_op jit(solution)/shard_map/ppermute | solution.py:363
  143.3 1.3 collective-permute-start.10
  144.7 4.9 %all-to-all-done.2 = bf16[8,4,64,1024]{3,2,1,0:T(8,128)(2,1)} async-done(((bf16[8,4,64,1024]{3,2,1,0:T(8,128)(2,1)}), bf16[8,4,64,1024]{3,2,1,0:T(8,128)(2,1)}, u32[]{:S(2)}, u32[]{:S(2)}) %all-to-all-start.2) | async-done | bytes 4194336 | tf_op jit(solution)/shard_map/all_to_all | solution.py:314
  149.6 4.5 %collective-permute-done.8.refs_1_ = s16[1,2064,128]{2,1,0:T(8,128)(2,1)S(1)} collective-permute-done((s16[1,2064,128]{2,1,0:T(8,128)(2,1)}, s16[1,2064,128]{2,1,0:T(8,128)(2,1)S(1)}, u32[]{:S(2)}, u32[]{:S(2)}) %collective-permute-start.8) | collective-permute-done | bytes 528416 | tf_op jit(solution)/shard_map/ppermute | solution.py:363
  154.1 9.7 %gram_tiles.3 = s16[4,2064,128]{2,1,0:T(8,128)(2,1)} custom-call(s32[128]{0:T(128)} %copy-done.7, s32[1]{0:T(128)S(6)} %copy.10.count_ref, bf16[32,64,1024]{2,1,0:T(8,128)(2,1)} %bitcast.3.refs_0_), custom_call_target="tpu_custom_call" | custom-call | flops 4294967296 | bytes 6291456 | tf_op jit(solution)/shard_map/gram_tiles/pallas_call | solution.py:203
  163.7 2.7 %collective-permute-done.9.refs_2_ = s16[1,2064,128]{2,1,0:T(8,128)(2,1)S(1)} collective-permute-done((s16[1,2064,128]{2,1,0:T(8,128)(2,1)}, s16[1,2064,128]{2,1,0:T(8,128)(2,1)S(1)}, u32[]{:S(2)}, u32[]{:S(2)}) %collective-permute-start.9) | collective-permute-done | bytes 528416 | tf_op jit(solution)/shard_map/ppermute | solution.py:363
  166.5 11.7 %all-to-all-start.3 = ((s16[4,2064,128]{2,1,0:T(8,128)(2,1)}), s16[4,2064,128]{2,1,0:T(8,128)(2,1)}, u32[]{:S(2)}, u32[]{:S(2)}) async-start(s16[4,2064,128]{2,1,0:T(8,128)(2,1)} %gram_tiles.3), calls=%async_computation.3 | async-start | bytes 4227072 | tf_op jit(solution)/shard_map/all_to_all | solution.py:314
  178.2 3.2 %sum_tiles.2 = s16[1,2064,128]{2,1,0:T(8,128)(2,1)} custom-call(s16[1,2064,128]{2,1,0:T(8,128)(2,1)} %get-tuple-element.42.refs_0_, s16[1,2064,128]{2,1,0:T(8,128)(2,1)} %copy-done.2, s16[1,2064,128]{2,1,0:T(8,128)(2,1)} %copy-done.3, s16[1,2064,128]{2,1,0:T(8,128)(2,1)} %copy-done.4), custom_call_target="tpu_custom_call" | custom-call | flops 4227072 | bytes 3170304 | tf_op jit(solution)/shard_map/sum_tiles/pallas_call | solution.py:274
  181.4 22.6 %collective-permute-done.11.refs_1_ = s16[1,2064,128]{2,1,0:T(8,128)(2,1)S(1)} collective-permute-done((s16[1,2064,128]{2,1,0:T(8,128)(2,1)}, s16[1,2064,128]{2,1,0:T(8,128)(2,1)S(1)}, u32[]{:S(2)}, u32[]{:S(2)}) %collective-permute-start.11) | collective-permute-done | bytes 528416 | tf_op jit(solution)/shard_map/ppermute | solution.py:311
  204.0 0.0 all-to-all-done.3.refs_0_
  204.0 0.8 copy-done.5
  204.9 3.4 %sum_tiles.3 = f32[16,128,128]{2,1,0:T(8,128)} custom-call(s16[4,2064,128]{2,1,0:T(8,128)(2,1)} %all-to-all-done.3.refs_0_, s16[1,2064,128]{2,1,0:T(8,128)(2,1)} %copy-done.5), custom_call_target="tpu_custom_call" | custom-call | flops 5283840 | bytes 3698688 | tf_op jit(solution)/shard_map/sum_tiles/pallas_call | solution.py:274
  (18 shorter events, 0.0 us)
Async XLA Ops:
  7.5 15.6 %copy-start.8 = (s32[1,64,2]{1,2,0:T(2,128)S(1)}, s32[1,64,2]{1,2,0:T(2,128)}, u32[]{:S(2)}) copy-start(s32[1,64,2]{1,2,0:T(2,128)} %param.10) | copy-start | bytes 1540
  7.5 43.3 %all-to-all-start = ((bf16[8,3,64,1024]{3,2,1,0:T(8,128)(2,1)}), bf16[8,3,64,1024]{3,2,1,0:T(8,128)(2,1)}, u32[]{:S(2)}, u32[]{:S(2)}) async-start(bf16[8,3,64,1024]{3,2,1,0:T(8,128)(2,1)} %bitcast.4), calls=%async_computation | async-start | bytes 6291456 | tf_op jit(solution)/shard_map/all_to_all | solution.py:314
  14.1 61.0 %collective-permute-start = (bf16[8,64,1024]{2,1,0:T(8,128)(2,1)}, bf16[8,64,1024]{2,1,0:T(8,128)(2,1)S(1)}, u32[]{:S(2)}, u32[]{:S(2)}) collective-permute-start(bf16[8,64,1024]{2,1,0:T(8,128)(2,1)} %get-tuple-element.24), channel_id=1, source_target_pairs={{0,8},{8,16},{16,24},{24,32},{32,40},{40,48},{48,56},{56,0},{1,9},... | collective-permute-start | bytes 3145736 | tf_op jit(solution)/shard_map/ppermute | solution.py:307
  14.3 60.8 %collective-permute-start.1 = (bf16[8,64,1024]{2,1,0:T(8,128)(2,1)}, bf16[8,64,1024]{2,1,0:T(8,128)(2,1)}, u32[]{:S(2)}, u32[]{:S(2)}) collective-permute-start(bf16[8,64,1024]{2,1,0:T(8,128)(2,1)} %get-tuple-element.25), channel_id=1, source_target_pairs={{0,56},{8,0},{16,8},{24,16},{32,24},{40,32},{48,40},{56,48},{1,57}... | collective-permute-start | bytes 3145736 | tf_op jit(solution)/shard_map/ppermute | solution.py:307
  18.2 56.8 %collective-permute-start.2 = (bf16[4,64,1024]{2,1,0:T(8,128)(2,1)}, bf16[4,64,1024]{2,1,0:T(8,128)(2,1)S(1)}, u32[]{:S(2)}, u32[]{:S(2)}) collective-permute-start(bf16[4,64,1024]{2,1,0:T(8,128)(2,1)} %get-tuple-element.26), channel_id=1, source_target_pairs={{0,16},{8,24},{16,32},{24,40},{32,48},{40,56},{48,0},{56,8},{1,17}... | collective-permute-start | bytes 1572872 | tf_op jit(solution)/shard_map/ppermute | solution.py:307
  18.3 56.8 %collective-permute-start.3 = (bf16[4,64,1024]{2,1,0:T(8,128)(2,1)}, bf16[4,64,1024]{2,1,0:T(8,128)(2,1)}, u32[]{:S(2)}, u32[]{:S(2)}) collective-permute-start(bf16[4,64,1024]{2,1,0:T(8,128)(2,1)} %get-tuple-element.27), channel_id=1, source_target_pairs={{0,48},{8,56},{16,0},{24,8},{32,16},{40,24},{48,32},{56,40},{1,49}... | collective-permute-start | bytes 1572872 | tf_op jit(solution)/shard_map/ppermute | solution.py:307
  23.3 51.8 %copy-start.7 = (s32[128]{0:T(128)}, s32[128]{0:T(128)S(1)}, u32[]{:S(2)}) copy-start(s32[128]{0:T(128)S(1)} %reshape.15.pairs_ref) | copy-start | bytes 1540
  23.3 42.7 %collective-permute-start.4 = (s32[129]{0:T(256)S(1)}, s32[129]{0:T(256)S(1)}, u32[]{:S(2)}, u32[]{:S(2)}) collective-permute-start(s32[129]{0:T(256)S(1)} %pad_add_fusion), channel_id=1, source_target_pairs={{0,24},{4,44},{8,32},{12,52},{16,40},{20,60},{24,48},{28,4},{32,56... | collective-permute-start | bytes 1556 | tf_op jit(solution)/shard_map/ppermute | solution.py:311
  66.0 28.9 %collective-permute-start.5 = (bf16[8,64,1024]{2,1,0:T(8,128)(2,1)}, bf16[8,64,1024]{2,1,0:T(8,128)(2,1)}, u32[]{:S(2)}, u32[]{:S(2)}) collective-permute-start(bf16[8,64,1024]{2,1,0:T(8,128)(2,1)} %get-tuple-element.33), channel_id=1, source_target_pairs={{0,48},{4,20},{8,56},{12,28},{16,0},{20,36},{24,8},{28,44},{32,16}... | collective-permute-start | bytes 3145736 | tf_op jit(solution)/shard_map/ppermute | solution.py:311
  75.1 5.9 %copy-start.6 = (bf16[4,64,1024]{2,1,0:T(8,128)(2,1)}, bf16[4,64,1024]{2,1,0:T(8,128)(2,1)S(1)}, u32[]{:S(2)}) copy-start(bf16[4,64,1024]{2,1,0:T(8,128)(2,1)S(1)} %collective-permute-done.2.refs_2_) | copy-start | bytes 1572868
  75.1 1.0 copy-start.1
  76.1 18.8 %all-to-all-start.1 = ((bf16[8,1,64,1024]{3,2,1,0:T(8,128)(2,1)}), bf16[8,1,64,1024]{3,2,1,0:T(8,128)(2,1)S(1)}, u32[]{:S(2)}, u32[]{:S(2)}) async-start(bf16[8,1,64,1024]{3,2,1,0:T(8,128)(2,1)} %bitcast.5), calls=%async_computation.1 | async-start | bytes 2097152 | tf_op jit(solution)/shard_map/all_to_all | solution.py:314
  95.0 1.0 copy-start
  95.9 53.6 %all-to-all-start.2 = ((bf16[8,4,64,1024]{3,2,1,0:T(8,128)(2,1)}), bf16[8,4,64,1024]{3,2,1,0:T(8,128)(2,1)}, u32[]{:S(2)}, u32[]{:S(2)}) async-start(bf16[8,4,64,1024]{3,2,1,0:T(8,128)(2,1)} %join_near.1), calls=%async_computation.2 | async-start | bytes 8388608 | tf_op jit(solution)/shard_map/all_to_all | solution.py:314
  101.7 24.6 %collective-permute-start.6 = (bf16[8,64,1024]{2,1,0:T(8,128)(2,1)}, bf16[8,64,1024]{2,1,0:T(8,128)(2,1)S(1)}, u32[]{:S(2)}, u32[]{:S(2)}) collective-permute-start(bf16[8,64,1024]{2,1,0:T(8,128)(2,1)} %get-tuple-element.35), channel_id=1, source_target_pairs={{0,56},{4,12},{8,0},{12,20},{16,8},{20,28},{24,16},{28,36},{32,24}... | collective-permute-start | bytes 3145736 | tf_op jit(solution)/shard_map/ppermute | solution.py:311
  104.8 23.7 %collective-permute-start.7 = (bf16[8,64,1024]{2,1,0:T(8,128)(2,1)}, bf16[8,64,1024]{2,1,0:T(8,128)(2,1)}, u32[]{:S(2)}, u32[]{:S(2)}) collective-permute-start(bf16[8,64,1024]{2,1,0:T(8,128)(2,1)} %part_far.3), channel_id=1, source_target_pairs={{0,8},{4,60},{8,16},{12,4},{16,24},{20,12},{24,32},{28,20},{32,40}... | collective-permute-start | bytes 3145736 | tf_op jit(solution)/shard_map/ppermute | solution.py:311
  126.3 2.1 %copy-start.9 = (bf16[8,64,1024]{2,1,0:T(8,128)(2,1)}, bf16[8,64,1024]{2,1,0:T(8,128)(2,1)S(1)}, u32[]{:S(2)}) copy-start(bf16[8,64,1024]{2,1,0:T(8,128)(2,1)S(1)} %collective-permute-done.6.refs_1_) | copy-start | bytes 3145732
  138.8 15.3 %collective-permute-start.8 = (s16[1,2064,128]{2,1,0:T(8,128)(2,1)}, s16[1,2064,128]{2,1,0:T(8,128)(2,1)S(1)}, u32[]{:S(2)}, u32[]{:S(2)}) collective-permute-start(s16[1,2064,128]{2,1,0:T(8,128)(2,1)} %get-tuple-element.36), channel_id=1, source_target_pairs={{0,1},{1,2},{2,3},{3,0},{4,5},{5,6},{6,7},{7,4},{8,9},{9,10},{10,1... | collective-permute-start | bytes 1585160 | tf_op jit(solution)/shard_map/ppermute | solution.py:363
  140.4 26.0 %collective-permute-start.9 = (s16[1,2064,128]{2,1,0:T(8,128)(2,1)}, s16[1,2064,128]{2,1,0:T(8,128)(2,1)S(1)}, u32[]{:S(2)}, u32[]{:S(2)}) collective-permute-start(s16[1,2064,128]{2,1,0:T(8,128)(2,1)} %get-tuple-element.39), channel_id=1, source_target_pairs={{0,2},{1,3},{2,0},{3,1},{4,6},{5,7},{6,4},{7,5},{8,10},{9,11},{10,... | collective-permute-start | bytes 1585160 | tf_op jit(solution)/shard_map/ppermute | solution.py:363
  143.3 23.1 %collective-permute-start.10 = (s16[1,2064,128]{2,1,0:T(8,128)(2,1)}, s16[1,2064,128]{2,1,0:T(8,128)(2,1)S(1)}, u32[]{:S(2)}, u32[]{:S(2)}) collective-permute-start(s16[1,2064,128]{2,1,0:T(8,128)(2,1)} %get-tuple-element.40), channel_id=1, source_target_pairs={{0,3},{1,0},{2,1},{3,2},{4,7},{5,4},{6,5},{7,6},{8,11},{9,8},{10,9... | collective-permute-start | bytes 1585160 | tf_op jit(solution)/shard_map/ppermute | solution.py:363
  154.1 9.7 %copy-start.2 = (s16[1,2064,128]{2,1,0:T(8,128)(2,1)}, s16[1,2064,128]{2,1,0:T(8,128)(2,1)S(1)}, u32[]{:S(2)}) copy-start(s16[1,2064,128]{2,1,0:T(8,128)(2,1)S(1)} %collective-permute-done.8.refs_1_) | copy-start | bytes 1585156
  166.5 11.8 %copy-start.3 = (s16[1,2064,128]{2,1,0:T(8,128)(2,1)}, s16[1,2064,128]{2,1,0:T(8,128)(2,1)S(1)}, u32[]{:S(2)}) copy-start(s16[1,2064,128]{2,1,0:T(8,128)(2,1)S(1)} %collective-permute-done.9.refs_2_) | copy-start | bytes 1585156
  166.5 11.8 %copy-start.4 = (s16[1,2064,128]{2,1,0:T(8,128)(2,1)}, s16[1,2064,128]{2,1,0:T(8,128)(2,1)S(1)}, u32[]{:S(2)}) copy-start(s16[1,2064,128]{2,1,0:T(8,128)(2,1)S(1)} %collective-permute-done.10.refs_3_) | copy-start | bytes 1585156
  166.5 37.6 %all-to-all-start.3 = ((s16[4,2064,128]{2,1,0:T(8,128)(2,1)}), s16[4,2064,128]{2,1,0:T(8,128)(2,1)}, u32[]{:S(2)}, u32[]{:S(2)}) async-start(s16[4,2064,128]{2,1,0:T(8,128)(2,1)} %gram_tiles.3), calls=%async_computation.3 | async-start | bytes 4227072 | tf_op jit(solution)/shard_map/all_to_all | solution.py:314
  181.4 22.6 %collective-permute-start.11 = (s16[1,2064,128]{2,1,0:T(8,128)(2,1)}, s16[1,2064,128]{2,1,0:T(8,128)(2,1)S(1)}, u32[]{:S(2)}, u32[]{:S(2)}) collective-permute-start(s16[1,2064,128]{2,1,0:T(8,128)(2,1)} %sum_tiles.2), channel_id=1, source_target_pairs={{0,40},{4,28},{8,48},{12,36},{16,56},{20,44},{24,0},{28,52},{32,8}... | collective-permute-start | bytes 1585160 | tf_op jit(solution)/shard_map/ppermute | solution.py:311
  204.0 0.8 copy-start.5

commit v6 on v5

--- a/solution.py
+++ b/solution.py
@@ -337,8 +337,9 @@
         return [away(part, steps[k]) for part, k in zip(parts, sent)]
 
     far_first = spread(far_first, ("c", "x"))
+    far_first = after(far_first, stay)
     far_parts = parted(far_first, FAR_FIRST)
-    far_then = after(far_then, far_first, *near_parts, far_wanted)
+    far_then = after(far_then, far_first, *near_parts)
     far_then = spread(far_then, ("c", "x"))
     far_parts += parted(far_then, FAR_THEN)
 
@@ -353,7 +354,7 @@
         ],
         "join_near",
     )
-    near = after(near, far_then, far_parts[0])
+    near = after(near, far_then, far_parts[0], far_wanted)
     near = spread(near, ("c", "x")).reshape(group * 4, *unit)
 
     far_pieces = [(q, whole) for q in range(len(far_parts))] + [(len(far_parts), (whole, FAR_FIRST.index(0)))]
@@ -361,7 +362,6 @@
     near = after(near, far_tiles[1])
     for k in range(1, quarters):
         far_tiles[k] = lax.ppermute(far_tiles[k], "y", [(b, (b + k) % quarters) for b in range(quarters)])
-    near = after(near, far_tiles[1])
     far_sum = away(sum_tiles(far_tiles, True), -FAR)
     near_pieces = [(0, pl.ds(8 * q, 8)) for q in range(4)]
     (near_tiles,) = gram_tiles([near], near_pieces, wanted[:-1], wanted[-1:], False)

time: 209 us -> 199 us (0.952); the launches traced: 208 us -> 196 us
  waiting for transfers between devices: 106 us -> 86.7 us
  starting transfers between devices: 48.8 us -> 56.6 us
    ppermute x5, waiting for transfers between devices: 56.7 us -> 39.2 us  [away(): return lax.ppermute(value, ('z', 'c'), moves)]
    ppermute x5, starting transfers between devices: 5.72 us -> 19.5 us  [away(): return lax.ppermute(value, ('z', 'c'), moves)]
    all_to_all x4, waiting for transfers between devices: 42 us -> 33.9 us  [spread(): return lax.all_to_all(value, axes, split_axis=0, concat_axis=0, tiled=True)]
    ppermute x4, waiting for transfers between devices: 0.01 us -> 5.97 us  [up(): lax.ppermute(value, 'z', [(b, (b + step) % planes) for b in range(planes)])]
    all_to_all x4, starting transfers between devices: 29 us -> 23.5 us  [spread(): return lax.all_to_all(value, axes, split_axis=0, concat_axis=0, tiled=True)]
  transfers between devices with their start and end apart: 16 -> 16, of which waited for: 9 -> 10; matrix products, arithmetic and copies ran while one was open for 1% -> 1% of each run, Pallas kernels for 18% -> 19%
where the time goes in v6:
time: 199 us; the launch traced here: 196 us
  waiting for transfers between devices  86.7 us (44%)
  starting transfers between devices  56.6 us (28%)
  Pallas kernels  48.4 us (24%)
  local copies, waits for them, and re-layouts  3.14 us (2%)
    ppermute x5, waiting for transfers between devices, away(): return lax.ppermute(value, ('z', 'c'), moves)  39.2 us
    all_to_all x4, waiting for transfers between devices, spread(): return lax.all_to_all(value, axes, split_axis=0, concat_axis=0, tiled=True)  33.9 us
    all_to_all x4, starting transfers between devices, spread(): return lax.all_to_all(value, axes, split_axis=0, concat_axis=0, tiled=True)  23.5 us
    pallas_call x2, Pallas kernels, gram_tiles(): pl.pallas_call(kernel, out_shape=[jax.ShapeDtypeStruct((n, quarter * BLOC...  20 us
    ppermute x5, starting transfers between devices, away(): return lax.ppermute(value, ('z', 'c'), moves)  19.5 us
    pallas_call x2, Pallas kernels, scale_columns(): pl.pallas_call(kernel, out_shape=[jax.ShapeDtypeStruct((size, rows, WIDTH...  13.7 us
    ppermute x4, starting transfers between devices, up(): lax.ppermute(value, 'z', [(b, (b + step) % planes) for b in range(planes)])  8.26 us
    pallas_call x3, Pallas kernels, copy_parts(): pl.pallas_call(kernel, out_shape=[jax.ShapeDtypeStruct(shape, arrays[0].d...  8.16 us
  transfers between devices with their start and end apart: 16, of which 10 were waited for; matrix products, arithmetic and copies ran while one was open for 1% of the time, Pallas kernels for 19%

profile of v6, /device:TPU:2, one launch (start us, length us, event | category | flops | bytes accessed | tf_op | source)
XLA Modules:
  0.0 195.6 jit_solution(12186545819011066691)
XLA Ops:
  0.0 7.5 %scale_columns.2 = (bf16[24,64,1024]{2,1,0:T(8,128)(2,1)}, bf16[8,64,1024]{2,1,0:T(8,128)(2,1)}, bf16[8,64,1024]{2,1,0:T(8,128)(2,1)}, bf16[4,64,1024]{2,1,0:T(8,128)(2,1)}, bf16[4,64,1024]{2,1,0:T(8,128)(2,1)}) custom-call(s32[48]{0:T(128)} %constant.4.clone.units_ref, s32[512]{0:T(512)} %order_ref.3, bf16[64,65536]{1,0:T(8,128)(2,1)} %jac_ref.3, ...), custom_call_target="tpu_custom_call" | custom-call | flops 3145728 | bytes 14680064 | tf_op jit(solution)/shard_map/scale_columns/pallas_call | solution.py:71
  7.5 6.6 %all-to-all-start = ((bf16[8,3,64,1024]{3,2,1,0:T(8,128)(2,1)}), bf16[8,3,64,1024]{3,2,1,0:T(8,128)(2,1)}, u32[]{:S(2)}, u32[]{:S(2)}) async-start(bf16[8,3,64,1024]{3,2,1,0:T(8,128)(2,1)} %bitcast.4), calls=%async_computation | async-start | bytes 6291456 | tf_op jit(solution)/shard_map/all_to_all | solution.py:314
  14.1 0.2 collective-permute-start
  14.3 3.9 %collective-permute-start.1 = (bf16[8,64,1024]{2,1,0:T(8,128)(2,1)}, bf16[8,64,1024]{2,1,0:T(8,128)(2,1)}, u32[]{:S(2)}, u32[]{:S(2)}) collective-permute-start(bf16[8,64,1024]{2,1,0:T(8,128)(2,1)} %get-tuple-element.25), channel_id=1, source_target_pairs={{0,56},{8,0},{16,8},{24,16},{32,24},{40,32},{48,40},{56,48},{1,57}... | collective-permute-start | bytes 3145736 | tf_op jit(solution)/shard_map/ppermute | solution.py:307
  18.3 0.0 collective-permute-start.2
  18.3 4.1 %collective-permute-start.3 = (bf16[4,64,1024]{2,1,0:T(8,128)(2,1)}, bf16[4,64,1024]{2,1,0:T(8,128)(2,1)}, u32[]{:S(2)}, u32[]{:S(2)}) collective-permute-start(bf16[4,64,1024]{2,1,0:T(8,128)(2,1)} %get-tuple-element.27), channel_id=1, source_target_pairs={{0,48},{8,56},{16,0},{24,8},{32,16},{40,24},{48,32},{56,40},{1,49}... | collective-permute-start | bytes 1572872 | tf_op jit(solution)/shard_map/ppermute | solution.py:307
  22.4 6.3 %scale_columns.3 = (bf16[8,64,1024]{2,1,0:T(8,128)(2,1)}, bf16[8,64,1024]{2,1,0:T(8,128)(2,1)}) custom-call(s32[16]{0:T(128)} %constant.5.clone.units_ref, s32[512]{0:T(512)} %order_ref.3, bf16[64,65536]{1,0:T(8,128)(2,1)} %jac_ref.3, f32[1,64]{1,0:T(1,128)} %bitcast.7), custom_call_target="tpu_custom_call" | custom-call | flops 1048576 | bytes 10485760 | tf_op jit(solution)/shard_map/scale_columns/pallas_call | solution.py:71
  28.7 0.0 copy-start.8
  28.7 22.1 %all-to-all-done.refs_0_.refs_3_ = bf16[8,3,64,1024]{3,2,1,0:T(8,128)(2,1)} async-done(((bf16[8,3,64,1024]{3,2,1,0:T(8,128)(2,1)}), bf16[8,3,64,1024]{3,2,1,0:T(8,128)(2,1)}, u32[]{:S(2)}, u32[]{:S(2)}) %all-to-all-start) | async-done | bytes 3145760 | tf_op jit(solution)/shard_map/all_to_all | solution.py:314
  50.8 2.5 %part_far.2 = (bf16[8,64,1024]{2,1,0:T(8,128)(2,1)}, bf16[8,64,1024]{2,1,0:T(8,128)(2,1)}) custom-call(bf16[8,3,64,1024]{3,2,1,0:T(8,128)(2,1)} %all-to-all-done.refs_0_.refs_3_), custom_call_target="tpu_custom_call" | custom-call | bytes 4194304 | tf_op jit(solution)/shard_map/part_far/pallas_call | solution.py:117
  53.3 4.6 %collective-permute-start.4 = (bf16[8,64,1024]{2,1,0:T(8,128)(2,1)}, bf16[8,64,1024]{2,1,0:T(8,128)(2,1)}, u32[]{:S(2)}, u32[]{:S(2)}) collective-permute-start(bf16[8,64,1024]{2,1,0:T(8,128)(2,1)} %get-tuple-element.34), channel_id=1, source_target_pairs={{0,48},{4,20},{8,56},{12,28},{16,0},{20,36},{24,8},{28,44},{32,16}... | collective-permute-start | bytes 3145736 | tf_op jit(solution)/shard_map/ppermute | solution.py:311
  57.9 0.0 collective-permute-done.2.refs_2_
  57.9 6.0 %collective-permute-done.3.refs_3_ = bf16[4,64,1024]{2,1,0:T(8,128)(2,1)} collective-permute-done((bf16[4,64,1024]{2,1,0:T(8,128)(2,1)}, bf16[4,64,1024]{2,1,0:T(8,128)(2,1)}, u32[]{:S(2)}, u32[]{:S(2)}) %collective-permute-start.3) | collective-permute-done | bytes 524320 | tf_op jit(solution)/shard_map/ppermute | solution.py:307
  63.9 0.0 collective-permute-done.refs_0_
  63.9 0.0 collective-permute-done.1.refs_1_
  63.9 1.0 copy-done.1
  64.9 5.9 %all-to-all-start.1 = ((bf16[8,1,64,1024]{3,2,1,0:T(8,128)(2,1)}), bf16[8,1,64,1024]{3,2,1,0:T(8,128)(2,1)S(1)}, u32[]{:S(2)}, u32[]{:S(2)}) async-start(bf16[8,1,64,1024]{3,2,1,0:T(8,128)(2,1)} %bitcast.5), calls=%async_computation.1 | async-start | bytes 2097152 | tf_op jit(solution)/shard_map/all_to_all | solution.py:314
  71.4 0.1 copy.9
  71.5 0.1 reshape.15.pairs_ref
  71.7 1.6 collective-permute-start.5
  73.3 3.6 %join_near.1 = bf16[8,4,64,1024]{3,2,1,0:T(8,128)(2,1)} custom-call(bf16[8,64,1024]{2,1,0:T(8,128)(2,1)} %copy-done.1, bf16[8,64,1024]{2,1,0:T(8,128)(2,1)} %collective-permute-done.1.refs_1_, bf16[4,64,1024]{2,1,0:T(8,128)(2,1)} %copy-done.6, bf16[4,64,1024]{2,1,0:T(8,128)(2,1)} %collective-permute-done.3.refs_3_, ...), custom_call_target="tpu_custom_call" | custom-call | bytes 8388608 | tf_op jit(solution)/shard_map/join_near/pallas_call | solution.py:117
  76.9 1.5 collective-permute-done.5
  78.4 6.3 %all-to-all-done.1.refs_0_ = bf16[8,1,64,1024]{3,2,1,0:T(8,128)(2,1)S(1)} async-done(((bf16[8,1,64,1024]{3,2,1,0:T(8,128)(2,1)}), bf16[8,1,64,1024]{3,2,1,0:T(8,128)(2,1)S(1)}, u32[]{:S(2)}, u32[]{:S(2)}) %all-to-all-start.1) | async-done | bytes 1048608 | tf_op jit(solution)/shard_map/all_to_all | solution.py:314
  84.8 1.5 collective-permute-done.4.refs_0_
  86.3 6.6 %all-to-all-start.2 = ((bf16[8,4,64,1024]{3,2,1,0:T(8,128)(2,1)}), bf16[8,4,64,1024]{3,2,1,0:T(8,128)(2,1)}, u32[]{:S(2)}, u32[]{:S(2)}) async-start(bf16[8,4,64,1024]{3,2,1,0:T(8,128)(2,1)} %join_near.1), calls=%async_computation.2 | async-start | bytes 8388608 | tf_op jit(solution)/shard_map/all_to_all | solution.py:314
  92.9 2.0 %collective-permute-start.6 = (bf16[8,64,1024]{2,1,0:T(8,128)(2,1)}, bf16[8,64,1024]{2,1,0:T(8,128)(2,1)S(1)}, u32[]{:S(2)}, u32[]{:S(2)}) collective-permute-start(bf16[8,64,1024]{2,1,0:T(8,128)(2,1)} %get-tuple-element.36), channel_id=1, source_target_pairs={{0,56},{4,12},{8,0},{12,20},{16,8},{20,28},{24,16},{28,36},{32,24}... | collective-permute-start | bytes 3145736 | tf_op jit(solution)/shard_map/ppermute | solution.py:311
  94.9 2.1 %part_far.3 = bf16[8,64,1024]{2,1,0:T(8,128)(2,1)} custom-call(bf16[8,1,64,1024]{3,2,1,0:T(8,128)(2,1)} %copy-done), custom_call_target="tpu_custom_call" | custom-call | bytes 2097152 | tf_op jit(solution)/shard_map/part_far/pallas_call | solution.py:117
  96.9 2.0 collective-permute-start.7
  98.9 0.5 slice.7.count_ref
  99.4 0.6 slice.6.pairs_ref
  100.0 15.4 %collective-permute-done.6.refs_1_ = bf16[8,64,1024]{2,1,0:T(8,128)(2,1)S(1)} collective-permute-done((bf16[8,64,1024]{2,1,0:T(8,128)(2,1)}, bf16[8,64,1024]{2,1,0:T(8,128)(2,1)S(1)}, u32[]{:S(2)}, u32[]{:S(2)}) %collective-permute-start.6) | collective-permute-done | bytes 1048608 | tf_op jit(solution)/shard_map/ppermute | solution.py:311
  115.4 4.2 %collective-permute-done.7.refs_2_ = bf16[8,64,1024]{2,1,0:T(8,128)(2,1)} collective-permute-done((bf16[8,64,1024]{2,1,0:T(8,128)(2,1)}, bf16[8,64,1024]{2,1,0:T(8,128)(2,1)}, u32[]{:S(2)}, u32[]{:S(2)}) %collective-permute-start.7) | collective-permute-done | bytes 1048608 | tf_op jit(solution)/shard_map/ppermute | solution.py:311
  119.6 10.3 %gram_tiles.2 = (s16[1,2064,128]{2,1,0:T(8,128)(2,1)}, s16[1,2064,128]{2,1,0:T(8,128)(2,1)}, s16[1,2064,128]{2,1,0:T(8,128)(2,1)}, s16[1,2064,128]{2,1,0:T(8,128)(2,1)}) custom-call(s32[128]{0:T(128)} %slice.6.pairs_ref, s32[1]{0:T(128)} %slice.7.count_ref, bf16[8,64,1024]{2,1,0:T(8,128)(2,1)} %collective-permute-done.4.refs_0_, ...), custom_call_target="tpu_custom_call" | custom-call | flops 4294967296 | bytes 6291456 | tf_op jit(solution)/shard_map/gram_tiles/pallas_call | solution.py:203
  129.9 3.3 %collective-permute-start.9 = (s16[1,2064,128]{2,1,0:T(8,128)(2,1)}, s16[1,2064,128]{2,1,0:T(8,128)(2,1)S(1)}, u32[]{:S(2)}, u32[]{:S(2)}) collective-permute-start(s16[1,2064,128]{2,1,0:T(8,128)(2,1)} %get-tuple-element.39), channel_id=1, source_target_pairs={{0,2},{1,3},{2,0},{3,1},{4,6},{5,7},{6,4},{7,5},{8,10},{9,11},{10,... | collective-permute-start | bytes 1585160 | tf_op jit(solution)/shard_map/ppermute | solution.py:364
  133.2 1.1 collective-permute-start.10
  134.3 1.0 collective-permute-start.8
  135.2 5.5 %all-to-all-done.2 = bf16[8,4,64,1024]{3,2,1,0:T(8,128)(2,1)} async-done(((bf16[8,4,64,1024]{3,2,1,0:T(8,128)(2,1)}), bf16[8,4,64,1024]{3,2,1,0:T(8,128)(2,1)}, u32[]{:S(2)}, u32[]{:S(2)}) %all-to-all-start.2) | async-done | bytes 4194336 | tf_op jit(solution)/shard_map/all_to_all | solution.py:314
  140.7 9.7 %gram_tiles.3 = s16[4,2064,128]{2,1,0:T(8,128)(2,1)} custom-call(s32[128]{0:T(128)} %copy-done.7, s32[1]{0:T(128)S(6)} %copy.10.count_ref, bf16[32,64,1024]{2,1,0:T(8,128)(2,1)} %bitcast.3.refs_0_), custom_call_target="tpu_custom_call" | custom-call | flops 4294967296 | bytes 6291456 | tf_op jit(solution)/shard_map/gram_tiles/pallas_call | solution.py:203
  150.4 0.0 collective-permute-done.9.refs_2_
  150.4 7.6 %collective-permute-done.10.refs_3_ = s16[1,2064,128]{2,1,0:T(8,128)(2,1)S(1)} collective-permute-done((s16[1,2064,128]{2,1,0:T(8,128)(2,1)}, s16[1,2064,128]{2,1,0:T(8,128)(2,1)S(1)}, u32[]{:S(2)}, u32[]{:S(2)}) %collective-permute-start.10) | collective-permute-done | bytes 528416 | tf_op jit(solution)/shard_map/ppermute | solution.py:364
  158.0 0.0 collective-permute-done.8.refs_1_
  158.0 4.5 %all-to-all-start.3 = ((s16[4,2064,128]{2,1,0:T(8,128)(2,1)}), s16[4,2064,128]{2,1,0:T(8,128)(2,1)}, u32[]{:S(2)}, u32[]{:S(2)}) async-start(s16[4,2064,128]{2,1,0:T(8,128)(2,1)} %gram_tiles.3), calls=%async_computation.3 | async-start | bytes 4227072 | tf_op jit(solution)/shard_map/all_to_all | solution.py:314
  162.5 3.2 %sum_tiles.2 = s16[1,2064,128]{2,1,0:T(8,128)(2,1)} custom-call(s16[1,2064,128]{2,1,0:T(8,128)(2,1)} %get-tuple-element.42.refs_0_, s16[1,2064,128]{2,1,0:T(8,128)(2,1)} %copy-done.4, s16[1,2064,128]{2,1,0:T(8,128)(2,1)} %copy-done.2, s16[1,2064,128]{2,1,0:T(8,128)(2,1)} %copy-done.3), custom_call_target="tpu_custom_call" | custom-call | flops 4227072 | bytes 3170304 | tf_op jit(solution)/shard_map/sum_tiles/pallas_call | solution.py:274
  165.7 9.3 %collective-permute-start.11 = (s16[1,2064,128]{2,1,0:T(8,128)(2,1)}, s16[1,2064,128]{2,1,0:T(8,128)(2,1)S(1)}, u32[]{:S(2)}, u32[]{:S(2)}) collective-permute-start(s16[1,2064,128]{2,1,0:T(8,128)(2,1)} %sum_tiles.2), channel_id=1, source_target_pairs={{0,40},{4,28},{8,48},{12,36},{16,56},{20,44},{24,0},{28,52},{32,8}... | collective-permute-start | bytes 1585160 | tf_op jit(solution)/shard_map/ppermute | solution.py:311
  175.0 16.5 %collective-permute-done.11.refs_1_ = s16[1,2064,128]{2,1,0:T(8,128)(2,1)S(1)} collective-permute-done((s16[1,2064,128]{2,1,0:T(8,128)(2,1)}, s16[1,2064,128]{2,1,0:T(8,128)(2,1)S(1)}, u32[]{:S(2)}, u32[]{:S(2)}) %collective-permute-start.11) | collective-permute-done | bytes 528416 | tf_op jit(solution)/shard_map/ppermute | solution.py:311
  191.5 0.0 all-to-all-done.3.refs_0_
  191.5 0.8 copy-done.5
  192.3 3.4 %sum_tiles.3 = f32[16,128,128]{2,1,0:T(8,128)} custom-call(s16[4,2064,128]{2,1,0:T(8,128)(2,1)} %all-to-all-done.3.refs_0_, s16[1,2064,128]{2,1,0:T(8,128)(2,1)} %copy-done.5), custom_call_target="tpu_custom_call" | custom-call | flops 5283840 | bytes 3698688 | tf_op jit(solution)/shard_map/sum_tiles/pallas_call | solution.py:274
  (18 shorter events, 0.0 us)
Async XLA Ops:
  7.5 43.3 %all-to-all-start = ((bf16[8,3,64,1024]{3,2,1,0:T(8,128)(2,1)}), bf16[8,3,64,1024]{3,2,1,0:T(8,128)(2,1)}, u32[]{:S(2)}, u32[]{:S(2)}) async-start(bf16[8,3,64,1024]{3,2,1,0:T(8,128)(2,1)} %bitcast.4), calls=%async_computation | async-start | bytes 6291456 | tf_op jit(solution)/shard_map/all_to_all | solution.py:314
  14.1 49.8 %collective-permute-start = (bf16[8,64,1024]{2,1,0:T(8,128)(2,1)}, bf16[8,64,1024]{2,1,0:T(8,128)(2,1)S(1)}, u32[]{:S(2)}, u32[]{:S(2)}) collective-permute-start(bf16[8,64,1024]{2,1,0:T(8,128)(2,1)} %get-tuple-element.24), channel_id=1, source_target_pairs={{0,8},{8,16},{16,24},{24,32},{32,40},{40,48},{48,56},{56,0},{1,9},... | collective-permute-start | bytes 3145736 | tf_op jit(solution)/shard_map/ppermute | solution.py:307
  14.3 49.6 %collective-permute-start.1 = (bf16[8,64,1024]{2,1,0:T(8,128)(2,1)}, bf16[8,64,1024]{2,1,0:T(8,128)(2,1)}, u32[]{:S(2)}, u32[]{:S(2)}) collective-permute-start(bf16[8,64,1024]{2,1,0:T(8,128)(2,1)} %get-tuple-element.25), channel_id=1, source_target_pairs={{0,56},{8,0},{16,8},{24,16},{32,24},{40,32},{48,40},{56,48},{1,57}... | collective-permute-start | bytes 3145736 | tf_op jit(solution)/shard_map/ppermute | solution.py:307
  18.3 39.7 %collective-permute-start.2 = (bf16[4,64,1024]{2,1,0:T(8,128)(2,1)}, bf16[4,64,1024]{2,1,0:T(8,128)(2,1)S(1)}, u32[]{:S(2)}, u32[]{:S(2)}) collective-permute-start(bf16[4,64,1024]{2,1,0:T(8,128)(2,1)} %get-tuple-element.26), channel_id=1, source_target_pairs={{0,16},{8,24},{16,32},{24,40},{32,48},{40,56},{48,0},{56,8},{1,17}... | collective-permute-start | bytes 1572872 | tf_op jit(solution)/shard_map/ppermute | solution.py:307
  18.3 45.6 %collective-permute-start.3 = (bf16[4,64,1024]{2,1,0:T(8,128)(2,1)}, bf16[4,64,1024]{2,1,0:T(8,128)(2,1)}, u32[]{:S(2)}, u32[]{:S(2)}) collective-permute-start(bf16[4,64,1024]{2,1,0:T(8,128)(2,1)} %get-tuple-element.27), channel_id=1, source_target_pairs={{0,48},{8,56},{16,0},{24,8},{32,16},{40,24},{48,32},{56,40},{1,49}... | collective-permute-start | bytes 1572872 | tf_op jit(solution)/shard_map/ppermute | solution.py:307
  28.7 42.7 %copy-start.8 = (s32[1,64,2]{1,2,0:T(2,128)S(1)}, s32[1,64,2]{1,2,0:T(2,128)}, u32[]{:S(2)}) copy-start(s32[1,64,2]{1,2,0:T(2,128)} %param.10) | copy-start | bytes 1540
  53.3 33.0 %collective-permute-start.4 = (bf16[8,64,1024]{2,1,0:T(8,128)(2,1)}, bf16[8,64,1024]{2,1,0:T(8,128)(2,1)}, u32[]{:S(2)}, u32[]{:S(2)}) collective-permute-start(bf16[8,64,1024]{2,1,0:T(8,128)(2,1)} %get-tuple-element.34), channel_id=1, source_target_pairs={{0,48},{4,20},{8,56},{12,28},{16,0},{20,36},{24,8},{28,44},{32,16}... | collective-permute-start | bytes 3145736 | tf_op jit(solution)/shard_map/ppermute | solution.py:311
  57.9 15.4 %copy-start.6 = (bf16[4,64,1024]{2,1,0:T(8,128)(2,1)}, bf16[4,64,1024]{2,1,0:T(8,128)(2,1)S(1)}, u32[]{:S(2)}) copy-start(bf16[4,64,1024]{2,1,0:T(8,128)(2,1)S(1)} %collective-permute-done.2.refs_2_) | copy-start | bytes 1572868
  63.9 1.0 copy-start.1
  64.9 19.9 %all-to-all-start.1 = ((bf16[8,1,64,1024]{3,2,1,0:T(8,128)(2,1)}), bf16[8,1,64,1024]{3,2,1,0:T(8,128)(2,1)S(1)}, u32[]{:S(2)}, u32[]{:S(2)}) async-start(bf16[8,1,64,1024]{3,2,1,0:T(8,128)(2,1)} %bitcast.5), calls=%async_computation.1 | async-start | bytes 2097152 | tf_op jit(solution)/shard_map/all_to_all | solution.py:314
  71.7 5.2 %copy-start.7 = (s32[128]{0:T(128)}, s32[128]{0:T(128)S(1)}, u32[]{:S(2)}) copy-start(s32[128]{0:T(128)S(1)} %reshape.15.pairs_ref) | copy-start | bytes 1540
  71.7 6.8 %collective-permute-start.5 = (s32[129]{0:T(256)S(1)}, s32[129]{0:T(256)S(1)}, u32[]{:S(2)}, u32[]{:S(2)}) collective-permute-start(s32[129]{0:T(256)S(1)} %pad_add_fusion), channel_id=1, source_target_pairs={{0,24},{4,44},{8,32},{12,52},{16,40},{20,60},{24,48},{28,4},{32,56... | collective-permute-start | bytes 1556 | tf_op jit(solution)/shard_map/ppermute | solution.py:311
  84.8 1.5 copy-start
  86.3 54.4 %all-to-all-start.2 = ((bf16[8,4,64,1024]{3,2,1,0:T(8,128)(2,1)}), bf16[8,4,64,1024]{3,2,1,0:T(8,128)(2,1)}, u32[]{:S(2)}, u32[]{:S(2)}) async-start(bf16[8,4,64,1024]{3,2,1,0:T(8,128)(2,1)} %join_near.1), calls=%async_computation.2 | async-start | bytes 8388608 | tf_op jit(solution)/shard_map/all_to_all | solution.py:314
  92.9 22.6 %collective-permute-start.6 = (bf16[8,64,1024]{2,1,0:T(8,128)(2,1)}, bf16[8,64,1024]{2,1,0:T(8,128)(2,1)S(1)}, u32[]{:S(2)}, u32[]{:S(2)}) collective-permute-start(bf16[8,64,1024]{2,1,0:T(8,128)(2,1)} %get-tuple-element.36), channel_id=1, source_target_pairs={{0,56},{4,12},{8,0},{12,20},{16,8},{20,28},{24,16},{28,36},{32,24}... | collective-permute-start | bytes 3145736 | tf_op jit(solution)/shard_map/ppermute | solution.py:311
  96.9 22.7 %collective-permute-start.7 = (bf16[8,64,1024]{2,1,0:T(8,128)(2,1)}, bf16[8,64,1024]{2,1,0:T(8,128)(2,1)}, u32[]{:S(2)}, u32[]{:S(2)}) collective-permute-start(bf16[8,64,1024]{2,1,0:T(8,128)(2,1)} %part_far.3), channel_id=1, source_target_pairs={{0,8},{4,60},{8,16},{12,4},{16,24},{20,12},{24,32},{28,20},{32,40}... | collective-permute-start | bytes 3145736 | tf_op jit(solution)/shard_map/ppermute | solution.py:311
  115.4 4.2 %copy-start.9 = (bf16[8,64,1024]{2,1,0:T(8,128)(2,1)}, bf16[8,64,1024]{2,1,0:T(8,128)(2,1)S(1)}, u32[]{:S(2)}) copy-start(bf16[8,64,1024]{2,1,0:T(8,128)(2,1)S(1)} %collective-permute-done.6.refs_1_) | copy-start | bytes 3145732
  129.9 20.5 %collective-permute-start.9 = (s16[1,2064,128]{2,1,0:T(8,128)(2,1)}, s16[1,2064,128]{2,1,0:T(8,128)(2,1)S(1)}, u32[]{:S(2)}, u32[]{:S(2)}) collective-permute-start(s16[1,2064,128]{2,1,0:T(8,128)(2,1)} %get-tuple-element.39), channel_id=1, source_target_pairs={{0,2},{1,3},{2,0},{3,1},{4,6},{5,7},{6,4},{7,5},{8,10},{9,11},{10,... | collective-permute-start | bytes 1585160 | tf_op jit(solution)/shard_map/ppermute | solution.py:364
  133.2 24.8 %collective-permute-start.10 = (s16[1,2064,128]{2,1,0:T(8,128)(2,1)}, s16[1,2064,128]{2,1,0:T(8,128)(2,1)S(1)}, u32[]{:S(2)}, u32[]{:S(2)}) collective-permute-start(s16[1,2064,128]{2,1,0:T(8,128)(2,1)} %get-tuple-element.40), channel_id=1, source_target_pairs={{0,3},{1,0},{2,1},{3,2},{4,7},{5,4},{6,5},{7,6},{8,11},{9,8},{10,9... | collective-permute-start | bytes 1585160 | tf_op jit(solution)/shard_map/ppermute | solution.py:364
  134.3 23.7 %collective-permute-start.8 = (s16[1,2064,128]{2,1,0:T(8,128)(2,1)}, s16[1,2064,128]{2,1,0:T(8,128)(2,1)S(1)}, u32[]{:S(2)}, u32[]{:S(2)}) collective-permute-start(s16[1,2064,128]{2,1,0:T(8,128)(2,1)} %get-tuple-element.37), channel_id=1, source_target_pairs={{0,1},{1,2},{2,3},{3,0},{4,5},{5,6},{6,7},{7,4},{8,9},{9,10},{10,1... | collective-permute-start | bytes 1585160 | tf_op jit(solution)/shard_map/ppermute | solution.py:364
  150.4 12.1 %copy-start.2 = (s16[1,2064,128]{2,1,0:T(8,128)(2,1)}, s16[1,2064,128]{2,1,0:T(8,128)(2,1)S(1)}, u32[]{:S(2)}) copy-start(s16[1,2064,128]{2,1,0:T(8,128)(2,1)S(1)} %collective-permute-done.9.refs_2_) | copy-start | bytes 1585156
  158.0 4.5 %copy-start.3 = (s16[1,2064,128]{2,1,0:T(8,128)(2,1)}, s16[1,2064,128]{2,1,0:T(8,128)(2,1)S(1)}, u32[]{:S(2)}) copy-start(s16[1,2064,128]{2,1,0:T(8,128)(2,1)S(1)} %collective-permute-done.10.refs_3_) | copy-start | bytes 1585156
  158.0 4.5 %copy-start.4 = (s16[1,2064,128]{2,1,0:T(8,128)(2,1)}, s16[1,2064,128]{2,1,0:T(8,128)(2,1)S(1)}, u32[]{:S(2)}) copy-start(s16[1,2064,128]{2,1,0:T(8,128)(2,1)S(1)} %collective-permute-done.8.refs_1_) | copy-start | bytes 1585156
  158.0 33.4 %all-to-all-start.3 = ((s16[4,2064,128]{2,1,0:T(8,128)(2,1)}), s16[4,2064,128]{2,1,0:T(8,128)(2,1)}, u32[]{:S(2)}, u32[]{:S(2)}) async-start(s16[4,2064,128]{2,1,0:T(8,128)(2,1)} %gram_tiles.3), calls=%async_computation.3 | async-start | bytes 4227072 | tf_op jit(solution)/shard_map/all_to_all | solution.py:314
  165.7 25.7 %collective-permute-start.11 = (s16[1,2064,128]{2,1,0:T(8,128)(2,1)}, s16[1,2064,128]{2,1,0:T(8,128)(2,1)S(1)}, u32[]{:S(2)}, u32[]{:S(2)}) collective-permute-start(s16[1,2064,128]{2,1,0:T(8,128)(2,1)} %sum_tiles.2), channel_id=1, source_target_pairs={{0,40},{4,28},{8,48},{12,36},{16,56},{20,44},{24,0},{28,52},{32,8}... | collective-permute-start | bytes 1585160 | tf_op jit(solution)/shard_map/ppermute | solution.py:311
  191.5 0.8 copy-start.5

commit v7 on v6

--- a/solution.py
+++ b/solution.py
@@ -334,7 +334,7 @@
         sent = [k for k, s in enumerate(steps) if s]
         copies = [(0, (h, k), (lines, *unit), q, h) for q, k in enumerate(sent) for h in half]
         parts = copy_parts([far], [(group, *unit)] * len(sent), copies, "part_far")
-        return [away(part, steps[k]) for part, k in zip(parts, sent)]
+        return [away(part, steps[k] // abs(steps[k])) for part, k in zip(parts, sent)]
 
     far_first = spread(far_first, ("c", "x"))
     far_first = after(far_first, stay)
@@ -354,7 +354,8 @@
         ],
         "join_near",
     )
-    near = after(near, far_then, far_parts[0], far_wanted)
+    near = after(near, far_then, far_parts[0], far_parts[1], far_wanted)
+    far_parts[0] = away(far_parts[0], -1)
     near = spread(near, ("c", "x")).reshape(group * 4, *unit)
 
     far_pieces = [(q, whole) for q in range(len(far_parts))] + [(len(far_parts), (whole, FAR_FIRST.index(0)))]

time: 199 us -> 196 us (0.985); the launches traced: 196 us -> 196 us
  starting transfers between devices: 56.6 us -> 54.4 us
    ppermute x5 -> x6, waiting for transfers between devices: 39.2 us -> 46.5 us  [away(): return lax.ppermute(value, ('z', 'c'), moves)]
    ppermute x4, waiting for transfers between devices: 5.97 us -> 0.01 us  [up(): lax.ppermute(value, 'z', [(b, (b + step) % planes) for b in range(planes)])]
    all_to_all x4, waiting for transfers between devices: 33.9 us -> 31.5 us  [spread(): return lax.all_to_all(value, axes, split_axis=0, concat_axis=0, tiled=True)]
    ppermute x5 -> x6, starting transfers between devices: 19.5 us -> 19.1 us  [away(): return lax.ppermute(value, ('z', 'c'), moves)]
  transfers between devices with their start and end apart: 16 -> 17, of which waited for: 10 -> 8; matrix products, arithmetic and copies ran while one was open for 1% -> 1% of each run, Pallas kernels for 19% -> 19%
where the time goes in v7:
time: 196 us
  waiting for transfers between devices  87.6 us (45%)
  starting transfers between devices  54.4 us (28%)
  Pallas kernels  48.5 us (25%)
  local copies, waits for them, and re-layouts  4.24 us (2%)
    ppermute x6, waiting for transfers between devices, away(): return lax.ppermute(value, ('z', 'c'), moves)  46.5 us
    all_to_all x4, waiting for transfers between devices, spread(): return lax.all_to_all(value, axes, split_axis=0, concat_axis=0, tiled=True)  31.5 us
    all_to_all x4, starting transfers between devices, spread(): return lax.all_to_all(value, axes, split_axis=0, concat_axis=0, tiled=True)  21.7 us
    pallas_call x2, Pallas kernels, gram_tiles(): pl.pallas_call(kernel, out_shape=[jax.ShapeDtypeStruct((n, quarter * BLOC...  20.1 us
    ppermute x6, starting transfers between devices, away(): return lax.ppermute(value, ('z', 'c'), moves)  19.1 us
    pallas_call x2, Pallas kernels, scale_columns(): pl.pallas_call(kernel, out_shape=[jax.ShapeDtypeStruct((size, rows, WIDTH...  13.7 us
    ppermute x3, waiting for transfers between devices, body(): lax.ppermute(far_tiles[k], 'y', [(b, (b + k) % quarters) for b in range(q...  9.53 us
    ppermute x4, starting transfers between devices, up(): lax.ppermute(value, 'z', [(b, (b + step) % planes) for b in range(planes)])  8.26 us
  transfers between devices with their start and end apart: 17, of which 8 were waited for; matrix products, arithmetic and copies ran while one was open for 1% of the time, Pallas kernels for 19%

profile of v7, /device:TPU:2, one launch (start us, length us, event | category | flops | bytes accessed | tf_op | source)
XLA Modules:
  0.0 195.5 jit_solution(12952742749440658974)
XLA Ops:
  0.0 7.5 %scale_columns.2 = (bf16[24,64,1024]{2,1,0:T(8,128)(2,1)}, bf16[8,64,1024]{2,1,0:T(8,128)(2,1)}, bf16[8,64,1024]{2,1,0:T(8,128)(2,1)}, bf16[4,64,1024]{2,1,0:T(8,128)(2,1)}, bf16[4,64,1024]{2,1,0:T(8,128)(2,1)}) custom-call(s32[48]{0:T(128)} %constant.4.clone.units_ref, s32[512]{0:T(512)} %order_ref.3, bf16[64,65536]{1,0:T(8,128)(2,1)} %jac_ref.3, ...), custom_call_target="tpu_custom_call" | custom-call | flops 3145728 | bytes 14680064 | tf_op jit(solution)/shard_map/scale_columns/pallas_call | solution.py:71
  7.5 6.6 %all-to-all-start = ((bf16[8,3,64,1024]{3,2,1,0:T(8,128)(2,1)}), bf16[8,3,64,1024]{3,2,1,0:T(8,128)(2,1)}, u32[]{:S(2)}, u32[]{:S(2)}) async-start(bf16[8,3,64,1024]{3,2,1,0:T(8,128)(2,1)} %bitcast.4), calls=%async_computation | async-start | bytes 6291456 | tf_op jit(solution)/shard_map/all_to_all | solution.py:314
  14.1 0.2 collective-permute-start
  14.3 3.9 %collective-permute-start.1 = (bf16[8,64,1024]{2,1,0:T(8,128)(2,1)}, bf16[8,64,1024]{2,1,0:T(8,128)(2,1)}, u32[]{:S(2)}, u32[]{:S(2)}) collective-permute-start(bf16[8,64,1024]{2,1,0:T(8,128)(2,1)} %get-tuple-element.25), channel_id=1, source_target_pairs={{0,56},{8,0},{16,8},{24,16},{32,24},{40,32},{48,40},{56,48},{1,57}... | collective-permute-start | bytes 3145736 | tf_op jit(solution)/shard_map/ppermute | solution.py:307
  18.2 0.0 collective-permute-start.2
  18.2 4.1 %collective-permute-start.3 = (bf16[4,64,1024]{2,1,0:T(8,128)(2,1)}, bf16[4,64,1024]{2,1,0:T(8,128)(2,1)}, u32[]{:S(2)}, u32[]{:S(2)}) collective-permute-start(bf16[4,64,1024]{2,1,0:T(8,128)(2,1)} %get-tuple-element.27), channel_id=1, source_target_pairs={{0,48},{8,56},{16,0},{24,8},{32,16},{40,24},{48,32},{56,40},{1,49}... | collective-permute-start | bytes 1572872 | tf_op jit(solution)/shard_map/ppermute | solution.py:307
  22.4 6.3 %scale_columns.3 = (bf16[8,64,1024]{2,1,0:T(8,128)(2,1)}, bf16[8,64,1024]{2,1,0:T(8,128)(2,1)}) custom-call(s32[16]{0:T(128)} %constant.5.clone.units_ref, s32[512]{0:T(512)} %order_ref.3, bf16[64,65536]{1,0:T(8,128)(2,1)} %jac_ref.3, f32[1,64]{1,0:T(1,128)} %bitcast.7), custom_call_target="tpu_custom_call" | custom-call | flops 1048576 | bytes 10485760 | tf_op jit(solution)/shard_map/scale_columns/pallas_call | solution.py:71
  28.6 0.0 copy-start.8
  28.7 22.1 %all-to-all-done.refs_0_.refs_3_ = bf16[8,3,64,1024]{3,2,1,0:T(8,128)(2,1)} async-done(((bf16[8,3,64,1024]{3,2,1,0:T(8,128)(2,1)}), bf16[8,3,64,1024]{3,2,1,0:T(8,128)(2,1)}, u32[]{:S(2)}, u32[]{:S(2)}) %all-to-all-start) | async-done | bytes 3145760 | tf_op jit(solution)/shard_map/all_to_all | solution.py:314
  50.7 2.4 %part_far.2 = (bf16[8,64,1024]{2,1,0:T(8,128)(2,1)}, bf16[8,64,1024]{2,1,0:T(8,128)(2,1)}) custom-call(bf16[8,3,64,1024]{3,2,1,0:T(8,128)(2,1)} %all-to-all-done.refs_0_.refs_3_), custom_call_target="tpu_custom_call" | custom-call | bytes 4194304 | tf_op jit(solution)/shard_map/part_far/pallas_call | solution.py:117
  53.2 4.2 %collective-permute-start.4 = (bf16[8,64,1024]{2,1,0:T(8,128)(2,1)}, bf16[8,64,1024]{2,1,0:T(8,128)(2,1)}, u32[]{:S(2)}, u32[]{:S(2)}) collective-permute-start(bf16[8,64,1024]{2,1,0:T(8,128)(2,1)} %get-tuple-element.34), channel_id=1, source_target_pairs={{0,56},{4,12},{8,0},{12,20},{16,8},{20,28},{24,16},{28,36},{32,24}... | collective-permute-start | bytes 3145736 | tf_op jit(solution)/shard_map/ppermute | solution.py:311
  57.4 0.0 collective-permute-done.2.refs_2_
  57.4 10.0 %collective-permute-start.5 = (bf16[8,64,1024]{2,1,0:T(8,128)(2,1)}, bf16[8,64,1024]{2,1,0:T(8,128)(2,1)}, u32[]{:S(2)}, u32[]{:S(2)}) collective-permute-start(bf16[8,64,1024]{2,1,0:T(8,128)(2,1)} %get-tuple-element.35), channel_id=1, source_target_pairs={{0,56},{4,12},{8,0},{12,20},{16,8},{20,28},{24,16},{28,36},{32,24}... | collective-permute-start | bytes 3145736 | tf_op jit(solution)/shard_map/ppermute | solution.py:311
  67.4 1.0 copy-done.1
  68.4 4.8 %all-to-all-start.1 = ((bf16[8,1,64,1024]{3,2,1,0:T(8,128)(2,1)}), bf16[8,1,64,1024]{3,2,1,0:T(8,128)(2,1)S(1)}, u32[]{:S(2)}, u32[]{:S(2)}) async-start(bf16[8,1,64,1024]{3,2,1,0:T(8,128)(2,1)} %bitcast.5), calls=%async_computation.1 | async-start | bytes 2097152 | tf_op jit(solution)/shard_map/all_to_all | solution.py:314
  73.8 0.1 copy.9
  73.9 0.1 reshape.15.pairs_ref
  74.1 0.1 collective-permute-start.6
  74.2 3.6 %join_near.1 = bf16[8,4,64,1024]{3,2,1,0:T(8,128)(2,1)} custom-call(bf16[8,64,1024]{2,1,0:T(8,128)(2,1)} %copy-done.1, bf16[8,64,1024]{2,1,0:T(8,128)(2,1)} %collective-permute-done.1.refs_1_, bf16[4,64,1024]{2,1,0:T(8,128)(2,1)} %copy-done.6, bf16[4,64,1024]{2,1,0:T(8,128)(2,1)} %collective-permute-done.3.refs_3_, ...), custom_call_target="tpu_custom_call" | custom-call | bytes 8388608 | tf_op jit(solution)/shard_map/join_near/pallas_call | solution.py:117
  77.8 3.0 %collective-permute-done.6 = s32[129]{0:T(256)S(1)} collective-permute-done((s32[129]{0:T(256)S(1)}, s32[129]{0:T(256)S(1)}, u32[]{:S(2)}, u32[]{:S(2)}) %collective-permute-start.6) | collective-permute-done | bytes 548 | tf_op jit(solution)/shard_map/ppermute | solution.py:311
  80.8 6.4 %all-to-all-done.1.refs_0_ = bf16[8,1,64,1024]{3,2,1,0:T(8,128)(2,1)S(1)} async-done(((bf16[8,1,64,1024]{3,2,1,0:T(8,128)(2,1)}), bf16[8,1,64,1024]{3,2,1,0:T(8,128)(2,1)S(1)}, u32[]{:S(2)}, u32[]{:S(2)}) %all-to-all-start.1) | async-done | bytes 1048608 | tf_op jit(solution)/shard_map/all_to_all | solution.py:314
  87.2 0.0 collective-permute-done.4
  87.2 0.0 collective-permute-done.5.refs_1_
  87.2 1.0 copy-done
  88.2 5.8 %all-to-all-start.2 = ((bf16[8,4,64,1024]{3,2,1,0:T(8,128)(2,1)}), bf16[8,4,64,1024]{3,2,1,0:T(8,128)(2,1)}, u32[]{:S(2)}, u32[]{:S(2)}) async-start(bf16[8,4,64,1024]{3,2,1,0:T(8,128)(2,1)} %join_near.1), calls=%async_computation.2 | async-start | bytes 8388608 | tf_op jit(solution)/shard_map/all_to_all | solution.py:314
  94.0 2.1 %part_far.3 = bf16[8,64,1024]{2,1,0:T(8,128)(2,1)} custom-call(bf16[8,1,64,1024]{3,2,1,0:T(8,128)(2,1)} %copy-done), custom_call_target="tpu_custom_call" | custom-call | bytes 2097152 | tf_op jit(solution)/shard_map/part_far/pallas_call | solution.py:117
  96.0 0.1 collective-permute-start.8
  96.1 3.2 %collective-permute-start.7 = (bf16[8,64,1024]{2,1,0:T(8,128)(2,1)}, bf16[8,64,1024]{2,1,0:T(8,128)(2,1)}, u32[]{:S(2)}, u32[]{:S(2)}) collective-permute-start(bf16[8,64,1024]{2,1,0:T(8,128)(2,1)} %collective-permute-done.4), channel_id=1, source_target_pairs={{0,56},{4,12},{8,0},{12,20},{16,8},{20,28},{24,16},{28,36},{32,24}... | collective-permute-start | bytes 3145736 | tf_op jit(solution)/shard_map/ppermute | solution.py:311
  99.3 0.6 slice.7.count_ref
  99.9 0.5 slice.6.pairs_ref
  100.4 22.9 %collective-permute-done.8.refs_2_ = bf16[8,64,1024]{2,1,0:T(8,128)(2,1)S(1)} collective-permute-done((bf16[8,64,1024]{2,1,0:T(8,128)(2,1)}, bf16[8,64,1024]{2,1,0:T(8,128)(2,1)S(1)}, u32[]{:S(2)}, u32[]{:S(2)}) %collective-permute-start.8) | collective-permute-done | bytes 1048608 | tf_op jit(solution)/shard_map/ppermute | solution.py:311
  123.3 0.0 collective-permute-done.7.refs_0_
  123.3 1.0 copy-done.9
  124.3 10.4 %gram_tiles.2 = (s16[1,2064,128]{2,1,0:T(8,128)(2,1)}, s16[1,2064,128]{2,1,0:T(8,128)(2,1)}, s16[1,2064,128]{2,1,0:T(8,128)(2,1)}, s16[1,2064,128]{2,1,0:T(8,128)(2,1)}) custom-call(s32[128]{0:T(128)} %slice.6.pairs_ref, s32[1]{0:T(128)} %slice.7.count_ref, bf16[8,64,1024]{2,1,0:T(8,128)(2,1)} %collective-permute-done.7.refs_0_, ...), custom_call_target="tpu_custom_call" | custom-call | flops 4294967296 | bytes 6291456 | tf_op jit(solution)/shard_map/gram_tiles/pallas_call | solution.py:203
  134.7 3.3 %collective-permute-start.10 = (s16[1,2064,128]{2,1,0:T(8,128)(2,1)}, s16[1,2064,128]{2,1,0:T(8,128)(2,1)S(1)}, u32[]{:S(2)}, u32[]{:S(2)}) collective-permute-start(s16[1,2064,128]{2,1,0:T(8,128)(2,1)} %get-tuple-element.39), channel_id=1, source_target_pairs={{0,2},{1,3},{2,0},{3,1},{4,6},{5,7},{6,4},{7,5},{8,10},{9,11},{10,... | collective-permute-start | bytes 1585160 | tf_op jit(solution)/shard_map/ppermute | solution.py:365
  138.0 1.1 collective-permute-start.11
  139.0 1.0 collective-permute-start.9
  140.0 1.8 all-to-all-done.2
  141.8 9.7 %gram_tiles.3 = s16[4,2064,128]{2,1,0:T(8,128)(2,1)} custom-call(s32[128]{0:T(128)} %copy-done.7, s32[1]{0:T(128)S(6)} %copy.10.count_ref, bf16[32,64,1024]{2,1,0:T(8,128)(2,1)} %bitcast.3.refs_0_), custom_call_target="tpu_custom_call" | custom-call | flops 4294967296 | bytes 6291456 | tf_op jit(solution)/shard_map/gram_tiles/pallas_call | solution.py:203
  151.5 0.0 collective-permute-done.10.refs_2_
  151.5 9.5 %collective-permute-done.11.refs_3_ = s16[1,2064,128]{2,1,0:T(8,128)(2,1)S(1)} collective-permute-done((s16[1,2064,128]{2,1,0:T(8,128)(2,1)}, s16[1,2064,128]{2,1,0:T(8,128)(2,1)S(1)}, u32[]{:S(2)}, u32[]{:S(2)}) %collective-permute-start.11) | collective-permute-done | bytes 528416 | tf_op jit(solution)/shard_map/ppermute | solution.py:365
  161.1 0.0 collective-permute-done.9.refs_1_
  161.1 4.5 %all-to-all-start.3 = ((s16[4,2064,128]{2,1,0:T(8,128)(2,1)}), s16[4,2064,128]{2,1,0:T(8,128)(2,1)}, u32[]{:S(2)}, u32[]{:S(2)}) async-start(s16[4,2064,128]{2,1,0:T(8,128)(2,1)} %gram_tiles.3), calls=%async_computation.3 | async-start | bytes 4227072 | tf_op jit(solution)/shard_map/all_to_all | solution.py:314
  165.6 3.2 %sum_tiles.2 = s16[1,2064,128]{2,1,0:T(8,128)(2,1)} custom-call(s16[1,2064,128]{2,1,0:T(8,128)(2,1)} %get-tuple-element.42.refs_0_, s16[1,2064,128]{2,1,0:T(8,128)(2,1)} %copy-done.4, s16[1,2064,128]{2,1,0:T(8,128)(2,1)} %copy-done.2, s16[1,2064,128]{2,1,0:T(8,128)(2,1)} %copy-done.3), custom_call_target="tpu_custom_call" | custom-call | flops 4227072 | bytes 3170304 | tf_op jit(solution)/shard_map/sum_tiles/pallas_call | solution.py:274
  168.8 1.5 collective-permute-start.12
  170.3 20.7 %collective-permute-done.12.refs_1_ = s16[1,2064,128]{2,1,0:T(8,128)(2,1)S(1)} collective-permute-done((s16[1,2064,128]{2,1,0:T(8,128)(2,1)}, s16[1,2064,128]{2,1,0:T(8,128)(2,1)S(1)}, u32[]{:S(2)}, u32[]{:S(2)}) %collective-permute-start.12) | collective-permute-done | bytes 528416 | tf_op jit(solution)/shard_map/ppermute | solution.py:311
  190.9 1.2 all-to-all-done.3.refs_0_
  192.2 3.4 %sum_tiles.3 = f32[16,128,128]{2,1,0:T(8,128)} custom-call(s16[4,2064,128]{2,1,0:T(8,128)(2,1)} %all-to-all-done.3.refs_0_, s16[1,2064,128]{2,1,0:T(8,128)(2,1)} %copy-done.5), custom_call_target="tpu_custom_call" | custom-call | flops 5283840 | bytes 3698688 | tf_op jit(solution)/shard_map/sum_tiles/pallas_call | solution.py:274
  (20 shorter events, 0.0 us)
Async XLA Ops:
  7.5 43.3 %all-to-all-start = ((bf16[8,3,64,1024]{3,2,1,0:T(8,128)(2,1)}), bf16[8,3,64,1024]{3,2,1,0:T(8,128)(2,1)}, u32[]{:S(2)}, u32[]{:S(2)}) async-start(bf16[8,3,64,1024]{3,2,1,0:T(8,128)(2,1)} %bitcast.4), calls=%async_computation | async-start | bytes 6291456 | tf_op jit(solution)/shard_map/all_to_all | solution.py:314
  14.1 53.3 %collective-permute-start = (bf16[8,64,1024]{2,1,0:T(8,128)(2,1)}, bf16[8,64,1024]{2,1,0:T(8,128)(2,1)S(1)}, u32[]{:S(2)}, u32[]{:S(2)}) collective-permute-start(bf16[8,64,1024]{2,1,0:T(8,128)(2,1)} %get-tuple-element.24), channel_id=1, source_target_pairs={{0,8},{8,16},{16,24},{24,32},{32,40},{40,48},{48,56},{56,0},{1,9},... | collective-permute-start | bytes 3145736 | tf_op jit(solution)/shard_map/ppermute | solution.py:307
  14.3 53.1 %collective-permute-start.1 = (bf16[8,64,1024]{2,1,0:T(8,128)(2,1)}, bf16[8,64,1024]{2,1,0:T(8,128)(2,1)}, u32[]{:S(2)}, u32[]{:S(2)}) collective-permute-start(bf16[8,64,1024]{2,1,0:T(8,128)(2,1)} %get-tuple-element.25), channel_id=1, source_target_pairs={{0,56},{8,0},{16,8},{24,16},{32,24},{40,32},{48,40},{56,48},{1,57}... | collective-permute-start | bytes 3145736 | tf_op jit(solution)/shard_map/ppermute | solution.py:307
  18.2 39.2 %collective-permute-start.2 = (bf16[4,64,1024]{2,1,0:T(8,128)(2,1)}, bf16[4,64,1024]{2,1,0:T(8,128)(2,1)S(1)}, u32[]{:S(2)}, u32[]{:S(2)}) collective-permute-start(bf16[4,64,1024]{2,1,0:T(8,128)(2,1)} %get-tuple-element.26), channel_id=1, source_target_pairs={{0,16},{8,24},{16,32},{24,40},{32,48},{40,56},{48,0},{56,8},{1,17}... | collective-permute-start | bytes 1572872 | tf_op jit(solution)/shard_map/ppermute | solution.py:307
  18.2 49.2 %collective-permute-start.3 = (bf16[4,64,1024]{2,1,0:T(8,128)(2,1)}, bf16[4,64,1024]{2,1,0:T(8,128)(2,1)}, u32[]{:S(2)}, u32[]{:S(2)}) collective-permute-start(bf16[4,64,1024]{2,1,0:T(8,128)(2,1)} %get-tuple-element.27), channel_id=1, source_target_pairs={{0,48},{8,56},{16,0},{24,8},{32,16},{40,24},{48,32},{56,40},{1,49}... | collective-permute-start | bytes 1572872 | tf_op jit(solution)/shard_map/ppermute | solution.py:307
  28.6 45.2 %copy-start.8 = (s32[1,64,2]{1,2,0:T(2,128)S(1)}, s32[1,64,2]{1,2,0:T(2,128)}, u32[]{:S(2)}) copy-start(s32[1,64,2]{1,2,0:T(2,128)} %param.10) | copy-start | bytes 1540
  53.2 34.0 %collective-permute-start.4 = (bf16[8,64,1024]{2,1,0:T(8,128)(2,1)}, bf16[8,64,1024]{2,1,0:T(8,128)(2,1)}, u32[]{:S(2)}, u32[]{:S(2)}) collective-permute-start(bf16[8,64,1024]{2,1,0:T(8,128)(2,1)} %get-tuple-element.34), channel_id=1, source_target_pairs={{0,56},{4,12},{8,0},{12,20},{16,8},{20,28},{24,16},{28,36},{32,24}... | collective-permute-start | bytes 3145736 | tf_op jit(solution)/shard_map/ppermute | solution.py:311
  57.4 16.8 %copy-start.6 = (bf16[4,64,1024]{2,1,0:T(8,128)(2,1)}, bf16[4,64,1024]{2,1,0:T(8,128)(2,1)S(1)}, u32[]{:S(2)}) copy-start(bf16[4,64,1024]{2,1,0:T(8,128)(2,1)S(1)} %collective-permute-done.2.refs_2_) | copy-start | bytes 1572868
  57.4 29.8 %collective-permute-start.5 = (bf16[8,64,1024]{2,1,0:T(8,128)(2,1)}, bf16[8,64,1024]{2,1,0:T(8,128)(2,1)}, u32[]{:S(2)}, u32[]{:S(2)}) collective-permute-start(bf16[8,64,1024]{2,1,0:T(8,128)(2,1)} %get-tuple-element.35), channel_id=1, source_target_pairs={{0,56},{4,12},{8,0},{12,20},{16,8},{20,28},{24,16},{28,36},{32,24}... | collective-permute-start | bytes 3145736 | tf_op jit(solution)/shard_map/ppermute | solution.py:311
  67.4 1.0 copy-start.1
  68.4 18.8 %all-to-all-start.1 = ((bf16[8,1,64,1024]{3,2,1,0:T(8,128)(2,1)}), bf16[8,1,64,1024]{3,2,1,0:T(8,128)(2,1)S(1)}, u32[]{:S(2)}, u32[]{:S(2)}) async-start(bf16[8,1,64,1024]{3,2,1,0:T(8,128)(2,1)} %bitcast.5), calls=%async_computation.1 | async-start | bytes 2097152 | tf_op jit(solution)/shard_map/all_to_all | solution.py:314
  74.1 3.7 %copy-start.7 = (s32[128]{0:T(128)}, s32[128]{0:T(128)S(1)}, u32[]{:S(2)}) copy-start(s32[128]{0:T(128)S(1)} %reshape.15.pairs_ref) | copy-start | bytes 1540
  74.1 6.7 %collective-permute-start.6 = (s32[129]{0:T(256)S(1)}, s32[129]{0:T(256)S(1)}, u32[]{:S(2)}, u32[]{:S(2)}) collective-permute-start(s32[129]{0:T(256)S(1)} %pad_add_fusion), channel_id=1, source_target_pairs={{0,24},{4,44},{8,32},{12,52},{16,40},{20,60},{24,48},{28,4},{32,56... | collective-permute-start | bytes 1556 | tf_op jit(solution)/shard_map/ppermute | solution.py:311
  87.2 1.0 copy-start
  88.2 53.6 %all-to-all-start.2 = ((bf16[8,4,64,1024]{3,2,1,0:T(8,128)(2,1)}), bf16[8,4,64,1024]{3,2,1,0:T(8,128)(2,1)}, u32[]{:S(2)}, u32[]{:S(2)}) async-start(bf16[8,4,64,1024]{3,2,1,0:T(8,128)(2,1)} %join_near.1), calls=%async_computation.2 | async-start | bytes 8388608 | tf_op jit(solution)/shard_map/all_to_all | solution.py:314
  96.0 27.3 %collective-permute-start.8 = (bf16[8,64,1024]{2,1,0:T(8,128)(2,1)}, bf16[8,64,1024]{2,1,0:T(8,128)(2,1)S(1)}, u32[]{:S(2)}, u32[]{:S(2)}) collective-permute-start(bf16[8,64,1024]{2,1,0:T(8,128)(2,1)} %part_far.3), channel_id=1, source_target_pairs={{0,8},{4,60},{8,16},{12,4},{16,24},{20,12},{24,32},{28,20},{32,40}... | collective-permute-start | bytes 3145736 | tf_op jit(solution)/shard_map/ppermute | solution.py:311
  96.1 27.2 %collective-permute-start.7 = (bf16[8,64,1024]{2,1,0:T(8,128)(2,1)}, bf16[8,64,1024]{2,1,0:T(8,128)(2,1)}, u32[]{:S(2)}, u32[]{:S(2)}) collective-permute-start(bf16[8,64,1024]{2,1,0:T(8,128)(2,1)} %collective-permute-done.4), channel_id=1, source_target_pairs={{0,56},{4,12},{8,0},{12,20},{16,8},{20,28},{24,16},{28,36},{32,24}... | collective-permute-start | bytes 3145736 | tf_op jit(solution)/shard_map/ppermute | solution.py:311
  123.3 1.0 copy-start.9
  134.7 16.8 %collective-permute-start.10 = (s16[1,2064,128]{2,1,0:T(8,128)(2,1)}, s16[1,2064,128]{2,1,0:T(8,128)(2,1)S(1)}, u32[]{:S(2)}, u32[]{:S(2)}) collective-permute-start(s16[1,2064,128]{2,1,0:T(8,128)(2,1)} %get-tuple-element.39), channel_id=1, source_target_pairs={{0,2},{1,3},{2,0},{3,1},{4,6},{5,7},{6,4},{7,5},{8,10},{9,11},{10,... | collective-permute-start | bytes 1585160 | tf_op jit(solution)/shard_map/ppermute | solution.py:365
  138.0 23.1 %collective-permute-start.11 = (s16[1,2064,128]{2,1,0:T(8,128)(2,1)}, s16[1,2064,128]{2,1,0:T(8,128)(2,1)S(1)}, u32[]{:S(2)}, u32[]{:S(2)}) collective-permute-start(s16[1,2064,128]{2,1,0:T(8,128)(2,1)} %get-tuple-element.40), channel_id=1, source_target_pairs={{0,3},{1,0},{2,1},{3,2},{4,7},{5,4},{6,5},{7,6},{8,11},{9,8},{10,9... | collective-permute-start | bytes 1585160 | tf_op jit(solution)/shard_map/ppermute | solution.py:365
  139.0 22.0 %collective-permute-start.9 = (s16[1,2064,128]{2,1,0:T(8,128)(2,1)}, s16[1,2064,128]{2,1,0:T(8,128)(2,1)S(1)}, u32[]{:S(2)}, u32[]{:S(2)}) collective-permute-start(s16[1,2064,128]{2,1,0:T(8,128)(2,1)} %get-tuple-element.37), channel_id=1, source_target_pairs={{0,1},{1,2},{2,3},{3,0},{4,5},{5,6},{6,7},{7,4},{8,9},{9,10},{10,1... | collective-permute-start | bytes 1585160 | tf_op jit(solution)/shard_map/ppermute | solution.py:365
  151.5 14.0 %copy-start.2 = (s16[1,2064,128]{2,1,0:T(8,128)(2,1)}, s16[1,2064,128]{2,1,0:T(8,128)(2,1)S(1)}, u32[]{:S(2)}) copy-start(s16[1,2064,128]{2,1,0:T(8,128)(2,1)S(1)} %collective-permute-done.10.refs_2_) | copy-start | bytes 1585156
  161.1 4.5 %copy-start.3 = (s16[1,2064,128]{2,1,0:T(8,128)(2,1)}, s16[1,2064,128]{2,1,0:T(8,128)(2,1)S(1)}, u32[]{:S(2)}) copy-start(s16[1,2064,128]{2,1,0:T(8,128)(2,1)S(1)} %collective-permute-done.11.refs_3_) | copy-start | bytes 1585156
  161.1 4.5 %copy-start.4 = (s16[1,2064,128]{2,1,0:T(8,128)(2,1)}, s16[1,2064,128]{2,1,0:T(8,128)(2,1)S(1)}, u32[]{:S(2)}) copy-start(s16[1,2064,128]{2,1,0:T(8,128)(2,1)S(1)} %collective-permute-done.9.refs_1_) | copy-start | bytes 1585156
  161.1 31.1 %all-to-all-start.3 = ((s16[4,2064,128]{2,1,0:T(8,128)(2,1)}), s16[4,2064,128]{2,1,0:T(8,128)(2,1)}, u32[]{:S(2)}, u32[]{:S(2)}) async-start(s16[4,2064,128]{2,1,0:T(8,128)(2,1)} %gram_tiles.3), calls=%async_computation.3 | async-start | bytes 4227072 | tf_op jit(solution)/shard_map/all_to_all | solution.py:314
  168.8 22.2 %collective-permute-start.12 = (s16[1,2064,128]{2,1,0:T(8,128)(2,1)}, s16[1,2064,128]{2,1,0:T(8,128)(2,1)S(1)}, u32[]{:S(2)}, u32[]{:S(2)}) collective-permute-start(s16[1,2064,128]{2,1,0:T(8,128)(2,1)} %sum_tiles.2), channel_id=1, source_target_pairs={{0,40},{4,28},{8,48},{12,36},{16,56},{20,44},{24,0},{28,52},{32,8}... | collective-permute-start | bytes 1585160 | tf_op jit(solution)/shard_map/ppermute | solution.py:311
  190.9 1.2 copy-start.5

commit v8 on v6

--- a/solution.py
+++ b/solution.py
@@ -141,8 +141,9 @@
 
 def gram_tiles(arrays, pieces, pairs, count, apart):
     rows = arrays[0].shape[-2]
-    deep = 8 * rows
-    total = len(pieces) * deep
+    per, join = 4, 2
+    deep = per * join * rows
+    total = len(pieces) * per * rows
     slots = pairs.shape[0] // 2
     quarter = slots // 4
     strip = 256
@@ -154,16 +155,17 @@
 
         def load(p):
             a, i = pieces[p]
-            return pltpu.make_async_copy(array_refs[a].at[i], held.at[pl.ds(p * 8, 8)], sems.at[p])
+            return pltpu.make_async_copy(array_refs[a].at[i], held.at[pl.ds(p * per, per)], sems.at[p])
 
         def store(t):
             return pltpu.make_async_copy(made.at[t], out_refs[t].at[0] if apart else out_refs[0].at[t], out_sems.at[t])
 
         for p in range(len(pieces)):
             load(p).start()
-        for p in range(len(pieces)):
-            load(p).wait()
-            units = pl.ds(p * 8, 8)
+        for p in range(0, len(pieces), join):
+            for q in range(p, p + join):
+                load(q).wait()
+            units = pl.ds(p * per, per * join)
 
             for m in range(0, WIDTH, strip):
                 part = lax.dot_general(
@@ -209,7 +211,7 @@
             in_specs=[HBM] * len(arrays),
             out_specs=[HBM] * len(outs),
             scratch_shapes=[
-                pltpu.VMEM((len(pieces) * 8, rows, WIDTH), jnp.bfloat16),
+                pltpu.VMEM((len(pieces) * per, rows, WIDTH), jnp.bfloat16),
                 pltpu.VMEM((WIDTH, WIDTH), jnp.float32),
                 pltpu.VMEM((4, quarter * BLOCK + quarter, BLOCK), jnp.int16),
                 pltpu.VMEM((quarter, BLOCK), jnp.float32),
@@ -328,18 +330,19 @@
     far_then, stay = scale_columns(units, block_order, jacobian, weight, [(group, len(FAR_THEN)), (group,)])
 
     unit = (rows, WIDTH)
-    whole, half = pl.ds(0, group), [pl.ds(0, lines), pl.ds(lines, lines)]
+    half = [pl.ds(0, lines), pl.ds(lines, lines)]
 
     def parted(far, steps):
         sent = [k for k, s in enumerate(steps) if s]
-        copies = [(0, (h, k), (lines, *unit), q, h) for q, k in enumerate(sent) for h in half]
-        parts = copy_parts([far], [(group, *unit)] * len(sent), copies, "part_far")
-        return [away(part, steps[k]) for part, k in zip(parts, sent)]
+        sent = [(k, h) for k in sent for h in half]
+        copies = [(0, (h, k), (lines, *unit), q, pl.ds(0, lines)) for q, (k, h) in enumerate(sent)]
+        parts = copy_parts([far], [(lines, *unit)] * len(sent), copies, "part_far")
+        return [away(part, steps[k] // abs(steps[k])) for part, (k, _) in zip(parts, sent)]
 
     far_first = spread(far_first, ("c", "x"))
     far_first = after(far_first, stay)
     far_parts = parted(far_first, FAR_FIRST)
-    far_then = after(far_then, far_first, *near_parts)
+    far_then = after(far_then, far_first, *near_parts, far_parts[0])
     far_then = spread(far_then, ("c", "x"))
     far_parts += parted(far_then, FAR_THEN)
 
@@ -354,16 +357,18 @@
         ],
         "join_near",
     )
-    near = after(near, far_then, far_parts[0], far_wanted)
+    near = after(near, far_then, *far_parts[:4], far_wanted)
+    far_parts[:2] = [away(part, -1) for part in far_parts[:2]]
     near = spread(near, ("c", "x")).reshape(group * 4, *unit)
 
-    far_pieces = [(q, whole) for q in range(len(far_parts))] + [(len(far_parts), (whole, FAR_FIRST.index(0)))]
+    far_pieces = [(q, pl.ds(0, lines)) for q in range(len(far_parts))]
+    far_pieces += [(len(far_parts), (h, FAR_FIRST.index(0))) for h in half]
     far_tiles = list(gram_tiles([*far_parts, far_first], far_pieces, far_wanted[:-1], far_wanted[-1:], True))
     near = after(near, far_tiles[1])
     for k in range(1, quarters):
         far_tiles[k] = lax.ppermute(far_tiles[k], "y", [(b, (b + k) % quarters) for b in range(quarters)])
     far_sum = away(sum_tiles(far_tiles, True), -FAR)
-    near_pieces = [(0, pl.ds(8 * q, 8)) for q in range(4)]
+    near_pieces = [(0, pl.ds(lines * q, lines)) for q in range(8)]
     (near_tiles,) = gram_tiles([near], near_pieces, wanted[:-1], wanted[-1:], False)
     near_tiles = after(near_tiles, *far_tiles[1:])
     return sum_tiles([spread(near_tiles, "y"), far_sum], False)

time: 199 us -> 204 us (1.025); the launches traced: 196 us -> 203 us
  waiting for transfers between devices: 86.7 us -> 98.1 us
  starting transfers between devices: 56.6 us -> 52.7 us
    ppermute x5 -> x10, waiting for transfers between devices: 39.2 us -> 57.1 us  [away(): return lax.ppermute(value, ('z', 'c'), moves)]
    all_to_all x4, waiting for transfers between devices: 33.9 us -> 26.8 us  [spread(): return lax.all_to_all(value, axes, split_axis=0, concat_axis=0, tiled=True)]
    all_to_all x4, starting transfers between devices: 23.5 us -> 20.9 us  [spread(): return lax.all_to_all(value, axes, split_axis=0, concat_axis=0, tiled=True)]
    ppermute x5 -> x10, starting transfers between devices: 19.5 us -> 18.2 us  [away(): return lax.ppermute(value, ('z', 'c'), moves)]
  transfers between devices with their start and end apart: 16 -> 21, of which waited for: 10 -> 12; matrix products, arithmetic and copies ran while one was open for 1% -> 1% of each run, Pallas kernels for 19% -> 19%
where the time goes in v8:
time: 204 us; the launch traced here: 203 us
  waiting for transfers between devices  98.1 us (48%)
  starting transfers between devices  52.7 us (26%)
  Pallas kernels  48.5 us (24%)
  local copies, waits for them, and re-layouts  3.11 us (2%)
    ppermute x10, waiting for transfers between devices, away(): return lax.ppermute(value, ('z', 'c'), moves)  57.1 us
    all_to_all x4, waiting for transfers between devices, spread(): return lax.all_to_all(value, axes, split_axis=0, concat_axis=0, tiled=True)  26.8 us
    all_to_all x4, starting transfers between devices, spread(): return lax.all_to_all(value, axes, split_axis=0, concat_axis=0, tiled=True)  20.9 us
    pallas_call x2, Pallas kernels, gram_tiles(): pl.pallas_call(kernel, out_shape=[jax.ShapeDtypeStruct((n, quarter * BLOC...  20 us
    ppermute x10, starting transfers between devices, away(): return lax.ppermute(value, ('z', 'c'), moves)  18.2 us
    pallas_call x2, Pallas kernels, scale_columns(): pl.pallas_call(kernel, out_shape=[jax.ShapeDtypeStruct((size, rows, WIDTH...  13.7 us
    ppermute x4, starting transfers between devices, up(): lax.ppermute(value, 'z', [(b, (b + step) % planes) for b in range(planes)])  8.26 us
    pallas_call x3, Pallas kernels, copy_parts(): pl.pallas_call(kernel, out_shape=[jax.ShapeDtypeStruct(shape, arrays[0].d...  8.2 us
  transfers between devices with their start and end apart: 21, of which 12 were waited for; matrix products, arithmetic and copies ran while one was open for 1% of the time, Pallas kernels for 19%

profile of v8, /device:TPU:2, one launch (start us, length us, event | category | flops | bytes accessed | tf_op | source)
XLA Modules:
  0.0 203.2 jit_solution(17043954622329002445)
XLA Ops:
  0.0 7.5 %scale_columns.2 = (bf16[24,64,1024]{2,1,0:T(8,128)(2,1)}, bf16[8,64,1024]{2,1,0:T(8,128)(2,1)}, bf16[8,64,1024]{2,1,0:T(8,128)(2,1)}, bf16[4,64,1024]{2,1,0:T(8,128)(2,1)}, bf16[4,64,1024]{2,1,0:T(8,128)(2,1)}) custom-call(s32[48]{0:T(128)} %constant.4.clone.units_ref, s32[512]{0:T(512)} %order_ref.3, bf16[64,65536]{1,0:T(8,128)(2,1)} %jac_ref.3, ...), custom_call_target="tpu_custom_call" | custom-call | flops 3145728 | bytes 14680064 | tf_op jit(solution)/shard_map/scale_columns/pallas_call | solution.py:71
  7.5 6.6 %all-to-all-start = ((bf16[8,3,64,1024]{3,2,1,0:T(8,128)(2,1)}), bf16[8,3,64,1024]{3,2,1,0:T(8,128)(2,1)}, u32[]{:S(2)}, u32[]{:S(2)}) async-start(bf16[8,3,64,1024]{3,2,1,0:T(8,128)(2,1)} %bitcast.4), calls=%async_computation | async-start | bytes 6291456 | tf_op jit(solution)/shard_map/all_to_all | solution.py:316
  14.1 0.2 collective-permute-start
  14.3 3.9 %collective-permute-start.1 = (bf16[8,64,1024]{2,1,0:T(8,128)(2,1)}, bf16[8,64,1024]{2,1,0:T(8,128)(2,1)}, u32[]{:S(2)}, u32[]{:S(2)}) collective-permute-start(bf16[8,64,1024]{2,1,0:T(8,128)(2,1)} %get-tuple-element.29), channel_id=1, source_target_pairs={{0,56},{8,0},{16,8},{24,16},{32,24},{40,32},{48,40},{56,48},{1,57}... | collective-permute-start | bytes 3145736 | tf_op jit(solution)/shard_map/ppermute | solution.py:309
  18.2 4.1 %collective-permute-start.3 = (bf16[4,64,1024]{2,1,0:T(8,128)(2,1)}, bf16[4,64,1024]{2,1,0:T(8,128)(2,1)}, u32[]{:S(2)}, u32[]{:S(2)}) collective-permute-start(bf16[4,64,1024]{2,1,0:T(8,128)(2,1)} %get-tuple-element.31), channel_id=1, source_target_pairs={{0,48},{8,56},{16,0},{24,8},{32,16},{40,24},{48,32},{56,40},{1,49}... | collective-permute-start | bytes 1572872 | tf_op jit(solution)/shard_map/ppermute | solution.py:309
  22.4 6.3 %scale_columns.3 = (bf16[8,64,1024]{2,1,0:T(8,128)(2,1)}, bf16[8,64,1024]{2,1,0:T(8,128)(2,1)}) custom-call(s32[16]{0:T(128)} %constant.5.clone.units_ref, s32[512]{0:T(512)} %order_ref.3, bf16[64,65536]{1,0:T(8,128)(2,1)} %jac_ref.3, f32[1,64]{1,0:T(1,128)} %bitcast.7), custom_call_target="tpu_custom_call" | custom-call | flops 1048576 | bytes 10485760 | tf_op jit(solution)/shard_map/scale_columns/pallas_call | solution.py:71
  28.7 0.0 copy-start.8
  28.7 22.1 %all-to-all-done.refs_0_.refs_6_ = bf16[8,3,64,1024]{3,2,1,0:T(8,128)(2,1)} async-done(((bf16[8,3,64,1024]{3,2,1,0:T(8,128)(2,1)}), bf16[8,3,64,1024]{3,2,1,0:T(8,128)(2,1)}, u32[]{:S(2)}, u32[]{:S(2)}) %all-to-all-start) | async-done | bytes 3145760 | tf_op jit(solution)/shard_map/all_to_all | solution.py:316
  50.7 2.5 %part_far.2 = (bf16[4,64,1024]{2,1,0:T(8,128)(2,1)}, bf16[4,64,1024]{2,1,0:T(8,128)(2,1)}, bf16[4,64,1024]{2,1,0:T(8,128)(2,1)}, bf16[4,64,1024]{2,1,0:T(8,128)(2,1)}) custom-call(bf16[8,3,64,1024]{3,2,1,0:T(8,128)(2,1)} %all-to-all-done.refs_0_.refs_6_), custom_call_target="tpu_custom_call" | custom-call | bytes 4194304 | tf_op jit(solution)/shard_map/part_far/pallas_call | solution.py:117
  53.3 4.2 %collective-permute-start.4 = (bf16[4,64,1024]{2,1,0:T(8,128)(2,1)}, bf16[4,64,1024]{2,1,0:T(8,128)(2,1)}, u32[]{:S(2)}, u32[]{:S(2)}) collective-permute-start(bf16[4,64,1024]{2,1,0:T(8,128)(2,1)} %get-tuple-element.37), channel_id=1, source_target_pairs={{0,56},{4,12},{8,0},{12,20},{16,8},{20,28},{24,16},{28,36},{32,24}... | collective-permute-start | bytes 1572872 | tf_op jit(solution)/shard_map/ppermute | solution.py:313
  57.5 6.3 %collective-permute-done.3.refs_3_ = bf16[4,64,1024]{2,1,0:T(8,128)(2,1)} collective-permute-done((bf16[4,64,1024]{2,1,0:T(8,128)(2,1)}, bf16[4,64,1024]{2,1,0:T(8,128)(2,1)}, u32[]{:S(2)}, u32[]{:S(2)}) %collective-permute-start.3) | collective-permute-done | bytes 524320 | tf_op jit(solution)/shard_map/ppermute | solution.py:309
  63.8 5.6 %collective-permute-done.4 = bf16[4,64,1024]{2,1,0:T(8,128)(2,1)} collective-permute-done((bf16[4,64,1024]{2,1,0:T(8,128)(2,1)}, bf16[4,64,1024]{2,1,0:T(8,128)(2,1)}, u32[]{:S(2)}, u32[]{:S(2)}) %collective-permute-start.4) | collective-permute-done | bytes 524320 | tf_op jit(solution)/shard_map/ppermute | solution.py:313
  69.4 5.0 %all-to-all-start.1 = ((bf16[8,1,64,1024]{3,2,1,0:T(8,128)(2,1)}), bf16[8,1,64,1024]{3,2,1,0:T(8,128)(2,1)S(1)}, u32[]{:S(2)}, u32[]{:S(2)}) async-start(bf16[8,1,64,1024]{3,2,1,0:T(8,128)(2,1)} %bitcast.5), calls=%async_computation.1 | async-start | bytes 2097152 | tf_op jit(solution)/shard_map/all_to_all | solution.py:316
  74.4 3.5 %collective-permute-start.5 = (bf16[4,64,1024]{2,1,0:T(8,128)(2,1)}, bf16[4,64,1024]{2,1,0:T(8,128)(2,1)}, u32[]{:S(2)}, u32[]{:S(2)}) collective-permute-start(bf16[4,64,1024]{2,1,0:T(8,128)(2,1)} %get-tuple-element.39), channel_id=1, source_target_pairs={{0,56},{4,12},{8,0},{12,20},{16,8},{20,28},{24,16},{28,36},{32,24}... | collective-permute-start | bytes 1572872 | tf_op jit(solution)/shard_map/ppermute | solution.py:313
  77.9 1.4 collective-permute-start.6
  79.3 0.1 collective-permute-start.7
  80.1 0.1 copy.9
  80.2 0.1 reshape.15.pairs_ref
  80.4 1.2 collective-permute-start.8
  81.6 3.6 %join_near.1 = bf16[8,4,64,1024]{3,2,1,0:T(8,128)(2,1)} custom-call(bf16[8,64,1024]{2,1,0:T(8,128)(2,1)} %copy-done.1, bf16[8,64,1024]{2,1,0:T(8,128)(2,1)} %collective-permute-done.1.refs_1_, bf16[4,64,1024]{2,1,0:T(8,128)(2,1)} %copy-done.6, bf16[4,64,1024]{2,1,0:T(8,128)(2,1)} %collective-permute-done.3.refs_3_, ...), custom_call_target="tpu_custom_call" | custom-call | bytes 8388608 | tf_op jit(solution)/shard_map/join_near/pallas_call | solution.py:117
  85.2 1.9 collective-permute-done.8
  87.1 3.5 %collective-permute-done.6.refs_2_ = bf16[4,64,1024]{2,1,0:T(8,128)(2,1)} collective-permute-done((bf16[4,64,1024]{2,1,0:T(8,128)(2,1)}, bf16[4,64,1024]{2,1,0:T(8,128)(2,1)}, u32[]{:S(2)}, u32[]{:S(2)}) %collective-permute-start.6) | collective-permute-done | bytes 524320 | tf_op jit(solution)/shard_map/ppermute | solution.py:313
  90.6 5.6 %collective-permute-done.7.refs_3_ = bf16[4,64,1024]{2,1,0:T(8,128)(2,1)} collective-permute-done((bf16[4,64,1024]{2,1,0:T(8,128)(2,1)}, bf16[4,64,1024]{2,1,0:T(8,128)(2,1)}, u32[]{:S(2)}, u32[]{:S(2)}) %collective-permute-start.7) | collective-permute-done | bytes 524320 | tf_op jit(solution)/shard_map/ppermute | solution.py:313
  96.2 1.0 copy-done
  97.2 4.8 %all-to-all-start.2 = ((bf16[8,4,64,1024]{3,2,1,0:T(8,128)(2,1)}), bf16[8,4,64,1024]{3,2,1,0:T(8,128)(2,1)}, u32[]{:S(2)}, u32[]{:S(2)}) async-start(bf16[8,4,64,1024]{3,2,1,0:T(8,128)(2,1)} %join_near.1), calls=%async_computation.2 | async-start | bytes 8388608 | tf_op jit(solution)/shard_map/all_to_all | solution.py:316
  102.0 3.7 %collective-permute-start.9 = (bf16[4,64,1024]{2,1,0:T(8,128)(2,1)}, bf16[4,64,1024]{2,1,0:T(8,128)(2,1)S(1)}, u32[]{:S(2)}, u32[]{:S(2)}) collective-permute-start(bf16[4,64,1024]{2,1,0:T(8,128)(2,1)} %collective-permute-done.4), channel_id=1, source_target_pairs={{0,56},{4,12},{8,0},{12,20},{16,8},{20,28},{24,16},{28,36},{32,24}... | collective-permute-start | bytes 1572872 | tf_op jit(solution)/shard_map/ppermute | solution.py:313
  105.7 0.2 collective-permute-start.10
  105.9 2.1 %part_far.3 = (bf16[4,64,1024]{2,1,0:T(8,128)(2,1)}, bf16[4,64,1024]{2,1,0:T(8,128)(2,1)}) custom-call(bf16[8,1,64,1024]{3,2,1,0:T(8,128)(2,1)} %copy-done), custom_call_target="tpu_custom_call" | custom-call | bytes 2097152 | tf_op jit(solution)/shard_map/part_far/pallas_call | solution.py:117
  108.0 1.9 collective-permute-start.11
  109.9 0.3 collective-permute-start.12
  110.1 0.5 slice.7.count_ref
  110.7 0.6 slice.6.pairs_ref
  111.2 4.5 %collective-permute-done.9.refs_0_ = bf16[4,64,1024]{2,1,0:T(8,128)(2,1)S(1)} collective-permute-done((bf16[4,64,1024]{2,1,0:T(8,128)(2,1)}, bf16[4,64,1024]{2,1,0:T(8,128)(2,1)S(1)}, u32[]{:S(2)}, u32[]{:S(2)}) %collective-permute-start.9) | collective-permute-done | bytes 524320 | tf_op jit(solution)/shard_map/ppermute | solution.py:313
  115.8 11.2 %collective-permute-done.10.refs_1_ = bf16[4,64,1024]{2,1,0:T(8,128)(2,1)S(1)} collective-permute-done((bf16[4,64,1024]{2,1,0:T(8,128)(2,1)}, bf16[4,64,1024]{2,1,0:T(8,128)(2,1)S(1)}, u32[]{:S(2)}, u32[]{:S(2)}) %collective-permute-start.10) | collective-permute-done | bytes 524320 | tf_op jit(solution)/shard_map/ppermute | solution.py:313
  127.0 2.5 %collective-permute-done.12.refs_5_ = bf16[4,64,1024]{2,1,0:T(8,128)(2,1)} collective-permute-done((bf16[4,64,1024]{2,1,0:T(8,128)(2,1)}, bf16[4,64,1024]{2,1,0:T(8,128)(2,1)}, u32[]{:S(2)}, u32[]{:S(2)}) %collective-permute-start.12) | collective-permute-done | bytes 524320 | tf_op jit(solution)/shard_map/ppermute | solution.py:313
  129.5 10.3 %gram_tiles.2 = (s16[1,2064,128]{2,1,0:T(8,128)(2,1)}, s16[1,2064,128]{2,1,0:T(8,128)(2,1)}, s16[1,2064,128]{2,1,0:T(8,128)(2,1)}, s16[1,2064,128]{2,1,0:T(8,128)(2,1)}) custom-call(s32[128]{0:T(128)} %slice.6.pairs_ref, s32[1]{0:T(128)} %slice.7.count_ref, bf16[4,64,1024]{2,1,0:T(8,128)(2,1)} %copy-done.9, bf16[4,64,1024]{2,1,0:T(8,128)(2,1)} %copy-done.10, ...), custom_call_target="tpu_custom_call" | custom-call | flops 4294967296 | bytes 6291456 | tf_op jit(solution)/shard_map/gram_tiles/pallas_call | solution.py:205
  139.8 3.3 %collective-permute-start.14 = (s16[1,2064,128]{2,1,0:T(8,128)(2,1)}, s16[1,2064,128]{2,1,0:T(8,128)(2,1)S(1)}, u32[]{:S(2)}, u32[]{:S(2)}) collective-permute-start(s16[1,2064,128]{2,1,0:T(8,128)(2,1)} %get-tuple-element.47), channel_id=1, source_target_pairs={{0,2},{1,3},{2,0},{3,1},{4,6},{5,7},{6,4},{7,5},{8,10},{9,11},{10,... | collective-permute-start | bytes 1585160 | tf_op jit(solution)/shard_map/ppermute | solution.py:369
  143.1 1.1 collective-permute-start.15
  144.1 1.0 collective-permute-start.13
  145.1 4.7 %all-to-all-done.2 = bf16[8,4,64,1024]{3,2,1,0:T(8,128)(2,1)} async-done(((bf16[8,4,64,1024]{3,2,1,0:T(8,128)(2,1)}), bf16[8,4,64,1024]{3,2,1,0:T(8,128)(2,1)}, u32[]{:S(2)}, u32[]{:S(2)}) %all-to-all-start.2) | async-done | bytes 4194336 | tf_op jit(solution)/shard_map/all_to_all | solution.py:316
  149.8 9.7 %gram_tiles.3 = s16[4,2064,128]{2,1,0:T(8,128)(2,1)} custom-call(s32[128]{0:T(128)} %copy-done.7, s32[1]{0:T(128)S(6)} %copy.10.count_ref, bf16[32,64,1024]{2,1,0:T(8,128)(2,1)} %bitcast.3.refs_0_), custom_call_target="tpu_custom_call" | custom-call | flops 4294967296 | bytes 6291456 | tf_op jit(solution)/shard_map/gram_tiles/pallas_call | solution.py:205
  159.6 7.9 %collective-permute-done.15.refs_3_ = s16[1,2064,128]{2,1,0:T(8,128)(2,1)S(1)} collective-permute-done((s16[1,2064,128]{2,1,0:T(8,128)(2,1)}, s16[1,2064,128]{2,1,0:T(8,128)(2,1)S(1)}, u32[]{:S(2)}, u32[]{:S(2)}) %collective-permute-start.15) | collective-permute-done | bytes 528416 | tf_op jit(solution)/shard_map/ppermute | solution.py:369
  167.4 4.5 %all-to-all-start.3 = ((s16[4,2064,128]{2,1,0:T(8,128)(2,1)}), s16[4,2064,128]{2,1,0:T(8,128)(2,1)}, u32[]{:S(2)}, u32[]{:S(2)}) async-start(s16[4,2064,128]{2,1,0:T(8,128)(2,1)} %gram_tiles.3), calls=%async_computation.3 | async-start | bytes 4227072 | tf_op jit(solution)/shard_map/all_to_all | solution.py:316
  171.9 3.2 %sum_tiles.2 = s16[1,2064,128]{2,1,0:T(8,128)(2,1)} custom-call(s16[1,2064,128]{2,1,0:T(8,128)(2,1)} %get-tuple-element.50.refs_0_, s16[1,2064,128]{2,1,0:T(8,128)(2,1)} %copy-done.4, s16[1,2064,128]{2,1,0:T(8,128)(2,1)} %copy-done.2, s16[1,2064,128]{2,1,0:T(8,128)(2,1)} %copy-done.3), custom_call_target="tpu_custom_call" | custom-call | flops 4227072 | bytes 3170304 | tf_op jit(solution)/shard_map/sum_tiles/pallas_call | solution.py:276
  175.1 1.7 collective-permute-start.16
  176.8 22.2 %collective-permute-done.16.refs_1_ = s16[1,2064,128]{2,1,0:T(8,128)(2,1)S(1)} collective-permute-done((s16[1,2064,128]{2,1,0:T(8,128)(2,1)}, s16[1,2064,128]{2,1,0:T(8,128)(2,1)S(1)}, u32[]{:S(2)}, u32[]{:S(2)}) %collective-permute-start.16) | collective-permute-done | bytes 528416 | tf_op jit(solution)/shard_map/ppermute | solution.py:313
  199.1 0.8 copy-done.5
  199.8 3.4 %sum_tiles.3 = f32[16,128,128]{2,1,0:T(8,128)} custom-call(s16[4,2064,128]{2,1,0:T(8,128)(2,1)} %all-to-all-done.3.refs_0_, s16[1,2064,128]{2,1,0:T(8,128)(2,1)} %copy-done.5), custom_call_target="tpu_custom_call" | custom-call | flops 5283840 | bytes 3698688 | tf_op jit(solution)/shard_map/sum_tiles/pallas_call | solution.py:276
  (32 shorter events, 0.1 us)
Async XLA Ops:
  7.5 43.3 %all-to-all-start = ((bf16[8,3,64,1024]{3,2,1,0:T(8,128)(2,1)}), bf16[8,3,64,1024]{3,2,1,0:T(8,128)(2,1)}, u32[]{:S(2)}, u32[]{:S(2)}) async-start(bf16[8,3,64,1024]{3,2,1,0:T(8,128)(2,1)} %bitcast.4), calls=%async_computation | async-start | bytes 6291456 | tf_op jit(solution)/shard_map/all_to_all | solution.py:316
  14.1 49.7 %collective-permute-start = (bf16[8,64,1024]{2,1,0:T(8,128)(2,1)}, bf16[8,64,1024]{2,1,0:T(8,128)(2,1)S(1)}, u32[]{:S(2)}, u32[]{:S(2)}) collective-permute-start(bf16[8,64,1024]{2,1,0:T(8,128)(2,1)} %get-tuple-element.28), channel_id=1, source_target_pairs={{0,8},{8,16},{16,24},{24,32},{32,40},{40,48},{48,56},{56,0},{1,9},... | collective-permute-start | bytes 3145736 | tf_op jit(solution)/shard_map/ppermute | solution.py:309
  14.3 49.5 %collective-permute-start.1 = (bf16[8,64,1024]{2,1,0:T(8,128)(2,1)}, bf16[8,64,1024]{2,1,0:T(8,128)(2,1)}, u32[]{:S(2)}, u32[]{:S(2)}) collective-permute-start(bf16[8,64,1024]{2,1,0:T(8,128)(2,1)} %get-tuple-element.29), channel_id=1, source_target_pairs={{0,56},{8,0},{16,8},{24,16},{32,24},{40,32},{48,40},{56,48},{1,57}... | collective-permute-start | bytes 3145736 | tf_op jit(solution)/shard_map/ppermute | solution.py:309
  18.2 39.2 %collective-permute-start.2 = (bf16[4,64,1024]{2,1,0:T(8,128)(2,1)}, bf16[4,64,1024]{2,1,0:T(8,128)(2,1)S(1)}, u32[]{:S(2)}, u32[]{:S(2)}) collective-permute-start(bf16[4,64,1024]{2,1,0:T(8,128)(2,1)} %get-tuple-element.30), channel_id=1, source_target_pairs={{0,16},{8,24},{16,32},{24,40},{32,48},{40,56},{48,0},{56,8},{1,17}... | collective-permute-start | bytes 1572872 | tf_op jit(solution)/shard_map/ppermute | solution.py:309
  18.2 45.6 %collective-permute-start.3 = (bf16[4,64,1024]{2,1,0:T(8,128)(2,1)}, bf16[4,64,1024]{2,1,0:T(8,128)(2,1)}, u32[]{:S(2)}, u32[]{:S(2)}) collective-permute-start(bf16[4,64,1024]{2,1,0:T(8,128)(2,1)} %get-tuple-element.31), channel_id=1, source_target_pairs={{0,48},{8,56},{16,0},{24,8},{32,16},{40,24},{48,32},{56,40},{1,49}... | collective-permute-start | bytes 1572872 | tf_op jit(solution)/shard_map/ppermute | solution.py:309
  28.7 51.5 %copy-start.8 = (s32[1,64,2]{1,2,0:T(2,128)S(1)}, s32[1,64,2]{1,2,0:T(2,128)}, u32[]{:S(2)}) copy-start(s32[1,64,2]{1,2,0:T(2,128)} %param.10) | copy-start | bytes 1540
  53.3 16.1 %collective-permute-start.4 = (bf16[4,64,1024]{2,1,0:T(8,128)(2,1)}, bf16[4,64,1024]{2,1,0:T(8,128)(2,1)}, u32[]{:S(2)}, u32[]{:S(2)}) collective-permute-start(bf16[4,64,1024]{2,1,0:T(8,128)(2,1)} %get-tuple-element.37), channel_id=1, source_target_pairs={{0,56},{4,12},{8,0},{12,20},{16,8},{20,28},{24,16},{28,36},{32,24}... | collective-permute-start | bytes 1572872 | tf_op jit(solution)/shard_map/ppermute | solution.py:313
  57.5 24.1 %copy-start.6 = (bf16[4,64,1024]{2,1,0:T(8,128)(2,1)}, bf16[4,64,1024]{2,1,0:T(8,128)(2,1)S(1)}, u32[]{:S(2)}) copy-start(bf16[4,64,1024]{2,1,0:T(8,128)(2,1)S(1)} %collective-permute-done.2.refs_2_) | copy-start | bytes 1572868
  63.8 5.6 %copy-start.1 = (bf16[8,64,1024]{2,1,0:T(8,128)(2,1)}, bf16[8,64,1024]{2,1,0:T(8,128)(2,1)S(1)}, u32[]{:S(2)}) copy-start(bf16[8,64,1024]{2,1,0:T(8,128)(2,1)S(1)} %collective-permute-done.refs_0_) | copy-start | bytes 3145732
  69.4 26.8 %all-to-all-start.1 = ((bf16[8,1,64,1024]{3,2,1,0:T(8,128)(2,1)}), bf16[8,1,64,1024]{3,2,1,0:T(8,128)(2,1)S(1)}, u32[]{:S(2)}, u32[]{:S(2)}) async-start(bf16[8,1,64,1024]{3,2,1,0:T(8,128)(2,1)} %bitcast.5), calls=%async_computation.1 | async-start | bytes 2097152 | tf_op jit(solution)/shard_map/all_to_all | solution.py:316
  74.4 12.7 %collective-permute-start.5 = (bf16[4,64,1024]{2,1,0:T(8,128)(2,1)}, bf16[4,64,1024]{2,1,0:T(8,128)(2,1)}, u32[]{:S(2)}, u32[]{:S(2)}) collective-permute-start(bf16[4,64,1024]{2,1,0:T(8,128)(2,1)} %get-tuple-element.39), channel_id=1, source_target_pairs={{0,56},{4,12},{8,0},{12,20},{16,8},{20,28},{24,16},{28,36},{32,24}... | collective-permute-start | bytes 1572872 | tf_op jit(solution)/shard_map/ppermute | solution.py:313
  77.9 12.7 %collective-permute-start.6 = (bf16[4,64,1024]{2,1,0:T(8,128)(2,1)}, bf16[4,64,1024]{2,1,0:T(8,128)(2,1)}, u32[]{:S(2)}, u32[]{:S(2)}) collective-permute-start(bf16[4,64,1024]{2,1,0:T(8,128)(2,1)} %get-tuple-element.40), channel_id=1, source_target_pairs={{0,56},{4,12},{8,0},{12,20},{16,8},{20,28},{24,16},{28,36},{32,24}... | collective-permute-start | bytes 1572872 | tf_op jit(solution)/shard_map/ppermute | solution.py:313
  79.3 16.9 %collective-permute-start.7 = (bf16[4,64,1024]{2,1,0:T(8,128)(2,1)}, bf16[4,64,1024]{2,1,0:T(8,128)(2,1)}, u32[]{:S(2)}, u32[]{:S(2)}) collective-permute-start(bf16[4,64,1024]{2,1,0:T(8,128)(2,1)} %get-tuple-element.41), channel_id=1, source_target_pairs={{0,56},{4,12},{8,0},{12,20},{16,8},{20,28},{24,16},{28,36},{32,24}... | collective-permute-start | bytes 1572872 | tf_op jit(solution)/shard_map/ppermute | solution.py:313
  80.4 4.8 %copy-start.7 = (s32[128]{0:T(128)}, s32[128]{0:T(128)S(1)}, u32[]{:S(2)}) copy-start(s32[128]{0:T(128)S(1)} %reshape.15.pairs_ref) | copy-start | bytes 1540
  80.4 6.7 %collective-permute-start.8 = (s32[129]{0:T(256)S(1)}, s32[129]{0:T(256)S(1)}, u32[]{:S(2)}, u32[]{:S(2)}) collective-permute-start(s32[129]{0:T(256)S(1)} %pad_add_fusion), channel_id=1, source_target_pairs={{0,24},{4,44},{8,32},{12,52},{16,40},{20,60},{24,48},{28,4},{32,56... | collective-permute-start | bytes 1556 | tf_op jit(solution)/shard_map/ppermute | solution.py:313
  96.2 1.0 copy-start
  97.2 52.6 %all-to-all-start.2 = ((bf16[8,4,64,1024]{3,2,1,0:T(8,128)(2,1)}), bf16[8,4,64,1024]{3,2,1,0:T(8,128)(2,1)}, u32[]{:S(2)}, u32[]{:S(2)}) async-start(bf16[8,4,64,1024]{3,2,1,0:T(8,128)(2,1)} %join_near.1), calls=%async_computation.2 | async-start | bytes 8388608 | tf_op jit(solution)/shard_map/all_to_all | solution.py:316
  102.0 13.8 %collective-permute-start.9 = (bf16[4,64,1024]{2,1,0:T(8,128)(2,1)}, bf16[4,64,1024]{2,1,0:T(8,128)(2,1)S(1)}, u32[]{:S(2)}, u32[]{:S(2)}) collective-permute-start(bf16[4,64,1024]{2,1,0:T(8,128)(2,1)} %collective-permute-done.4), channel_id=1, source_target_pairs={{0,56},{4,12},{8,0},{12,20},{16,8},{20,28},{24,16},{28,36},{32,24}... | collective-permute-start | bytes 1572872 | tf_op jit(solution)/shard_map/ppermute | solution.py:313
  105.7 21.3 %collective-permute-start.10 = (bf16[4,64,1024]{2,1,0:T(8,128)(2,1)}, bf16[4,64,1024]{2,1,0:T(8,128)(2,1)S(1)}, u32[]{:S(2)}, u32[]{:S(2)}) collective-permute-start(bf16[4,64,1024]{2,1,0:T(8,128)(2,1)} %collective-permute-done.5), channel_id=1, source_target_pairs={{0,56},{4,12},{8,0},{12,20},{16,8},{20,28},{24,16},{28,36},{32,24}... | collective-permute-start | bytes 1572872 | tf_op jit(solution)/shard_map/ppermute | solution.py:313
  108.0 19.0 %collective-permute-start.11 = (bf16[4,64,1024]{2,1,0:T(8,128)(2,1)}, bf16[4,64,1024]{2,1,0:T(8,128)(2,1)S(1)}, u32[]{:S(2)}, u32[]{:S(2)}) collective-permute-start(bf16[4,64,1024]{2,1,0:T(8,128)(2,1)} %get-tuple-element.43), channel_id=1, source_target_pairs={{0,8},{4,60},{8,16},{12,4},{16,24},{20,12},{24,32},{28,20},{32,40}... | collective-permute-start | bytes 1572872 | tf_op jit(solution)/shard_map/ppermute | solution.py:313
  109.9 19.6 %collective-permute-start.12 = (bf16[4,64,1024]{2,1,0:T(8,128)(2,1)}, bf16[4,64,1024]{2,1,0:T(8,128)(2,1)}, u32[]{:S(2)}, u32[]{:S(2)}) collective-permute-start(bf16[4,64,1024]{2,1,0:T(8,128)(2,1)} %get-tuple-element.44), channel_id=1, source_target_pairs={{0,8},{4,60},{8,16},{12,4},{16,24},{20,12},{24,32},{28,20},{32,40}... | collective-permute-start | bytes 1572872 | tf_op jit(solution)/shard_map/ppermute | solution.py:313
  115.8 13.7 %copy-start.9 = (bf16[4,64,1024]{2,1,0:T(8,128)(2,1)}, bf16[4,64,1024]{2,1,0:T(8,128)(2,1)S(1)}, u32[]{:S(2)}) copy-start(bf16[4,64,1024]{2,1,0:T(8,128)(2,1)S(1)} %collective-permute-done.9.refs_0_) | copy-start | bytes 1572868
  127.0 2.5 %copy-start.10 = (bf16[4,64,1024]{2,1,0:T(8,128)(2,1)}, bf16[4,64,1024]{2,1,0:T(8,128)(2,1)S(1)}, u32[]{:S(2)}) copy-start(bf16[4,64,1024]{2,1,0:T(8,128)(2,1)S(1)} %collective-permute-done.10.refs_1_) | copy-start | bytes 1572868
  127.0 2.5 %copy-start.11 = (bf16[4,64,1024]{2,1,0:T(8,128)(2,1)}, bf16[4,64,1024]{2,1,0:T(8,128)(2,1)S(1)}, u32[]{:S(2)}) copy-start(bf16[4,64,1024]{2,1,0:T(8,128)(2,1)S(1)} %collective-permute-done.11.refs_4_) | copy-start | bytes 1572868
  139.8 19.7 %collective-permute-start.14 = (s16[1,2064,128]{2,1,0:T(8,128)(2,1)}, s16[1,2064,128]{2,1,0:T(8,128)(2,1)S(1)}, u32[]{:S(2)}, u32[]{:S(2)}) collective-permute-start(s16[1,2064,128]{2,1,0:T(8,128)(2,1)} %get-tuple-element.47), channel_id=1, source_target_pairs={{0,2},{1,3},{2,0},{3,1},{4,6},{5,7},{6,4},{7,5},{8,10},{9,11},{10,... | collective-permute-start | bytes 1585160 | tf_op jit(solution)/shard_map/ppermute | solution.py:369
  143.1 24.3 %collective-permute-start.15 = (s16[1,2064,128]{2,1,0:T(8,128)(2,1)}, s16[1,2064,128]{2,1,0:T(8,128)(2,1)S(1)}, u32[]{:S(2)}, u32[]{:S(2)}) collective-permute-start(s16[1,2064,128]{2,1,0:T(8,128)(2,1)} %get-tuple-element.48), channel_id=1, source_target_pairs={{0,3},{1,0},{2,1},{3,2},{4,7},{5,4},{6,5},{7,6},{8,11},{9,8},{10,9... | collective-permute-start | bytes 1585160 | tf_op jit(solution)/shard_map/ppermute | solution.py:369
  144.1 23.3 %collective-permute-start.13 = (s16[1,2064,128]{2,1,0:T(8,128)(2,1)}, s16[1,2064,128]{2,1,0:T(8,128)(2,1)S(1)}, u32[]{:S(2)}, u32[]{:S(2)}) collective-permute-start(s16[1,2064,128]{2,1,0:T(8,128)(2,1)} %get-tuple-element.45), channel_id=1, source_target_pairs={{0,1},{1,2},{2,3},{3,0},{4,5},{5,6},{6,7},{7,4},{8,9},{9,10},{10,1... | collective-permute-start | bytes 1585160 | tf_op jit(solution)/shard_map/ppermute | solution.py:369
  159.5 12.4 %copy-start.2 = (s16[1,2064,128]{2,1,0:T(8,128)(2,1)}, s16[1,2064,128]{2,1,0:T(8,128)(2,1)S(1)}, u32[]{:S(2)}) copy-start(s16[1,2064,128]{2,1,0:T(8,128)(2,1)S(1)} %collective-permute-done.14.refs_2_) | copy-start | bytes 1585156
  167.4 4.5 %copy-start.3 = (s16[1,2064,128]{2,1,0:T(8,128)(2,1)}, s16[1,2064,128]{2,1,0:T(8,128)(2,1)S(1)}, u32[]{:S(2)}) copy-start(s16[1,2064,128]{2,1,0:T(8,128)(2,1)S(1)} %collective-permute-done.15.refs_3_) | copy-start | bytes 1585156
  167.4 4.5 %copy-start.4 = (s16[1,2064,128]{2,1,0:T(8,128)(2,1)}, s16[1,2064,128]{2,1,0:T(8,128)(2,1)S(1)}, u32[]{:S(2)}) copy-start(s16[1,2064,128]{2,1,0:T(8,128)(2,1)S(1)} %collective-permute-done.13.refs_1_) | copy-start | bytes 1585156
  167.4 31.6 %all-to-all-start.3 = ((s16[4,2064,128]{2,1,0:T(8,128)(2,1)}), s16[4,2064,128]{2,1,0:T(8,128)(2,1)}, u32[]{:S(2)}, u32[]{:S(2)}) async-start(s16[4,2064,128]{2,1,0:T(8,128)(2,1)} %gram_tiles.3), calls=%async_computation.3 | async-start | bytes 4227072 | tf_op jit(solution)/shard_map/all_to_all | solution.py:316
  175.1 23.9 %collective-permute-start.16 = (s16[1,2064,128]{2,1,0:T(8,128)(2,1)}, s16[1,2064,128]{2,1,0:T(8,128)(2,1)S(1)}, u32[]{:S(2)}, u32[]{:S(2)}) collective-permute-start(s16[1,2064,128]{2,1,0:T(8,128)(2,1)} %sum_tiles.2), channel_id=1, source_target_pairs={{0,40},{4,28},{8,48},{12,36},{16,56},{20,44},{24,0},{28,52},{32,8}... | collective-permute-start | bytes 1585160 | tf_op jit(solution)/shard_map/ppermute | solution.py:313
  199.1 0.8 copy-start.5
